TPU v7x, 512 devices: a whole 4x8x8 slice. The times are simulated.
512 devices in a mesh: rows: 512 (over z, x, y, core).
Axes of the slice: x: 4, y: 8, z: 8, core: 2. Of those that a mesh axis runs over, the one named last changes fastest.
Arguments:
- bases: float32 [5, 524288, 128], P(None, 'rows'), may hold values from -1 to 1
- targets: float32 [524288, 128], P('rows'), may hold values from -8 to 8
Outputs:
- solved: float32 [524288, 128], P('rows')
All inputs are finite; a program needn't handle non-finite values.
Results may differ from a plain program's by a relative error of at most 0.0001.
Values sent between devices are 32-bit elements; how exact they have to be, the bound alone decides.
No kernel may reach another device: no remote copies, remote signals or barrier semaphores. Data moves between devices by JAX's collectives and lax.ppermute only.
A program may use at most 64 MiB of HBM per device.

v0:
```python
import jax
import jax.numpy as jnp
from jax import lax
from jax.sharding import PartitionSpec as P


def from_partner(value, axis, stride):
    mask = 2**stride
    pairs = [(source, source ^ mask) for source in range(lax.axis_size(axis))]
    return lax.ppermute(value, axis, pairs)


def solve_core(left_sums, right_sums):
    identity = jnp.eye(left_sums.shape[-1], dtype=jnp.float32)
    gram_a = left_sums[0]
    gram_b = right_sums[0]
    proj_a = left_sums[1:]
    proj_b = right_sums[1:]
    chol_a = jnp.linalg.cholesky(gram_a)
    inverse_a = jax.scipy.linalg.cho_solve((chol_a, True), identity)
    schur_part = inverse_a - gram_b
    chol_s = jnp.linalg.cholesky(schur_part)
    inverse_s = jax.scipy.linalg.cho_solve((chol_s, True), identity)
    target_b = (
        jnp.einsum("kl,mln->mkn", inverse_a, proj_a, precision=lax.Precision.HIGHEST) - proj_b
    )
    coef_b = jnp.einsum("kl,mln->mkn", inverse_s, target_b, precision=lax.Precision.HIGHEST)
    coef_a = proj_b - jnp.einsum("kl,mln->mkn", gram_b, coef_b, precision=lax.Precision.HIGHEST)
    return (coef_a, coef_b)


def slot_sums(payload, child_id, parity, level_no):
    child_count = 2 ** (level_no + 1)
    onehot = (jnp.arange(child_count, dtype=jnp.int32) == child_id).astype(jnp.float32)
    slotted = onehot[:, None, None, None] * payload[None]
    summed = lax.psum(slotted, "rows")
    own_sums = lax.dynamic_index_in_dim(summed, child_id, 0, keepdims=False)
    sib_sums = lax.dynamic_index_in_dim(summed, child_id + 1 - 2 * parity, 0, keepdims=False)
    return (own_sums, sib_sums)


def per_device(bases, targets):
    levels = bases.shape[0]
    devices = lax.axis_size("rows")
    tree_depth = devices.bit_length() - 1
    my_index = lax.axis_index("rows")
    slot_levels = 1
    fields = [bases[level_no] for level_no in range(levels)] + [targets]
    for level_no in reversed(range(levels)):
        group_bits = tree_depth - level_no - 1
        child_id = my_index // 2**group_bits
        parity = child_id % 2
        own_basis = fields[level_no]
        coarser = jnp.stack(fields[:level_no] + [fields[levels]])
        gram = jnp.einsum("rk,rl->kl", own_basis, own_basis, precision=lax.Precision.HIGHEST)
        proj = jnp.einsum("rk,mrl->mkl", own_basis, coarser, precision=lax.Precision.HIGHEST)
        payload = jnp.concatenate([gram[None], proj], 0)
        if level_no < slot_levels:
            own_sums, sib_sums = slot_sums(payload, child_id, parity, level_no)
        else:
            own_sums = payload
            for bit_no in range(group_bits):
                own_sums = own_sums + from_partner(own_sums, "rows", bit_no)
            sib_sums = from_partner(own_sums, "rows", group_bits)
        is_left = parity == 0
        left_sums = jnp.where(is_left, own_sums, sib_sums)
        right_sums = jnp.where(is_left, sib_sums, own_sums)
        coef_a, coef_b = solve_core(left_sums, right_sums)
        own_coef = jnp.where(is_left, coef_a, coef_b)
        corrected = coarser - jnp.einsum(
            "rk,mkl->mrl", own_basis, own_coef, precision=lax.Precision.HIGHEST
        )
        fields = (
            [corrected[m_no] for m_no in range(level_no)]
            + fields[level_no:levels]
            + [corrected[level_no]]
        )
    return fields[levels]


def solution(mesh):
    return jax.shard_map(
        per_device,
        mesh=mesh,
        in_specs=(P(None, "rows", None), P("rows", None)),
        out_specs=P("rows", None),
        check_vma=False,
    )
```

profile of v0, /device:TPU:23, one launch (start us, length us, event | category | flops | bytes accessed | tf_op | source)
XLA Modules:
  0.0 881.4 jit_solution(12693625848405230575)
XLA Ops:
  24.5 9.0 %collective-permute-done.1 = f32[6,128,128]{1,2,0:T(8,128)S(1)} collective-permute-done((f32[6,128,128]{1,2,0:T(8,128)S(1)}, f32[6,128,128]{1,2,0:T(8,128)S(1)}, u32[]{:S(2)}, u32[]{:S(2)}) %collective-permute-start.1) | collective-permute-done | bytes 393248 | tf_op jit(solution)/shard_map/ppermute | solution.py:10
  35.5 16.2 %collective-permute-done.2 = f32[6,128,128]{1,2,0:T(8,128)S(1)} collective-permute-done((f32[6,128,128]{1,2,0:T(8,128)S(1)}, f32[6,128,128]{1,2,0:T(8,128)S(1)}, u32[]{:S(2)}, u32[]{:S(2)}) %collective-permute-start.2) | collective-permute-done | bytes 393248 | tf_op jit(solution)/shard_map/ppermute | solution.py:10
  51.8 8.3 collective-permute-start.3
  60.1 13.4 %collective-permute-done.3 = f32[6,128,128]{1,2,0:T(8,128)S(1)} collective-permute-done((f32[6,128,128]{1,2,0:T(8,128)S(1)}, f32[6,128,128]{1,2,0:T(8,128)S(1)}, u32[]{:S(2)}, u32[]{:S(2)}) %collective-permute-start.3) | collective-permute-done | bytes 393248 | tf_op jit(solution)/shard_map/ppermute | solution.py:10
  76.4 8.5 collective-permute-done.4
  86.1 11.7 %cholesky.164 = f32[128,128]{1,0:T(8,128)S(1)} custom-call(f32[128,128]{1,0:T(8,128)S(1)} %fusion.87), custom_call_target="Cholesky" | custom-call | tf_op jit(solution)/shard_map/jit(cholesky)/cholesky | solution.py:19
  99.9 10.6 %custom-call.16 = f32[1,128,128]{1,2,0:T(8,128)S(1)} custom-call(f32[1,128,128]{2,1,0:T(8,128)} %fusion.72), custom_call_target="InvertDiagBlocksLowerTriangular" | custom-call | tf_op jit(solution)/shard_map/jit(_cho_solve)/triangular_solve | solution.py:20
  112.5 11.7 %cholesky.175 = f32[128,128]{1,0:T(8,128)S(1)} custom-call(f32[128,128]{1,0:T(8,128)S(1)} %fusion.122), custom_call_target="Cholesky" | custom-call | tf_op jit(solution)/shard_map/jit(cholesky)/cholesky | solution.py:22
  125.7 10.2 %custom-call.17 = f32[1,128,128]{1,2,0:T(8,128)S(1)} custom-call(f32[1,128,128]{2,1,0:T(8,128)S(1)} %fusion.73), custom_call_target="InvertDiagBlocksLowerTriangular" | custom-call | tf_op jit(solution)/shard_map/jit(_cho_solve)/triangular_solve | solution.py:23
  150.4 9.7 %collective-permute-start.6 = (f32[5,128,128]{1,2,0:T(8,128)S(1)}, f32[5,128,128]{1,2,0:T(8,128)S(1)}, u32[]{:S(2)}, u32[]{:S(2)}) collective-permute-start(f32[5,128,128]{1,2,0:T(8,128)S(1)} %fusion.138), channel_id=1, source_target_pairs={{0,2},{1,3},{2,0},{3,1},{4,6},{5,7},{6,4},{7,5},{8,10},{9,11},{10,... | collective-permute-start | bytes 983048 | tf_op jit(solution)/shard_map/ppermute | solution.py:10
  160.1 7.7 collective-permute-done.6
  170.0 13.8 %collective-permute-done.7 = f32[5,128,128]{1,2,0:T(8,128)S(1)} collective-permute-done((f32[5,128,128]{1,2,0:T(8,128)S(1)}, f32[5,128,128]{1,2,0:T(8,128)S(1)}, u32[]{:S(2)}, u32[]{:S(2)}) %collective-permute-start.7) | collective-permute-done | bytes 327712 | tf_op jit(solution)/shard_map/ppermute | solution.py:10
  188.3 9.6 %collective-permute-done.8 = f32[5,128,128]{1,2,0:T(8,128)S(1)} collective-permute-done((f32[5,128,128]{1,2,0:T(8,128)S(1)}, f32[5,128,128]{1,2,0:T(8,128)S(1)}, u32[]{:S(2)}, u32[]{:S(2)}) %collective-permute-start.8) | collective-permute-done | bytes 327712 | tf_op jit(solution)/shard_map/ppermute | solution.py:10
  200.5 6.6 collective-permute-done.9
  207.1 6.2 collective-permute-start.10
  213.4 5.6 collective-permute-done.10
  219.2 11.7 %cholesky.186 = f32[128,128]{1,0:T(8,128)S(1)} custom-call(f32[128,128]{1,0:T(8,128)S(1)} %fusion.86), custom_call_target="Cholesky" | custom-call | tf_op jit(solution)/shard_map/jit(cholesky)/cholesky | solution.py:19
  232.3 9.8 %custom-call.18 = f32[1,128,128]{1,2,0:T(8,128)S(1)} custom-call(f32[1,128,128]{2,1,0:T(8,128)S(1)} %fusion.74), custom_call_target="InvertDiagBlocksLowerTriangular" | custom-call | tf_op jit(solution)/shard_map/jit(_cho_solve)/triangular_solve | solution.py:20
  243.2 11.7 %cholesky.197 = f32[128,128]{1,0:T(8,128)S(1)} custom-call(f32[128,128]{1,0:T(8,128)S(1)} %fusion.114), custom_call_target="Cholesky" | custom-call | tf_op jit(solution)/shard_map/jit(cholesky)/cholesky | solution.py:22
  256.3 10.2 %custom-call.19 = f32[1,128,128]{1,2,0:T(8,128)S(1)} custom-call(f32[1,128,128]{2,1,0:T(8,128)S(1)} %fusion.75), custom_call_target="InvertDiagBlocksLowerTriangular" | custom-call | tf_op jit(solution)/shard_map/jit(_cho_solve)/triangular_solve | solution.py:23
  278.7 15.2 %collective-permute-start.12 = (f32[4,128,128]{1,2,0:T(8,128)S(1)}, f32[4,128,128]{1,2,0:T(8,128)S(1)}, u32[]{:S(2)}, u32[]{:S(2)}) collective-permute-start(f32[4,128,128]{1,2,0:T(8,128)S(1)} %fusion.137), channel_id=1, source_target_pairs={{0,2},{1,3},{2,0},{3,1},{4,6},{5,7},{6,4},{7,5},{8,10},{9,11},{10,... | collective-permute-start | bytes 786440 | tf_op jit(solution)/shard_map/ppermute | solution.py:10
  293.9 6.3 collective-permute-done.12
  302.1 10.7 %collective-permute-done.13 = f32[4,128,128]{1,2,0:T(8,128)S(1)} collective-permute-done((f32[4,128,128]{1,2,0:T(8,128)S(1)}, f32[4,128,128]{1,2,0:T(8,128)S(1)}, u32[]{:S(2)}, u32[]{:S(2)}) %collective-permute-start.13) | collective-permute-done | bytes 262176 | tf_op jit(solution)/shard_map/ppermute | solution.py:10
  317.2 8.1 collective-permute-done.14
  327.7 5.1 collective-permute-done.15
  332.8 6.9 collective-permute-start.16
  346.2 5.2 collective-permute-done.17
  351.5 11.7 %cholesky.208 = f32[128,128]{1,0:T(8,128)S(1)} custom-call(f32[128,128]{1,0:T(8,128)S(1)} %fusion.85), custom_call_target="Cholesky" | custom-call | tf_op jit(solution)/shard_map/jit(cholesky)/cholesky | solution.py:19
  364.6 9.8 %custom-call.20 = f32[1,128,128]{1,2,0:T(8,128)S(1)} custom-call(f32[1,128,128]{2,1,0:T(8,128)S(1)} %fusion.76), custom_call_target="InvertDiagBlocksLowerTriangular" | custom-call | tf_op jit(solution)/shard_map/jit(_cho_solve)/triangular_solve | solution.py:20
  375.5 11.7 %cholesky.219 = f32[128,128]{1,0:T(8,128)S(1)} custom-call(f32[128,128]{1,0:T(8,128)S(1)} %fusion.106), custom_call_target="Cholesky" | custom-call | tf_op jit(solution)/shard_map/jit(cholesky)/cholesky | solution.py:22
  388.5 9.9 %custom-call.21 = f32[1,128,128]{1,2,0:T(8,128)S(1)} custom-call(f32[1,128,128]{2,1,0:T(8,128)S(1)} %fusion.77), custom_call_target="InvertDiagBlocksLowerTriangular" | custom-call | tf_op jit(solution)/shard_map/jit(_cho_solve)/triangular_solve | solution.py:23
  403.8 5.8 collective-permute-start.18
  410.7 14.1 %collective-permute-start.19 = (f32[3,128,128]{1,2,0:T(8,128)S(1)}, f32[3,128,128]{1,2,0:T(8,128)S(1)}, u32[]{:S(2)}, u32[]{:S(2)}) collective-permute-start(f32[3,128,128]{1,2,0:T(8,128)S(1)} %fusion.136), channel_id=1, source_target_pairs={{0,2},{1,3},{2,0},{3,1},{4,6},{5,7},{6,4},{7,5},{8,10},{9,11},{10,... | collective-permute-start | bytes 589832 | tf_op jit(solution)/shard_map/ppermute | solution.py:10
  424.8 4.9 collective-permute-done.19
  431.7 7.9 collective-permute-done.20
  439.6 4.9 collective-permute-start.21
  444.5 6.0 collective-permute-done.21
  457.0 6.2 collective-permute-start.23
  477.2 5.1 collective-permute-done.25
  482.5 11.7 %cholesky.230 = f32[128,128]{1,0:T(8,128)S(1)} custom-call(f32[128,128]{1,0:T(8,128)S(1)} %fusion.84), custom_call_target="Cholesky" | custom-call | tf_op jit(solution)/shard_map/jit(cholesky)/cholesky | solution.py:19
  495.7 9.8 %custom-call.22 = f32[1,128,128]{1,2,0:T(8,128)S(1)} custom-call(f32[1,128,128]{2,1,0:T(8,128)S(1)} %fusion.78), custom_call_target="InvertDiagBlocksLowerTriangular" | custom-call | tf_op jit(solution)/shard_map/jit(_cho_solve)/triangular_solve | solution.py:20
  506.5 11.7 %cholesky.241 = f32[128,128]{1,0:T(8,128)S(1)} custom-call(f32[128,128]{1,0:T(8,128)S(1)} %fusion.98), custom_call_target="Cholesky" | custom-call | tf_op jit(solution)/shard_map/jit(cholesky)/cholesky | solution.py:22
  519.7 10.0 %custom-call.23 = f32[1,128,128]{1,2,0:T(8,128)S(1)} custom-call(f32[1,128,128]{2,1,0:T(8,128)S(1)} %fusion.79), custom_call_target="InvertDiagBlocksLowerTriangular" | custom-call | tf_op jit(solution)/shard_map/jit(_cho_solve)/triangular_solve | solution.py:23
  534.9 288.6 %all-reduce.2.cloned.1.call-done = f32[2,2,128,128]{2,3,1,0:T(8,128)} async-done(((f32[2,2,128,128]{2,3,1,0:T(8,128)}), f32[2,2,128,128]{2,3,1,0:T(8,128)}) %all-reduce.2.cloned.1.call-update) | async-done | bytes 262160 | tf_op jit(solution)/shard_map/psum | solution.py:36
  824.6 11.7 %cholesky.252 = f32[128,128]{1,0:T(8,128)S(1)} custom-call(f32[128,128]{1,0:T(8,128)S(1)} %fusion.83), custom_call_target="Cholesky" | custom-call | tf_op jit(solution)/shard_map/jit(cholesky)/cholesky | solution.py:19
  837.7 9.8 %custom-call.24 = f32[1,128,128]{1,2,0:T(8,128)S(1)} custom-call(f32[1,128,128]{2,1,0:T(8,128)S(1)} %fusion.80), custom_call_target="InvertDiagBlocksLowerTriangular" | custom-call | tf_op jit(solution)/shard_map/jit(_cho_solve)/triangular_solve | solution.py:20
  848.5 11.9 %cholesky.263 = f32[128,128]{1,0:T(8,128)S(1)} custom-call(f32[128,128]{1,0:T(8,128)S(1)} %fusion.91), custom_call_target="Cholesky" | custom-call | tf_op jit(solution)/shard_map/jit(cholesky)/cholesky | solution.py:22
  861.7 9.8 %custom-call.25 = f32[1,128,128]{1,2,0:T(8,128)S(1)} custom-call(f32[1,128,128]{2,1,0:T(8,128)S(1)} %fusion.81), custom_call_target="InvertDiagBlocksLowerTriangular" | custom-call | tf_op jit(solution)/shard_map/jit(_cho_solve)/triangular_solve | solution.py:23
  (196 shorter events, 133.1 us)
Async XLA Ops:
  6.5 816.9 %all-reduce.2.cloned.1.call-start = ((), (), s32[]{:S(2)}) async-start(), calls=%async_computation | async-start | bytes 524288 | tf_op jit(solution)/shard_map/psum | solution.py:36
  11.8 2.0 copy-start.4
  17.3 3.9 collective-permute-start
  21.3 12.2 %collective-permute-start.1 = (f32[6,128,128]{1,2,0:T(8,128)S(1)}, f32[6,128,128]{1,2,0:T(8,128)S(1)}, u32[]{:S(2)}, u32[]{:S(2)}) collective-permute-start(f32[6,128,128]{1,2,0:T(8,128)S(1)} %fusion.139), channel_id=1, source_target_pairs={{0,2},{1,3},{2,0},{3,1},{4,6},{5,7},{6,4},{7,5},{8,10},{9,11},{10,... | collective-permute-start | bytes 1179656 | tf_op jit(solution)/shard_map/ppermute | solution.py:10
  33.5 18.2 %collective-permute-start.2 = (f32[6,128,128]{1,2,0:T(8,128)S(1)}, f32[6,128,128]{1,2,0:T(8,128)S(1)}, u32[]{:S(2)}, u32[]{:S(2)}) collective-permute-start(f32[6,128,128]{1,2,0:T(8,128)S(1)} %add.112), channel_id=1, source_target_pairs={{0,4},{1,5},{2,6},{3,7},{4,0},{5,1},{6,2},{7,3},{8,12},{9,13},{10,... | collective-permute-start | bytes 1179656 | tf_op jit(solution)/shard_map/ppermute | solution.py:10
  51.8 21.8 %collective-permute-start.3 = (f32[6,128,128]{1,2,0:T(8,128)S(1)}, f32[6,128,128]{1,2,0:T(8,128)S(1)}, u32[]{:S(2)}, u32[]{:S(2)}) collective-permute-start(f32[6,128,128]{1,2,0:T(8,128)S(1)} %add.113), channel_id=1, source_target_pairs={{0,8},{1,9},{2,10},{3,11},{4,12},{5,13},{6,14},{7,15},{8,0},{9,1},... | collective-permute-start | bytes 1179656 | tf_op jit(solution)/shard_map/ppermute | solution.py:10
  73.6 2.7 copy-start.3
  73.6 11.2 %collective-permute-start.4 = (f32[6,128,128]{1,2,0:T(8,128)S(1)}, f32[6,128,128]{1,2,0:T(8,128)}, u32[]{:S(2)}, u32[]{:S(2)}) collective-permute-start(f32[6,128,128]{1,2,0:T(8,128)S(1)} %add.114), channel_id=1, source_target_pairs={{0,16},{1,17},{2,18},{3,19},{4,20},{5,21},{6,22},{7,23},{8,24},{9,... | collective-permute-start | bytes 1179656 | tf_op jit(solution)/shard_map/ppermute | solution.py:10
  141.5 1.5 copy-start
  144.9 5.5 collective-permute-start.5
  150.4 17.4 %collective-permute-start.6 = (f32[5,128,128]{1,2,0:T(8,128)S(1)}, f32[5,128,128]{1,2,0:T(8,128)S(1)}, u32[]{:S(2)}, u32[]{:S(2)}) collective-permute-start(f32[5,128,128]{1,2,0:T(8,128)S(1)} %fusion.138), channel_id=1, source_target_pairs={{0,2},{1,3},{2,0},{3,1},{4,6},{5,7},{6,4},{7,5},{8,10},{9,11},{10,... | collective-permute-start | bytes 983048 | tf_op jit(solution)/shard_map/ppermute | solution.py:10
  167.8 16.0 %collective-permute-start.7 = (f32[5,128,128]{1,2,0:T(8,128)S(1)}, f32[5,128,128]{1,2,0:T(8,128)S(1)}, u32[]{:S(2)}, u32[]{:S(2)}) collective-permute-start(f32[5,128,128]{1,2,0:T(8,128)S(1)} %add.117), channel_id=1, source_target_pairs={{0,4},{1,5},{2,6},{3,7},{4,0},{5,1},{6,2},{7,3},{8,12},{9,13},{10,... | collective-permute-start | bytes 983048 | tf_op jit(solution)/shard_map/ppermute | solution.py:10
  183.8 14.0 %collective-permute-start.8 = (f32[5,128,128]{1,2,0:T(8,128)S(1)}, f32[5,128,128]{1,2,0:T(8,128)S(1)}, u32[]{:S(2)}, u32[]{:S(2)}) collective-permute-start(f32[5,128,128]{1,2,0:T(8,128)S(1)} %add.118), channel_id=1, source_target_pairs={{0,8},{1,9},{2,10},{3,11},{4,12},{5,13},{6,14},{7,15},{8,0},{9,1},... | collective-permute-start | bytes 983048 | tf_op jit(solution)/shard_map/ppermute | solution.py:10
  197.9 9.2 %collective-permute-start.9 = (f32[5,128,128]{1,2,0:T(8,128)S(1)}, f32[5,128,128]{1,2,0:T(8,128)S(1)}, u32[]{:S(2)}, u32[]{:S(2)}) collective-permute-start(f32[5,128,128]{1,2,0:T(8,128)S(1)} %add.119), channel_id=1, source_target_pairs={{0,16},{1,17},{2,18},{3,19},{4,20},{5,21},{6,22},{7,23},{8,24},{9,... | collective-permute-start | bytes 983048 | tf_op jit(solution)/shard_map/ppermute | solution.py:10
  207.1 11.9 %collective-permute-start.10 = (f32[5,128,128]{1,2,0:T(8,128)S(1)}, f32[5,128,128]{1,2,0:T(8,128)S(1)}, u32[]{:S(2)}, u32[]{:S(2)}) collective-permute-start(f32[5,128,128]{1,2,0:T(8,128)S(1)} %add.120), channel_id=1, source_target_pairs={{0,32},{1,33},{2,34},{3,35},{4,36},{5,37},{6,38},{7,39},{8,40},{9,... | collective-permute-start | bytes 983048 | tf_op jit(solution)/shard_map/ppermute | solution.py:10
  270.6 2.2 copy-start.1
  272.8 5.8 collective-permute-start.11
  278.7 21.5 %collective-permute-start.12 = (f32[4,128,128]{1,2,0:T(8,128)S(1)}, f32[4,128,128]{1,2,0:T(8,128)S(1)}, u32[]{:S(2)}, u32[]{:S(2)}) collective-permute-start(f32[4,128,128]{1,2,0:T(8,128)S(1)} %fusion.137), channel_id=1, source_target_pairs={{0,2},{1,3},{2,0},{3,1},{4,6},{5,7},{6,4},{7,5},{8,10},{9,11},{10,... | collective-permute-start | bytes 786440 | tf_op jit(solution)/shard_map/ppermute | solution.py:10
  300.2 12.7 %collective-permute-start.13 = (f32[4,128,128]{1,2,0:T(8,128)S(1)}, f32[4,128,128]{1,2,0:T(8,128)S(1)}, u32[]{:S(2)}, u32[]{:S(2)}) collective-permute-start(f32[4,128,128]{1,2,0:T(8,128)S(1)} %add.123), channel_id=1, source_target_pairs={{0,4},{1,5},{2,6},{3,7},{4,0},{5,1},{6,2},{7,3},{8,12},{9,13},{10,... | collective-permute-start | bytes 786440 | tf_op jit(solution)/shard_map/ppermute | solution.py:10
  312.9 12.4 %collective-permute-start.14 = (f32[4,128,128]{1,2,0:T(8,128)S(1)}, f32[4,128,128]{1,2,0:T(8,128)S(1)}, u32[]{:S(2)}, u32[]{:S(2)}) collective-permute-start(f32[4,128,128]{1,2,0:T(8,128)S(1)} %add.124), channel_id=1, source_target_pairs={{0,8},{1,9},{2,10},{3,11},{4,12},{5,13},{6,14},{7,15},{8,0},{9,1},... | collective-permute-start | bytes 786440 | tf_op jit(solution)/shard_map/ppermute | solution.py:10
  325.3 7.5 collective-permute-start.15
  332.8 11.4 %collective-permute-start.16 = (f32[4,128,128]{1,2,0:T(8,128)S(1)}, f32[4,128,128]{1,2,0:T(8,128)S(1)}, u32[]{:S(2)}, u32[]{:S(2)}) collective-permute-start(f32[4,128,128]{1,2,0:T(8,128)S(1)} %add.126), channel_id=1, source_target_pairs={{0,32},{1,33},{2,34},{3,35},{4,36},{5,37},{6,38},{7,39},{8,40},{9,... | collective-permute-start | bytes 786440 | tf_op jit(solution)/shard_map/ppermute | solution.py:10
  344.3 7.1 collective-permute-start.17
  402.2 37.4 %copy-start.2 = (f32[1,1024,128]{1,2,0:T(8,128)}, f32[1,1024,128]{1,2,0:T(8,128)S(1)}, u32[]{:S(2)}) copy-start(f32[1,1024,128]{1,2,0:T(8,128)S(1)} %get-tuple-element.8) | copy-start | bytes 1572868
  403.8 6.9 collective-permute-start.18
  410.7 19.0 %collective-permute-start.19 = (f32[3,128,128]{1,2,0:T(8,128)S(1)}, f32[3,128,128]{1,2,0:T(8,128)S(1)}, u32[]{:S(2)}, u32[]{:S(2)}) collective-permute-start(f32[3,128,128]{1,2,0:T(8,128)S(1)} %fusion.136), channel_id=1, source_target_pairs={{0,2},{1,3},{2,0},{3,1},{4,6},{5,7},{6,4},{7,5},{8,10},{9,11},{10,... | collective-permute-start | bytes 589832 | tf_op jit(solution)/shard_map/ppermute | solution.py:10
  429.7 9.8 %collective-permute-start.20 = (f32[3,128,128]{1,2,0:T(8,128)S(1)}, f32[3,128,128]{1,2,0:T(8,128)S(1)}, u32[]{:S(2)}, u32[]{:S(2)}) collective-permute-start(f32[3,128,128]{1,2,0:T(8,128)S(1)} %add.130), channel_id=1, source_target_pairs={{0,4},{1,5},{2,6},{3,7},{4,0},{5,1},{6,2},{7,3},{8,12},{9,13},{10,... | collective-permute-start | bytes 589832 | tf_op jit(solution)/shard_map/ppermute | solution.py:10
  439.6 10.9 %collective-permute-start.21 = (f32[3,128,128]{1,2,0:T(8,128)S(1)}, f32[3,128,128]{1,2,0:T(8,128)S(1)}, u32[]{:S(2)}, u32[]{:S(2)}) collective-permute-start(f32[3,128,128]{1,2,0:T(8,128)S(1)} %add.131), channel_id=1, source_target_pairs={{0,8},{1,9},{2,10},{3,11},{4,12},{5,13},{6,14},{7,15},{8,0},{9,1},... | collective-permute-start | bytes 589832 | tf_op jit(solution)/shard_map/ppermute | solution.py:10
  450.5 6.4 collective-permute-start.22
  457.0 9.3 %collective-permute-start.23 = (f32[3,128,128]{1,2,0:T(8,128)S(1)}, f32[3,128,128]{1,2,0:T(8,128)S(1)}, u32[]{:S(2)}, u32[]{:S(2)}) collective-permute-start(f32[3,128,128]{1,2,0:T(8,128)S(1)} %add.133), channel_id=1, source_target_pairs={{0,32},{1,33},{2,34},{3,35},{4,36},{5,37},{6,38},{7,39},{8,40},{9,... | collective-permute-start | bytes 589832 | tf_op jit(solution)/shard_map/ppermute | solution.py:10
  466.3 6.4 collective-permute-start.24
  472.7 9.6 %collective-permute-start.25 = (f32[3,128,128]{1,2,0:T(8,128)S(1)}, f32[3,128,128]{1,2,0:T(8,128)S(1)}, u32[]{:S(2)}, u32[]{:S(2)}) collective-permute-start(f32[3,128,128]{1,2,0:T(8,128)S(1)} %add.135), channel_id=1, source_target_pairs={{0,128},{1,129},{2,130},{3,131},{4,132},{5,133},{6,134},{7,135},{8... | collective-permute-start | bytes 589832 | tf_op jit(solution)/shard_map/ppermute | solution.py:10
Sparse Core Ops, SparseCore 0:
  535.0 288.4 all-reduce.1
where the time goes:
time: 887 us; the launch traced here: 881 us
  waiting for transfers between devices  459 us (52%)
  other arithmetic  236 us (27%)
  starting transfers between devices  127 us (14%)
  matrix products  35.2 us (4%)
  between operations  15.3 us (2%)
    psum x1, waiting for transfers between devices, slot_sums(): summed = lax.psum(slotted, 'rows')  289 us
    ppermute x26, waiting for transfers between devices, from_partner(): return lax.ppermute(value, axis, pairs)  170 us
    ppermute x26, starting transfers between devices, from_partner(): return lax.ppermute(value, axis, pairs)  127 us
    another operation x15, other arithmetic, solve_core(): chol_s = jnp.linalg.cholesky(schur_part)  62.3 us
    another operation x15, other arithmetic, solve_core(): chol_a = jnp.linalg.cholesky(gram_a)  62.1 us
    another operation x10, other arithmetic, solve_core(): inverse_a = jax.scipy.linalg.cho_solve((chol_a, True), identity)  53.9 us
    another operation x10, other arithmetic, solve_core(): inverse_s = jax.scipy.linalg.cho_solve((chol_s, True), identity)  53.5 us
  transfers between devices with their start and end apart: 27, of which 27 were waited for; matrix products, arithmetic and copies ran while one was open for 0% of the time, Pallas kernels for 0%

commit v1 on v0

v1 whole, which is shorter than its diff:
```python
import functools

import jax
import jax.numpy as jnp
from jax import lax
from jax.experimental import pallas as pl
from jax.experimental.pallas import tpu as pltpu
from jax.sharding import Mesh
from jax.sharding import PartitionSpec as P

LEVELS = 5
K = 128
HALF = K // 2
AXES = ("z", "x", "y", "c")
SIZES = (8, 4, 8, 2)
HIGHEST = lax.Precision.HIGHEST
VMEM_SPEC = pl.BlockSpec(memory_space=pltpu.VMEM)
SMEM_SPEC = pl.BlockSpec(memory_space=pltpu.SMEM)

TOTAL = sum(level_no + 2 for level_no in range(LEVELS))
CHIPS = 8
TILE = HALF // CHIPS


def rows_up_to(level_no):
    return sum(below + 2 for below in range(level_no + 1))


def mm(left, right):
    return jnp.dot(left, right, preferred_element_type=jnp.float32, precision=HIGHEST)


def mtm(left, right):
    return lax.dot_general(
        left,
        right,
        (((0,), (0,)), ((), ())),
        preferred_element_type=jnp.float32,
        precision=HIGHEST,
    )


def two_parts(value):
    high = value.astype(jnp.bfloat16)
    return high, (value - high.astype(jnp.float32)).astype(jnp.bfloat16)


def dot_parts(left, right, dims):
    dot = functools.partial(
        lax.dot_general, dimension_numbers=(dims, ((), ())), preferred_element_type=jnp.float32
    )
    return dot(left[0], right[0]) + (dot(left[0], right[1]) + dot(left[1], right[0]))


def call(body, out_shapes, core, *args, scratch=()):
    outs = pl.pallas_call(
        body,
        out_shape=[jax.ShapeDtypeStruct(shape, jnp.float32) for shape in out_shapes],
        in_specs=[SMEM_SPEC] + [VMEM_SPEC] * len(args),
        out_specs=[VMEM_SPEC] * len(out_shapes),
        scratch_shapes=[pltpu.VMEM(shape, jnp.float32) for shape in scratch],
    )(core, *args)
    return list(outs)


def row_order(level_no):
    return [level_no] + list(range(level_no)) + [LEVELS]


GROUPS = (((4, 3), (4, 3, 2, 1, 0, 5)), ((2, 1), (2, 1, 0, 5)), ((0,), (0, 5)))


def gram_body(core_ref, bases_ref, targets_ref, keep_ref, send_ref, sum_ref):
    step = pl.program_id(0)
    parts = [two_parts(bases_ref[level_no]) for level_no in range(LEVELS)]
    parts.append(two_parts(targets_ref[...]))

    def wide(fields):
        return [jnp.concatenate([parts[m_no][i] for m_no in fields], 1) for i in range(2)]

    starts = {}
    at = 0
    for level_no in reversed(range(LEVELS)):
        starts[level_no] = at
        at += level_no + 2
    for lefts, rights in GROUPS:
        block = dot_parts(wide(lefts), wide(rights), ((0,), (0,)))
        for top, level_no in enumerate(lefts):
            for m_no, field in enumerate(row_order(level_no)):
                to = rights.index(field)
                value = block[top * K : (top + 1) * K, to * K : (to + 1) * K]
                tiles = value.reshape(2, CHIPS, TILE, K)
                at = starts[level_no] + m_no

                @pl.when(step == 0)
                def _():
                    sum_ref[:, :, at] = tiles

                @pl.when(step > 0)
                def _():
                    sum_ref[:, :, at] += tiles

    @pl.when(step == pl.num_programs(0) - 1)
    def _():
        keep_ref[...] = sum_ref[core_ref[0]]
        send_ref[...] = sum_ref[1 - core_ref[0]]


def local_grams(core, bases, targets, block=512):
    rows = bases.shape[1]
    shape = (CHIPS, TOTAL, TILE, K)
    whole = pl.BlockSpec(shape, lambda i: (0, 0, 0, 0))
    return pl.pallas_call(
        gram_body,
        grid=(rows // block,),
        out_shape=[jax.ShapeDtypeStruct(shape, jnp.float32)] * 2,
        in_specs=[
            SMEM_SPEC,
            pl.BlockSpec((LEVELS, block, K), lambda i: (0, i, 0)),
            pl.BlockSpec((block, K), lambda i: (i, 0)),
        ],
        out_specs=[whole, whole],
        scratch_shapes=[pltpu.VMEM((2,) + shape, jnp.float32)],
    )(core, bases, targets)


def inverse_of_complement(product, work_ref):
    row_no = lax.broadcasted_iota(jnp.int32, (K, K), 0)
    column_no = lax.broadcasted_iota(jnp.int32, (K, K), 1)
    eye = (row_no == column_no).astype(jnp.float32)

    def factor(power, inverse):
        power = mm(power, power)
        return power, inverse + mm(inverse, power)

    def size(value):
        return jnp.sum(value * value)

    power, inverse = product, eye + product
    for _ in range(3):
        power, inverse = factor(power, inverse)
    work_ref[0] = power
    work_ref[1] = inverse

    def more(carry):
        step, square = carry
        return (step < 64) & (square * square > 1e-20)

    def body(carry):
        power, inverse = factor(work_ref[0], work_ref[1])
        work_ref[0] = power
        work_ref[1] = inverse
        return carry[0] + 1, size(power)

    lax.while_loop(more, body, (jnp.int32(0), size(power)))
    return work_ref[1]


def solve_pair(gram_own, gram_sib, proj_own, proj_sib, work_ref):
    inverse = inverse_of_complement(mm(gram_sib, gram_own), work_ref)
    coef_own = mm(inverse, proj_sib - mm(gram_sib, proj_own))
    coef_sib = proj_own - mm(gram_own, coef_own)
    return coef_own, coef_sib


def wide_of(ref, first, count):
    return jnp.concatenate([ref[first + m_no] for m_no in range(count)], 1)


def put_wide(ref, first, value):
    for m_no in range(value.shape[1] // K):
        ref[first + m_no] = value[:, m_no * K : (m_no + 1) * K]


def eliminate(level_no, core_no, own, sib, both, next_ref, send_ref, coef_ref, work_ref):
    count = level_no + 1
    proj_own = jnp.concatenate([own(1 + m_no) for m_no in range(count)], 1)
    proj_sib = jnp.concatenate([sib(1 + m_no) for m_no in range(count)], 1)
    coef_own, coef_sib = solve_pair(own(0), sib(0), proj_own, proj_sib, work_ref)
    put_wide(coef_ref, 0, coef_own)
    left = jnp.concatenate([proj_own + coef_sib, proj_sib + coef_own], 0)
    right = jnp.concatenate([coef_own, coef_sib], 0)
    at = 0
    for row_no in reversed(range(level_no)):
        order = [row_no] + list(range(row_no)) + [level_no]
        picked = [right[:, m_no * K : (m_no + 1) * K] for m_no in order]
        row = mtm(left[:, row_no * K : (row_no + 1) * K], jnp.concatenate(picked, 1))
        for m_no in range(row_no + 2):
            next_ref[at] = both(at) - row[:, m_no * K : (m_no + 1) * K]
            at += 1
    if send_ref is not None:
        first = pl.multiple_of(core_no * HALF, HALF)
        for at in range(rows_up_to(level_no - 1)):
            send_ref[at] = next_ref[at, pl.ds(first, HALF)]


def finest_body(core_ref, half_ref, far_ref, next_ref, send_ref, coef_ref, work_ref, all_ref):
    level_no = LEVELS - 1
    core_no = core_ref[0]
    count = level_no + 2
    for at in range(half_ref.shape[1]):
        all_ref[at, pl.ds(pl.multiple_of(core_no * HALF, HALF), HALF)] = half_ref[
            :, at
        ].reshape(HALF, K)
        all_ref[at, pl.ds(pl.multiple_of((1 - core_no) * HALF, HALF), HALF)] = far_ref[
            :, at
        ].reshape(HALF, K)
    eliminate(
        level_no,
        core_no,
        lambda at: all_ref[at],
        lambda at: all_ref[count + at],
        lambda at: all_ref[2 * count + at],
        next_ref,
        send_ref,
        coef_ref,
        work_ref,
    )


def middle_body(level_no, core_ref, own_ref, half_ref, far_ref, next_ref, *refs):
    send_ref, coef_ref, work_ref, sib_ref = refs if len(refs) == 4 else (None,) + refs
    core_no = core_ref[0]
    for at in range(half_ref.shape[0]):
        sib_ref[at, pl.ds(pl.multiple_of(core_no * HALF, HALF), HALF)] = half_ref[at]
        sib_ref[at, pl.ds(pl.multiple_of((1 - core_no) * HALF, HALF), HALF)] = far_ref[at]
    below = level_no + 2
    eliminate(
        level_no,
        core_no,
        lambda at: own_ref[at],
        lambda at: sib_ref[at],
        lambda at: own_ref[below + at] + sib_ref[below + at],
        next_ref,
        send_ref,
        coef_ref,
        work_ref,
    )


def fold_body(level_no, core_ref, coef_ref, *refs):
    finer = LEVELS - 1 - level_no
    coef = wide_of(coef_ref, 0, level_no + 1)
    for at in range(finer):
        old_ref, new_ref = refs[at], refs[finer + at]
        kept = list(range(level_no)) + [level_no + 1]
        old = jnp.concatenate([old_ref[m_no] for m_no in kept], 1)
        put_wide(new_ref, 0, old - mm(old_ref[level_no], coef))


def coarsest_body(core_ref, own_ref, sib_ref, bases_ref, targets_ref, *refs):
    olds, out_ref, work_ref = refs[:-2], refs[-2], refs[-1]
    coef, _ = solve_pair(own_ref[0], sib_ref[0], own_ref[1], sib_ref[1], work_ref)
    mults = [coef]
    for old_ref in reversed(olds):
        mults.append(old_ref[1] - mm(old_ref[0], coef))
    tall = two_parts(jnp.concatenate(mults, 0))
    rows = targets_ref.shape[0]
    block = 256
    for first in range(0, rows, block):
        some = pl.ds(first, block)
        wide = [bases_ref[level_no, some] for level_no in range(LEVELS)]
        wide = two_parts(jnp.concatenate(wide, 1))
        out_ref[some] = targets_ref[some] - dot_parts(wide, tall, ((1,), (0,)))


def swap(value, axis, partner):
    pairs = [(source, partner(source)) for source in range(lax.axis_size(axis))]
    return lax.ppermute(value, axis, pairs)


def swap_cores(value):
    return swap(value, "c", lambda at: at ^ 1)


PARTNERS = {
    4: ("x", lambda at: at ^ 1),
    3: ("x", lambda at: 3 - at),
    2: ("z", lambda at: at ^ 1),
    1: ("z", lambda at: at ^ 2),
    0: ("z", lambda at: (6, 7, 4, 5, 2, 3, 0, 1)[at]),
}
WORK = (2, K, K)


def per_device(bases, targets):
    top = LEVELS - 1
    head = top + 2
    core = lax.axis_index("c").astype(jnp.int32).reshape(1)
    keep, send = local_grams(core, bases, targets)
    part = keep + swap_cores(send)
    part = lax.all_to_all(part, "y", 0, 0).sum(0)
    other = swap(part, *PARTNERS[top])
    piece = jnp.concatenate([part[:head], other[:head], part[head:] + other[head:]], 0)
    half = gather_chips(piece)
    far = swap_cores(half)
    below = rows_up_to(top - 1)
    own, send, coef = call(
        finest_body,
        [(below, K, K), (below, HALF, K), (top + 1, K, K)],
        core,
        half,
        far,
        scratch=[WORK, (piece.shape[0], K, K)],
    )
    mults = [coef]
    for level_no in range(top - 1, 0, -1):
        half = swap(send, *PARTNERS[level_no])
        far = swap_cores(half)
        below = rows_up_to(level_no - 1)
        shapes = [(below, K, K), (below, HALF, K), (level_no + 1, K, K)]
        if level_no == 1:
            del shapes[1]
        outs = call(
            functools.partial(middle_body, level_no),
            shapes,
            core,
            own,
            half,
            far,
            scratch=[WORK, own.shape],
        )
        own, send, coef = outs[0], outs[-2], outs[-1]
        folded = call(
            functools.partial(fold_body, level_no),
            [(level_no + 1, K, K)] * len(mults),
            core,
            coef,
            *mults,
        )
        mults = folded + [coef]
    sib = swap(own, *PARTNERS[0])
    (solved,) = call(
        coarsest_body, [targets.shape], core, own, sib, bases, targets, *mults, scratch=[WORK]
    )
    return solved


def gather_chips(piece):
    return lax.all_gather(piece, "y")


def solution(mesh):
    split = Mesh(mesh.devices.reshape(SIZES), AXES)
    return jax.shard_map(
        per_device,
        mesh=split,
        in_specs=(P(None, AXES, None), P(AXES, None)),
        out_specs=P(AXES, None),
        check_vma=False,
    )
```

time: 887 us -> 175 us (0.20)
  the two profiles are of different devices: /device:TPU:23 before, /device:TPU:71 now
where the time goes in v1:
time: 175 us
  blocking collectives  47.5 us (27%)
  starting transfers between devices  42.1 us (24%)
  Pallas kernels  41.2 us (24%)
  waiting for transfers between devices  39 us (22%)
  local copies, waits for them, and re-layouts  3.73 us (2%)
    ppermute x10, starting transfers between devices, swap(): return lax.ppermute(value, axis, pairs)  42.1 us
    ppermute x10, waiting for transfers between devices, swap(): return lax.ppermute(value, axis, pairs)  39 us
    pallas_call x8, Pallas kernels, call(): pl.pallas_call(body, out_shape=[jax.ShapeDtypeStruct(shape, jnp.float32)...  33.4 us
    all_to_all x1, blocking collectives, per_device(): part = lax.all_to_all(part, 'y', 0, 0).sum(0)  26.2 us
    all_gather x1, blocking collectives, gather_chips(): return lax.all_gather(piece, 'y')  21.3 us
    pallas_call x1, Pallas kernels, local_grams(): pl.pallas_call(gram_body, grid=(rows // block,), out_shape=[jax.ShapeDtyp...  7.82 us
    unnamed x18, local copies, waits for them, and re-layouts  3.72 us
  transfers between devices with their start and end apart: 10, of which 9 were waited for; matrix products, arithmetic and copies ran while one was open for 0% of the time, Pallas kernels for 4%

profile of v1, /device:TPU:71, one launch (start us, length us, event | category | flops | bytes accessed | tf_op | source)
XLA Modules:
  0.0 174.8 jit_solution(15337561898451678238)
XLA Ops:
  0.0 7.8 %shard_map.28 = (f32[8,20,8,128]{3,2,1,0:T(8,128)}, f32[8,20,8,128]{3,2,1,0:T(8,128)}) custom-call(s32[1]{0:T(128)} %bitcast.core_ref, f32[5,1024,128]{2,1,0:T(8,128)} %bases_ref.3, f32[1024,128]{1,0:T(8,128)} %targets_ref.3), custom_call_target="tpu_custom_call" | custom-call | tf_op jit(solution)/shard_map/pallas_call | solution.py:113
  7.8 2.6 %collective-permute-start = (f32[8,20,8,128]{3,2,1,0:T(8,128)}, f32[8,20,8,128]{3,2,1,0:T(8,128)S(1)}, u32[]{:S(2)}, u32[]{:S(2)}) collective-permute-start(f32[8,20,8,128]{3,2,1,0:T(8,128)} %get-tuple-element.24), channel_id=1, source_target_pairs={{0,1},{1,0},{2,3},{3,2},{4,5},{5,4},{6,7},{7,6},{8,9},{9,8},{10,11... | collective-permute-start | bytes 1966088 | tf_op jit(solution)/shard_map/ppermute | solution.py:269
  10.4 1.9 %collective-permute-done = f32[8,20,8,128]{3,2,1,0:T(8,128)S(1)} collective-permute-done((f32[8,20,8,128]{3,2,1,0:T(8,128)}, f32[8,20,8,128]{3,2,1,0:T(8,128)S(1)}, u32[]{:S(2)}, u32[]{:S(2)}) %collective-permute-start) | collective-permute-done | bytes 655392 | tf_op jit(solution)/shard_map/ppermute | solution.py:269
  12.3 1.2 add.6
  13.5 26.2 %all_to_all.5 = f32[8,20,8,128]{3,2,1,0:T(8,128)S(1)} all-to-all(f32[8,20,8,128]{3,2,1,0:T(8,128)S(1)} %add.6), channel_id=1, replica_groups=mesh['z'=8,'x'=4,'y'=8,'c'=2] {'y'}, dimensions={0} | all-to-all | bytes 1310720 | tf_op jit(solution)/shard_map/all_to_all | solution.py:292
  39.7 2.5 %collective-permute-start.1 = (f32[20,8,128]{2,1,0:T(8,128)S(1)}, f32[20,8,128]{2,1,0:T(8,128)S(1)}, u32[]{:S(2)}, u32[]{:S(2)}) collective-permute-start(f32[20,8,128]{2,1,0:T(8,128)S(1)} %reduce_sum.9), channel_id=1, source_target_pairs={{0,16},{16,0},{32,48},{48,32},{1,17},{17,1},{33,49},{49,33},{2,18}... | collective-permute-start | bytes 245768 | tf_op jit(solution)/shard_map/ppermute | solution.py:269
  42.2 2.7 %collective-permute-done.1 = f32[20,8,128]{2,1,0:T(8,128)S(1)} collective-permute-done((f32[20,8,128]{2,1,0:T(8,128)S(1)}, f32[20,8,128]{2,1,0:T(8,128)S(1)}, u32[]{:S(2)}, u32[]{:S(2)}) %collective-permute-start.1) | collective-permute-done | bytes 81952 | tf_op jit(solution)/shard_map/ppermute | solution.py:269
  44.9 21.3 %all-gather = f32[208,8,128]{2,1,0:T(8,128)S(1)} all-gather(f32[26,8,128]{2,1,0:T(8,128)S(1)} %pad_maximum_fusion), channel_id=2, replica_groups=mesh['z'=8,'x'=4,'y'=8,'c'=2] {'y'}, dimensions={0}, use_global_device_ids=true | all-gather | bytes 958464 | tf_op jit(solution)/shard_map/all_gather | solution.py:340
  66.2 0.0 copy-start
  66.2 9.5 %collective-permute-start.2 = (f32[8,26,8,128]{3,2,1,0:T(8,128)S(1)}, f32[8,26,8,128]{3,2,1,0:T(8,128)S(1)}, u32[]{:S(2)}, u32[]{:S(2)}) collective-permute-start(f32[8,26,8,128]{3,2,1,0:T(8,128)S(1)} %bitcast.2), channel_id=1, source_target_pairs={{0,1},{1,0},{2,3},{3,2},{4,5},{5,4},{6,7},{7,6},{8,9},{9,8},{10,11... | collective-permute-start | bytes 2555912 | tf_op jit(solution)/shard_map/ppermute | solution.py:269
  75.7 2.0 %collective-permute-done.2.far_ref = f32[8,26,8,128]{3,2,1,0:T(8,128)S(1)} collective-permute-done((f32[8,26,8,128]{3,2,1,0:T(8,128)S(1)}, f32[8,26,8,128]{3,2,1,0:T(8,128)S(1)}, u32[]{:S(2)}, u32[]{:S(2)}) %collective-permute-start.2) | collective-permute-done | bytes 852000 | tf_op jit(solution)/shard_map/ppermute | solution.py:269
  77.7 0.0 copy-done
  77.7 0.0 copy-start.1
  77.7 0.9 copy-done.1
  78.6 5.9 %shard_map.29 = (f32[14,128,128]{2,1,0:T(8,128)}, f32[14,64,128]{2,1,0:T(8,128)}, f32[5,128,128]{2,1,0:T(8,128)}) custom-call(s32[1]{0:T(128)} %bitcast.core_ref, f32[8,26,8,128]{3,2,1,0:T(8,128)} %bitcast.3, f32[8,26,8,128]{3,2,1,0:T(8,128)} %copy-done.1), custom_call_target="tpu_custom_call" | custom-call | tf_op jit(solution)/shard_map/pallas_call | solution.py:56
  84.6 2.1 %collective-permute-start.3 = (f32[14,64,128]{2,1,0:T(8,128)}, f32[14,64,128]{2,1,0:T(8,128)S(1)}, u32[]{:S(2)}, u32[]{:S(2)}) collective-permute-start(f32[14,64,128]{2,1,0:T(8,128)} %get-tuple-element.26), channel_id=1, source_target_pairs={{0,48},{16,32},{32,16},{48,0},{1,49},{17,33},{33,17},{49,1},{2,50}... | collective-permute-start | bytes 1376264 | tf_op jit(solution)/shard_map/ppermute | solution.py:269
  86.7 12.9 %collective-permute-done.3.half_ref = f32[14,64,128]{2,1,0:T(8,128)S(1)} collective-permute-done((f32[14,64,128]{2,1,0:T(8,128)}, f32[14,64,128]{2,1,0:T(8,128)S(1)}, u32[]{:S(2)}, u32[]{:S(2)}) %collective-permute-start.3) | collective-permute-done | bytes 458784 | tf_op jit(solution)/shard_map/ppermute | solution.py:269
  99.6 0.0 copy-start.2
  99.6 3.1 %collective-permute-start.4 = (f32[14,64,128]{2,1,0:T(8,128)S(1)}, f32[14,64,128]{2,1,0:T(8,128)S(1)}, u32[]{:S(2)}, u32[]{:S(2)}) collective-permute-start(f32[14,64,128]{2,1,0:T(8,128)S(1)} %collective-permute-done.3.half_ref), channel_id=1, source_target_pairs={{0,1},{1,0},{2,3},{3,2},{4,5},{5,4},{6,7},{7,6},{8,9},{9,8},{10,11... | collective-permute-start | bytes 1376264 | tf_op jit(solution)/shard_map/ppermute | solution.py:269
  102.7 1.4 collective-permute-done.4.far_ref
  104.1 0.0 copy-done.2
  104.1 0.8 copy-done.3
  104.9 5.6 %shard_map.30 = (f32[9,128,128]{2,1,0:T(8,128)}, f32[9,64,128]{2,1,0:T(8,128)}, f32[4,128,128]{2,1,0:T(8,128)}) custom-call(s32[1]{0:T(128)} %bitcast.core_ref, f32[14,128,128]{2,1,0:T(8,128)} %get-tuple-element.25.own_ref, f32[14,64,128]{2,1,0:T(8,128)} %copy-done.2, f32[14,64,128]{2,1,0:T(8,128)} %copy-done.3), custom_call_target="tpu_custom_call" | custom-call | tf_op jit(solution)/shard_map/pallas_call | solution.py:56
  110.5 1.9 %collective-permute-start.5 = (f32[9,64,128]{2,1,0:T(8,128)}, f32[9,64,128]{2,1,0:T(8,128)S(1)}, u32[]{:S(2)}, u32[]{:S(2)}) collective-permute-start(f32[9,64,128]{2,1,0:T(8,128)} %get-tuple-element.28), channel_id=1, source_target_pairs={{0,64},{64,0},{128,192},{192,128},{256,320},{320,256},{384,448},{4... | collective-permute-start | bytes 884744 | tf_op jit(solution)/shard_map/ppermute | solution.py:269
  112.4 8.4 %collective-permute-done.5.half_ref = f32[9,64,128]{2,1,0:T(8,128)S(1)} collective-permute-done((f32[9,64,128]{2,1,0:T(8,128)}, f32[9,64,128]{2,1,0:T(8,128)S(1)}, u32[]{:S(2)}, u32[]{:S(2)}) %collective-permute-start.5) | collective-permute-done | bytes 294944 | tf_op jit(solution)/shard_map/ppermute | solution.py:269
  120.8 0.0 copy-start.4
  120.8 3.1 %collective-permute-start.6 = (f32[9,64,128]{2,1,0:T(8,128)S(1)}, f32[9,64,128]{2,1,0:T(8,128)S(1)}, u32[]{:S(2)}, u32[]{:S(2)}) collective-permute-start(f32[9,64,128]{2,1,0:T(8,128)S(1)} %collective-permute-done.5.half_ref), channel_id=1, source_target_pairs={{0,1},{1,0},{2,3},{3,2},{4,5},{5,4},{6,7},{7,6},{8,9},{9,8},{10,11... | collective-permute-start | bytes 884744 | tf_op jit(solution)/shard_map/ppermute | solution.py:269
  123.9 1.2 collective-permute-done.6.far_ref
  125.1 0.0 copy-start.5
  125.1 0.0 copy-done.4
  125.1 0.7 copy-done.5
  125.8 4.8 %shard_map.31 = (f32[5,128,128]{2,1,0:T(8,128)}, f32[5,64,128]{2,1,0:T(8,128)}, f32[3,128,128]{2,1,0:T(8,128)}) custom-call(s32[1]{0:T(128)} %bitcast.core_ref, f32[9,128,128]{2,1,0:T(8,128)} %get-tuple-element.27.own_ref, f32[9,64,128]{2,1,0:T(8,128)} %copy-done.4, f32[9,64,128]{2,1,0:T(8,128)} %copy-done.5), custom_call_target="tpu_custom_call" | custom-call | tf_op jit(solution)/shard_map/pallas_call | solution.py:56
  130.6 5.8 %collective-permute-start.7 = (f32[5,64,128]{2,1,0:T(8,128)}, f32[5,64,128]{2,1,0:T(8,128)S(1)}, u32[]{:S(2)}, u32[]{:S(2)}) collective-permute-start(f32[5,64,128]{2,1,0:T(8,128)} %get-tuple-element.30), channel_id=1, source_target_pairs={{0,128},{64,192},{128,0},{192,64},{256,384},{320,448},{384,256},{4... | collective-permute-start | bytes 491528 | tf_op jit(solution)/shard_map/ppermute | solution.py:269
  136.4 7.5 %collective-permute-done.7.half_ref = f32[5,64,128]{2,1,0:T(8,128)S(1)} collective-permute-done((f32[5,64,128]{2,1,0:T(8,128)}, f32[5,64,128]{2,1,0:T(8,128)S(1)}, u32[]{:S(2)}, u32[]{:S(2)}) %collective-permute-start.7) | collective-permute-done | bytes 163872 | tf_op jit(solution)/shard_map/ppermute | solution.py:269
  143.9 0.0 copy-start.6
  143.9 2.4 %collective-permute-start.8 = (f32[5,64,128]{2,1,0:T(8,128)S(1)}, f32[5,64,128]{2,1,0:T(8,128)S(1)}, u32[]{:S(2)}, u32[]{:S(2)}) collective-permute-start(f32[5,64,128]{2,1,0:T(8,128)S(1)} %collective-permute-done.7.half_ref), channel_id=1, source_target_pairs={{0,1},{1,0},{2,3},{3,2},{4,5},{5,4},{6,7},{7,6},{8,9},{9,8},{10,11... | collective-permute-start | bytes 491528 | tf_op jit(solution)/shard_map/ppermute | solution.py:269
  146.2 1.0 collective-permute-done.8.far_ref
  147.2 0.0 copy-start.7
  147.3 0.0 copy-done.6
  147.3 0.7 copy-done.7
  147.9 4.4 %shard_map.32 = (f32[2,128,128]{2,1,0:T(8,128)}, f32[2,128,128]{2,1,0:T(8,128)}) custom-call(s32[1]{0:T(128)} %bitcast.core_ref, f32[5,128,128]{2,1,0:T(8,128)} %get-tuple-element.29.own_ref, f32[5,64,128]{2,1,0:T(8,128)} %copy-done.6, f32[5,64,128]{2,1,0:T(8,128)} %copy-done.7), custom_call_target="tpu_custom_call" | custom-call | tf_op jit(solution)/shard_map/pallas_call | solution.py:56
  152.3 9.1 %collective-permute-start.9 = (f32[2,128,128]{2,1,0:T(8,128)}, f32[2,128,128]{2,1,0:T(8,128)S(1)}, u32[]{:S(2)}, u32[]{:S(2)}) collective-permute-start(f32[2,128,128]{2,1,0:T(8,128)} %get-tuple-element.31.own_ref), channel_id=1, source_target_pairs={{0,384},{64,448},{128,256},{192,320},{256,128},{320,192},{384,0},{... | collective-permute-start | bytes 393224 | tf_op jit(solution)/shard_map/ppermute | solution.py:269
  161.4 2.1 %shard_map.33.refs_0_ = f32[4,128,128]{2,1,0:T(8,128)} custom-call(s32[1]{0:T(128)} %bitcast.core_ref, f32[4,128,128]{2,1,0:T(8,128)} %get-tuple-element.34.coef_ref.refs_1_, f32[5,128,128]{2,1,0:T(8,128)} %get-tuple-element.35.refs_0_), custom_call_target="tpu_custom_call" | custom-call | tf_op jit(solution)/shard_map/pallas_call | solution.py:56
  163.6 2.3 %shard_map.34 = (f32[3,128,128]{2,1,0:T(8,128)}, f32[3,128,128]{2,1,0:T(8,128)}) custom-call(s32[1]{0:T(128)} %bitcast.core_ref, f32[3,128,128]{2,1,0:T(8,128)} %get-tuple-element.33.coef_ref.refs_2_, f32[4,128,128]{2,1,0:T(8,128)} %shard_map.33.refs_0_, f32[4,128,128]{2,1,0:T(8,128)} %get-tuple-element.34.coef_ref.refs_1_), custom_call_target="tpu_custom_call" | custom-call | tf_op jit(solution)/shard_map/pallas_call | solution.py:56
  165.8 2.3 %shard_map.35 = (f32[2,128,128]{2,1,0:T(8,128)}, f32[2,128,128]{2,1,0:T(8,128)}, f32[2,128,128]{2,1,0:T(8,128)}) custom-call(s32[1]{0:T(128)} %bitcast.core_ref, f32[2,128,128]{2,1,0:T(8,128)} %get-tuple-element.32.coef_ref.refs_3_, f32[3,128,128]{2,1,0:T(8,128)} %get-tuple-element.36.refs_0_, f32[3,128,128]{2,1,0:T(8,128)} %get-tuple-element.37.refs_1_, ...), custom_call_target="tpu_custom_call" | custom-call | tf_op jit(solution)/shard_map/pallas_call | solution.py:56
  168.2 0.0 collective-permute-done.9.sib_ref
  168.2 0.7 copy-done.8
  168.8 5.9 %shard_map.36 = f32[1024,128]{1,0:T(8,128)} custom-call(s32[1]{0:T(128)} %bitcast.core_ref, f32[2,128,128]{2,1,0:T(8,128)} %get-tuple-element.31.own_ref, f32[2,128,128]{2,1,0:T(8,128)} %copy-done.8, f32[5,1024,128]{2,1,0:T(8,128)} %bases_ref.3, f32[1024,128]{1,0:T(8,128)} %targets_ref.3, f32[2,128,128]{2,1,0:T(8,128)} %get-tuple-element.38.refs_0_, ...), custom_call_target="tpu_custom_call" | custom-call | tf_op jit(solution)/shard_map/pallas_call | solution.py:56
  (7 shorter events, 0.1 us)
Async XLA Ops:
  7.8 4.5 %collective-permute-start = (f32[8,20,8,128]{3,2,1,0:T(8,128)}, f32[8,20,8,128]{3,2,1,0:T(8,128)S(1)}, u32[]{:S(2)}, u32[]{:S(2)}) collective-permute-start(f32[8,20,8,128]{3,2,1,0:T(8,128)} %get-tuple-element.24), channel_id=1, source_target_pairs={{0,1},{1,0},{2,3},{3,2},{4,5},{5,4},{6,7},{7,6},{8,9},{9,8},{10,11... | collective-permute-start | bytes 1966088 | tf_op jit(solution)/shard_map/ppermute | solution.py:269
  39.7 5.2 %collective-permute-start.1 = (f32[20,8,128]{2,1,0:T(8,128)S(1)}, f32[20,8,128]{2,1,0:T(8,128)S(1)}, u32[]{:S(2)}, u32[]{:S(2)}) collective-permute-start(f32[20,8,128]{2,1,0:T(8,128)S(1)} %reduce_sum.9), channel_id=1, source_target_pairs={{0,16},{16,0},{32,48},{48,32},{1,17},{17,1},{33,49},{49,33},{2,18}... | collective-permute-start | bytes 245768 | tf_op jit(solution)/shard_map/ppermute | solution.py:269
  66.2 11.5 %copy-start = (f32[208,8,128]{2,1,0:T(8,128)}, f32[208,8,128]{2,1,0:T(8,128)S(1)}, u32[]{:S(2)}) copy-start(f32[208,8,128]{2,1,0:T(8,128)S(1)} %all-gather) | copy-start | bytes 2555908
  66.2 11.5 %collective-permute-start.2 = (f32[8,26,8,128]{3,2,1,0:T(8,128)S(1)}, f32[8,26,8,128]{3,2,1,0:T(8,128)S(1)}, u32[]{:S(2)}, u32[]{:S(2)}) collective-permute-start(f32[8,26,8,128]{3,2,1,0:T(8,128)S(1)} %bitcast.2), channel_id=1, source_target_pairs={{0,1},{1,0},{2,3},{3,2},{4,5},{5,4},{6,7},{7,6},{8,9},{9,8},{10,11... | collective-permute-start | bytes 2555912 | tf_op jit(solution)/shard_map/ppermute | solution.py:269
  77.7 0.9 copy-start.1
  84.6 15.0 %collective-permute-start.3 = (f32[14,64,128]{2,1,0:T(8,128)}, f32[14,64,128]{2,1,0:T(8,128)S(1)}, u32[]{:S(2)}, u32[]{:S(2)}) collective-permute-start(f32[14,64,128]{2,1,0:T(8,128)} %get-tuple-element.26), channel_id=1, source_target_pairs={{0,48},{16,32},{32,16},{48,0},{1,49},{17,33},{33,17},{49,1},{2,50}... | collective-permute-start | bytes 1376264 | tf_op jit(solution)/shard_map/ppermute | solution.py:269
  99.6 4.6 %copy-start.2 = (f32[14,64,128]{2,1,0:T(8,128)}, f32[14,64,128]{2,1,0:T(8,128)S(1)}, u32[]{:S(2)}) copy-start(f32[14,64,128]{2,1,0:T(8,128)S(1)} %collective-permute-done.3.half_ref) | copy-start | bytes 1376260
  99.6 4.6 %collective-permute-start.4 = (f32[14,64,128]{2,1,0:T(8,128)S(1)}, f32[14,64,128]{2,1,0:T(8,128)S(1)}, u32[]{:S(2)}, u32[]{:S(2)}) collective-permute-start(f32[14,64,128]{2,1,0:T(8,128)S(1)} %collective-permute-done.3.half_ref), channel_id=1, source_target_pairs={{0,1},{1,0},{2,3},{3,2},{4,5},{5,4},{6,7},{7,6},{8,9},{9,8},{10,11... | collective-permute-start | bytes 1376264 | tf_op jit(solution)/shard_map/ppermute | solution.py:269
  104.1 0.8 copy-start.3
  110.5 10.3 %collective-permute-start.5 = (f32[9,64,128]{2,1,0:T(8,128)}, f32[9,64,128]{2,1,0:T(8,128)S(1)}, u32[]{:S(2)}, u32[]{:S(2)}) collective-permute-start(f32[9,64,128]{2,1,0:T(8,128)} %get-tuple-element.28), channel_id=1, source_target_pairs={{0,64},{64,0},{128,192},{192,128},{256,320},{320,256},{384,448},{4... | collective-permute-start | bytes 884744 | tf_op jit(solution)/shard_map/ppermute | solution.py:269
  120.8 4.3 %copy-start.4 = (f32[9,64,128]{2,1,0:T(8,128)}, f32[9,64,128]{2,1,0:T(8,128)S(1)}, u32[]{:S(2)}) copy-start(f32[9,64,128]{2,1,0:T(8,128)S(1)} %collective-permute-done.5.half_ref) | copy-start | bytes 884740
  120.8 4.3 %collective-permute-start.6 = (f32[9,64,128]{2,1,0:T(8,128)S(1)}, f32[9,64,128]{2,1,0:T(8,128)S(1)}, u32[]{:S(2)}, u32[]{:S(2)}) collective-permute-start(f32[9,64,128]{2,1,0:T(8,128)S(1)} %collective-permute-done.5.half_ref), channel_id=1, source_target_pairs={{0,1},{1,0},{2,3},{3,2},{4,5},{5,4},{6,7},{7,6},{8,9},{9,8},{10,11... | collective-permute-start | bytes 884744 | tf_op jit(solution)/shard_map/ppermute | solution.py:269
  125.1 0.7 copy-start.5
  130.6 13.3 %collective-permute-start.7 = (f32[5,64,128]{2,1,0:T(8,128)}, f32[5,64,128]{2,1,0:T(8,128)S(1)}, u32[]{:S(2)}, u32[]{:S(2)}) collective-permute-start(f32[5,64,128]{2,1,0:T(8,128)} %get-tuple-element.30), channel_id=1, source_target_pairs={{0,128},{64,192},{128,0},{192,64},{256,384},{320,448},{384,256},{4... | collective-permute-start | bytes 491528 | tf_op jit(solution)/shard_map/ppermute | solution.py:269
  143.9 3.4 %copy-start.6 = (f32[5,64,128]{2,1,0:T(8,128)}, f32[5,64,128]{2,1,0:T(8,128)S(1)}, u32[]{:S(2)}) copy-start(f32[5,64,128]{2,1,0:T(8,128)S(1)} %collective-permute-done.7.half_ref) | copy-start | bytes 491524
  143.9 3.4 %collective-permute-start.8 = (f32[5,64,128]{2,1,0:T(8,128)S(1)}, f32[5,64,128]{2,1,0:T(8,128)S(1)}, u32[]{:S(2)}, u32[]{:S(2)}) collective-permute-start(f32[5,64,128]{2,1,0:T(8,128)S(1)} %collective-permute-done.7.half_ref), channel_id=1, source_target_pairs={{0,1},{1,0},{2,3},{3,2},{4,5},{5,4},{6,7},{7,6},{8,9},{9,8},{10,11... | collective-permute-start | bytes 491528 | tf_op jit(solution)/shard_map/ppermute | solution.py:269
  147.2 0.7 copy-start.7
  152.3 15.8 %collective-permute-start.9 = (f32[2,128,128]{2,1,0:T(8,128)}, f32[2,128,128]{2,1,0:T(8,128)S(1)}, u32[]{:S(2)}, u32[]{:S(2)}) collective-permute-start(f32[2,128,128]{2,1,0:T(8,128)} %get-tuple-element.31.own_ref), channel_id=1, source_target_pairs={{0,384},{64,448},{128,256},{192,320},{256,128},{320,192},{384,0},{... | collective-permute-start | bytes 393224 | tf_op jit(solution)/shard_map/ppermute | solution.py:269
  168.2 0.7 copy-start.8

commit v2 on v1

--- a/solution.py
+++ b/solution.py
@@ -52,14 +52,25 @@
     return dot(left[0], right[0]) + (dot(left[0], right[1]) + dot(left[1], right[0]))
 
 
-def call(body, out_shapes, core, *args, scratch=()):
+GRANT = pltpu.CompilerParams(vmem_limit_bytes=16 * 2**20)
+
+
+def call(body, out_shapes, core, *args, scratch=(), after=()):
+    used = len(args) + 1
+
+    def whole_body(*refs):
+        body(*refs[:used], *refs[used + len(after) :])
+
     outs = pl.pallas_call(
-        body,
+        whole_body,
         out_shape=[jax.ShapeDtypeStruct(shape, jnp.float32) for shape in out_shapes],
-        in_specs=[SMEM_SPEC] + [VMEM_SPEC] * len(args),
+        in_specs=[SMEM_SPEC]
+        + [VMEM_SPEC] * len(args)
+        + [pl.BlockSpec(memory_space=pl.ANY)] * len(after),
         out_specs=[VMEM_SPEC] * len(out_shapes),
         scratch_shapes=[pltpu.VMEM(shape, jnp.float32) for shape in scratch],
-    )(core, *args)
+        compiler_params=GRANT,
+    )(core, *args, *after)
     return list(outs)
 
 
@@ -70,8 +81,8 @@
 GROUPS = (((4, 3), (4, 3, 2, 1, 0, 5)), ((2, 1), (2, 1, 0, 5)), ((0,), (0, 5)))
 
 
-def gram_body(core_ref, bases_ref, targets_ref, keep_ref, send_ref, sum_ref):
-    step = pl.program_id(0)
+def gram_body(core_ref, bases_ref, targets_ref, keep_ref, send_ref):
+    first = core_ref[0] == 0
     parts = [two_parts(bases_ref[level_no]) for level_no in range(LEVELS)]
     parts.append(two_parts(targets_ref[...]))
 
@@ -89,39 +100,16 @@
             for m_no, field in enumerate(row_order(level_no)):
                 to = rights.index(field)
                 value = block[top * K : (top + 1) * K, to * K : (to + 1) * K]
-                tiles = value.reshape(2, CHIPS, TILE, K)
+                low = value[:HALF].reshape(CHIPS, TILE, K)
+                high = value[HALF:].reshape(CHIPS, TILE, K)
                 at = starts[level_no] + m_no
-
-                @pl.when(step == 0)
-                def _():
-                    sum_ref[:, :, at] = tiles
-
-                @pl.when(step > 0)
-                def _():
-                    sum_ref[:, :, at] += tiles
-
-    @pl.when(step == pl.num_programs(0) - 1)
-    def _():
-        keep_ref[...] = sum_ref[core_ref[0]]
-        send_ref[...] = sum_ref[1 - core_ref[0]]
-
-
-def local_grams(core, bases, targets, block=512):
-    rows = bases.shape[1]
+                keep_ref[:, at] = jnp.where(first, low, high)
+                send_ref[:, at] = jnp.where(first, high, low)
+
+
+def local_grams(core, bases, targets):
     shape = (CHIPS, TOTAL, TILE, K)
-    whole = pl.BlockSpec(shape, lambda i: (0, 0, 0, 0))
-    return pl.pallas_call(
-        gram_body,
-        grid=(rows // block,),
-        out_shape=[jax.ShapeDtypeStruct(shape, jnp.float32)] * 2,
-        in_specs=[
-            SMEM_SPEC,
-            pl.BlockSpec((LEVELS, block, K), lambda i: (0, i, 0)),
-            pl.BlockSpec((block, K), lambda i: (i, 0)),
-        ],
-        out_specs=[whole, whole],
-        scratch_shapes=[pltpu.VMEM((2,) + shape, jnp.float32)],
-    )(core, bases, targets)
+    return call(gram_body, [shape, shape], core, bases, targets)
 
 
 def inverse_of_complement(product, work_ref):
@@ -248,20 +236,30 @@
         put_wide(new_ref, 0, old - mm(old_ref[level_no], coef))
 
 
-def coarsest_body(core_ref, own_ref, sib_ref, bases_ref, targets_ref, *refs):
-    olds, out_ref, work_ref = refs[:-2], refs[-2], refs[-1]
-    coef, _ = solve_pair(own_ref[0], sib_ref[0], own_ref[1], sib_ref[1], work_ref)
+def tail_body(core_ref, coef_ref, bases_ref, targets_ref, *refs):
+    olds, (base_ref, rest_ref) = refs[:-2], refs[-2:]
+    coef = wide_of(coef_ref, 0, 2)
     mults = [coef]
     for old_ref in reversed(olds):
-        mults.append(old_ref[1] - mm(old_ref[0], coef))
+        old = jnp.concatenate([old_ref[0], old_ref[2]], 1)
+        mults.append(old - mm(old_ref[1], coef))
     tall = two_parts(jnp.concatenate(mults, 0))
     rows = targets_ref.shape[0]
     block = 256
     for first in range(0, rows, block):
         some = pl.ds(first, block)
-        wide = [bases_ref[level_no, some] for level_no in range(LEVELS)]
+        wide = [bases_ref[level_no, some] for level_no in range(1, LEVELS)]
         wide = two_parts(jnp.concatenate(wide, 1))
-        out_ref[some] = targets_ref[some] - dot_parts(wide, tall, ((1,), (0,)))
+        taken = dot_parts(wide, tall, ((1,), (0,)))
+        base_ref[some] = bases_ref[0, some] - taken[:, :K]
+        rest_ref[some] = targets_ref[some] - taken[:, K:]
+
+
+def coarsest_body(core_ref, own_ref, sib_ref, base_ref, rest_ref, out_ref, work_ref):
+    inverse = inverse_of_complement(mm(sib_ref[0], own_ref[0]), work_ref)
+    coef = mm(inverse, sib_ref[1] - mm(sib_ref[0], own_ref[1]))
+    taken = dot_parts(two_parts(base_ref[...]), two_parts(coef), ((1,), (0,)))
+    out_ref[...] = rest_ref[...] - taken
 
 
 def swap(value, axis, partner):
@@ -304,6 +302,7 @@
         scratch=[WORK, (piece.shape[0], K, K)],
     )
     mults = [coef]
+    folded = []
     for level_no in range(top - 1, 0, -1):
         half = swap(send, *PARTNERS[level_no])
         far = swap_cores(half)
@@ -319,19 +318,24 @@
             half,
             far,
             scratch=[WORK, own.shape],
+            after=folded,
         )
         own, send, coef = outs[0], outs[-2], outs[-1]
-        folded = call(
-            functools.partial(fold_body, level_no),
-            [(level_no + 1, K, K)] * len(mults),
-            core,
-            coef,
-            *mults,
-        )
-        mults = folded + [coef]
+        if level_no > 1:
+            folded = call(
+                functools.partial(fold_body, level_no),
+                [(level_no + 1, K, K)] * len(mults),
+                core,
+                coef,
+                *mults,
+            )
+            mults = folded + [coef]
     sib = swap(own, *PARTNERS[0])
+    base, rest = call(
+        tail_body, [targets.shape, targets.shape], core, coef, bases, targets, *mults
+    )
     (solved,) = call(
-        coarsest_body, [targets.shape], core, own, sib, bases, targets, *mults, scratch=[WORK]
+        coarsest_body, [targets.shape], core, own, sib, base, rest, scratch=[WORK]
     )
     return solved
 

time: 175 us -> 152 us (0.87)
  the two profiles are of different devices: /device:TPU:71 before, /device:TPU:135 now
where the time goes in v2:
time: 152 us
  blocking collectives  47.5 us (31%)
  starting transfers between devices  41.1 us (27%)
  waiting for transfers between devices  40.8 us (27%)
  Pallas kernels  19.4 us (13%)
  local copies, waits for them, and re-layouts  2.8 us (2%)
    ppermute x10, starting transfers between devices, swap(): return lax.ppermute(value, axis, pairs)  41.1 us
    ppermute x10, waiting for transfers between devices, swap(): return lax.ppermute(value, axis, pairs)  40.8 us
    all_to_all x1, blocking collectives, per_device(): part = lax.all_to_all(part, 'y', 0, 0).sum(0)  26.2 us
    all_gather x1, blocking collectives, gather_chips(): return lax.all_gather(piece, 'y')  21.3 us
    pallas_call x9, Pallas kernels, call(): pl.pallas_call(whole_body, out_shape=[jax.ShapeDtypeStruct(shape, jnp.flo...  19.4 us
  transfers between devices with their start and end apart: 10, of which 10 were waited for; matrix products, arithmetic and copies ran while one was open for 0% of the time, Pallas kernels for 2%

profile of v2, /device:TPU:135, one launch (start us, length us, event | category | flops | bytes accessed | tf_op | source)
XLA Modules:
  0.0 151.9 jit_solution(158706779164658569)
XLA Ops:
  0.0 0.0 copy-start
  0.0 1.7 %copy-done = f32[5,1024,128]{2,1,0:T(8,128)S(1)} copy-done((f32[5,1024,128]{2,1,0:T(8,128)S(1)}, f32[5,1024,128]{2,1,0:T(8,128)}, u32[]{:S(2)}) %copy-start) | copy-done | bytes 2621464
  1.7 0.0 copy-start.2
  1.7 1.0 copy-done.2
  2.8 2.5 %shard_map.28 = (f32[8,20,8,128]{3,2,1,0:T(8,128)S(1)}, f32[8,20,8,128]{3,2,1,0:T(8,128)S(1)}) custom-call(s32[1]{0:T(128)} %bitcast.refs_0_, f32[5,1024,128]{2,1,0:T(8,128)S(1)} %copy-done, f32[1024,128]{1,0:T(8,128)S(1)} %copy-done.2), custom_call_target="tpu_custom_call" | custom-call | tf_op jit(solution)/shard_map/pallas_call | solution.py:64
  5.3 2.6 %collective-permute-start = (f32[8,20,8,128]{3,2,1,0:T(8,128)S(1)}, f32[8,20,8,128]{3,2,1,0:T(8,128)S(1)}, u32[]{:S(2)}, u32[]{:S(2)}) collective-permute-start(f32[8,20,8,128]{3,2,1,0:T(8,128)S(1)} %get-tuple-element.23), channel_id=1, source_target_pairs={{0,1},{1,0},{2,3},{3,2},{4,5},{5,4},{6,7},{7,6},{8,9},{9,8},{10,11... | collective-permute-start | bytes 1966088 | tf_op jit(solution)/shard_map/ppermute | solution.py:267
  7.9 1.7 %collective-permute-done = f32[8,20,8,128]{3,2,1,0:T(8,128)S(1)} collective-permute-done((f32[8,20,8,128]{3,2,1,0:T(8,128)S(1)}, f32[8,20,8,128]{3,2,1,0:T(8,128)S(1)}, u32[]{:S(2)}, u32[]{:S(2)}) %collective-permute-start) | collective-permute-done | bytes 655392 | tf_op jit(solution)/shard_map/ppermute | solution.py:267
  9.6 0.1 add.6
  9.7 26.2 %all_to_all.5 = f32[8,20,8,128]{3,2,1,0:T(8,128)S(1)} all-to-all(f32[8,20,8,128]{3,2,1,0:T(8,128)S(1)} %add.6), channel_id=1, replica_groups=mesh['z'=8,'x'=4,'y'=8,'c'=2] {'y'}, dimensions={0} | all-to-all | bytes 1310720 | tf_op jit(solution)/shard_map/all_to_all | solution.py:290
  35.9 2.5 %collective-permute-start.1 = (f32[20,8,128]{2,1,0:T(8,128)S(1)}, f32[20,8,128]{2,1,0:T(8,128)S(1)}, u32[]{:S(2)}, u32[]{:S(2)}) collective-permute-start(f32[20,8,128]{2,1,0:T(8,128)S(1)} %reduce_sum.9), channel_id=1, source_target_pairs={{0,16},{16,0},{32,48},{48,32},{1,17},{17,1},{33,49},{49,33},{2,18}... | collective-permute-start | bytes 245768 | tf_op jit(solution)/shard_map/ppermute | solution.py:267
  38.4 2.7 %collective-permute-done.1 = f32[20,8,128]{2,1,0:T(8,128)S(1)} collective-permute-done((f32[20,8,128]{2,1,0:T(8,128)S(1)}, f32[20,8,128]{2,1,0:T(8,128)S(1)}, u32[]{:S(2)}, u32[]{:S(2)}) %collective-permute-start.1) | collective-permute-done | bytes 81952 | tf_op jit(solution)/shard_map/ppermute | solution.py:267
  41.1 21.3 %all-gather = f32[208,8,128]{2,1,0:T(8,128)S(1)} all-gather(f32[26,8,128]{2,1,0:T(8,128)S(1)} %pad_maximum_fusion), channel_id=2, replica_groups=mesh['z'=8,'x'=4,'y'=8,'c'=2] {'y'}, dimensions={0}, use_global_device_ids=true | all-gather | bytes 958464 | tf_op jit(solution)/shard_map/all_gather | solution.py:344
  62.4 9.5 %collective-permute-start.2 = (f32[8,26,8,128]{3,2,1,0:T(8,128)S(1)}, f32[8,26,8,128]{3,2,1,0:T(8,128)S(1)}, u32[]{:S(2)}, u32[]{:S(2)}) collective-permute-start(f32[8,26,8,128]{3,2,1,0:T(8,128)S(1)} %bitcast.2), channel_id=1, source_target_pairs={{0,1},{1,0},{2,3},{3,2},{4,5},{5,4},{6,7},{7,6},{8,9},{9,8},{10,11... | collective-permute-start | bytes 2555912 | tf_op jit(solution)/shard_map/ppermute | solution.py:267
  72.0 2.0 %collective-permute-done.2.refs_2_ = f32[8,26,8,128]{3,2,1,0:T(8,128)S(1)} collective-permute-done((f32[8,26,8,128]{3,2,1,0:T(8,128)S(1)}, f32[8,26,8,128]{3,2,1,0:T(8,128)S(1)}, u32[]{:S(2)}, u32[]{:S(2)}) %collective-permute-start.2) | collective-permute-done | bytes 852000 | tf_op jit(solution)/shard_map/ppermute | solution.py:267
  74.0 3.4 %shard_map.29 = (f32[14,128,128]{2,1,0:T(8,128)S(1)}, f32[14,64,128]{2,1,0:T(8,128)S(1)}, f32[5,128,128]{2,1,0:T(8,128)S(1)}) custom-call(s32[1]{0:T(128)} %bitcast.refs_0_, f32[8,26,8,128]{3,2,1,0:T(8,128)S(1)} %bitcast.3, f32[8,26,8,128]{3,2,1,0:T(8,128)S(1)} %collective-permute-done.2.refs_2_), custom_call_target="tpu_custom_call" | custom-call | tf_op jit(solution)/shard_map/pallas_call | solution.py:64
  77.4 2.1 %collective-permute-start.3 = (f32[14,64,128]{2,1,0:T(8,128)S(1)}, f32[14,64,128]{2,1,0:T(8,128)S(1)}, u32[]{:S(2)}, u32[]{:S(2)}) collective-permute-start(f32[14,64,128]{2,1,0:T(8,128)S(1)} %get-tuple-element.25), channel_id=1, source_target_pairs={{0,48},{16,32},{32,16},{48,0},{1,49},{17,33},{33,17},{49,1},{2,50}... | collective-permute-start | bytes 1376264 | tf_op jit(solution)/shard_map/ppermute | solution.py:267
  79.5 12.7 %collective-permute-done.3.refs_2_ = f32[14,64,128]{2,1,0:T(8,128)S(1)} collective-permute-done((f32[14,64,128]{2,1,0:T(8,128)S(1)}, f32[14,64,128]{2,1,0:T(8,128)S(1)}, u32[]{:S(2)}, u32[]{:S(2)}) %collective-permute-start.3) | collective-permute-done | bytes 458784 | tf_op jit(solution)/shard_map/ppermute | solution.py:267
  92.2 3.1 %collective-permute-start.4 = (f32[14,64,128]{2,1,0:T(8,128)S(1)}, f32[14,64,128]{2,1,0:T(8,128)S(1)}, u32[]{:S(2)}, u32[]{:S(2)}) collective-permute-start(f32[14,64,128]{2,1,0:T(8,128)S(1)} %collective-permute-done.3.refs_2_), channel_id=1, source_target_pairs={{0,1},{1,0},{2,3},{3,2},{4,5},{5,4},{6,7},{7,6},{8,9},{9,8},{10,11... | collective-permute-start | bytes 1376264 | tf_op jit(solution)/shard_map/ppermute | solution.py:267
  95.3 1.4 collective-permute-done.4.refs_3_
  96.7 0.0 copy-start.1
  96.7 0.0 copy-start.3
  96.7 3.2 %shard_map.30 = (f32[9,128,128]{2,1,0:T(8,128)S(1)}, f32[9,64,128]{2,1,0:T(8,128)S(1)}, f32[4,128,128]{2,1,0:T(8,128)S(1)}) custom-call(s32[1]{0:T(128)} %bitcast.refs_0_, f32[14,128,128]{2,1,0:T(8,128)S(1)} %get-tuple-element.24.refs_1_, f32[14,64,128]{2,1,0:T(8,128)S(1)} %collective-permute-done.3.refs_2_, f32[14,64,128]{2,1,0:T(8,128)S(1)} %collective-permute-done.4.refs_3_), custom_call_target="tpu_custom_call" | custom-call | tf_op jit(solution)/shard_map/pallas_call | solution.py:64
  99.9 4.0 %collective-permute-start.5 = (f32[9,64,128]{2,1,0:T(8,128)S(1)}, f32[9,64,128]{2,1,0:T(8,128)S(1)}, u32[]{:S(2)}, u32[]{:S(2)}) collective-permute-start(f32[9,64,128]{2,1,0:T(8,128)S(1)} %get-tuple-element.27), channel_id=1, source_target_pairs={{0,64},{64,0},{128,192},{192,128},{256,320},{320,256},{384,448},{4... | collective-permute-start | bytes 884744 | tf_op jit(solution)/shard_map/ppermute | solution.py:267
  103.9 7.0 %collective-permute-done.5.refs_2_ = f32[9,64,128]{2,1,0:T(8,128)S(1)} collective-permute-done((f32[9,64,128]{2,1,0:T(8,128)S(1)}, f32[9,64,128]{2,1,0:T(8,128)S(1)}, u32[]{:S(2)}, u32[]{:S(2)}) %collective-permute-start.5) | collective-permute-done | bytes 294944 | tf_op jit(solution)/shard_map/ppermute | solution.py:267
  110.9 2.9 %collective-permute-start.6 = (f32[9,64,128]{2,1,0:T(8,128)S(1)}, f32[9,64,128]{2,1,0:T(8,128)S(1)}, u32[]{:S(2)}, u32[]{:S(2)}) collective-permute-start(f32[9,64,128]{2,1,0:T(8,128)S(1)} %collective-permute-done.5.refs_2_), channel_id=1, source_target_pairs={{0,1},{1,0},{2,3},{3,2},{4,5},{5,4},{6,7},{7,6},{8,9},{9,8},{10,11... | collective-permute-start | bytes 884744 | tf_op jit(solution)/shard_map/ppermute | solution.py:267
  113.7 0.4 shard_map.31.refs_4_.refs_2_
  114.1 0.8 collective-permute-done.6.refs_3_
  114.9 2.7 %shard_map.32 = (f32[5,128,128]{2,1,0:T(8,128)S(1)}, f32[5,64,128]{2,1,0:T(8,128)S(1)}, f32[3,128,128]{2,1,0:T(8,128)S(1)}) custom-call(s32[1]{0:T(128)} %bitcast.refs_0_, f32[9,128,128]{2,1,0:T(8,128)S(1)} %get-tuple-element.26.refs_1_, f32[9,64,128]{2,1,0:T(8,128)S(1)} %collective-permute-done.5.refs_2_, f32[9,64,128]{2,1,0:T(8,128)S(1)} %collective-permute-done.6.refs_3_, ...), custom_call_target="tpu_custom_call" | custom-call | tf_op jit(solution)/shard_map/pallas_call | solution.py:64
  117.7 1.9 %collective-permute-start.7 = (f32[5,64,128]{2,1,0:T(8,128)S(1)}, f32[5,64,128]{2,1,0:T(8,128)S(1)}, u32[]{:S(2)}, u32[]{:S(2)}) collective-permute-start(f32[5,64,128]{2,1,0:T(8,128)S(1)} %get-tuple-element.31), channel_id=1, source_target_pairs={{0,128},{64,192},{128,0},{192,64},{256,384},{320,448},{384,256},{4... | collective-permute-start | bytes 491528 | tf_op jit(solution)/shard_map/ppermute | solution.py:267
  119.6 6.9 %collective-permute-done.7.refs_2_ = f32[5,64,128]{2,1,0:T(8,128)S(1)} collective-permute-done((f32[5,64,128]{2,1,0:T(8,128)S(1)}, f32[5,64,128]{2,1,0:T(8,128)S(1)}, u32[]{:S(2)}, u32[]{:S(2)}) %collective-permute-start.7) | collective-permute-done | bytes 163872 | tf_op jit(solution)/shard_map/ppermute | solution.py:267
  126.5 3.0 %collective-permute-start.8 = (f32[5,64,128]{2,1,0:T(8,128)S(1)}, f32[5,64,128]{2,1,0:T(8,128)S(1)}, u32[]{:S(2)}, u32[]{:S(2)}) collective-permute-start(f32[5,64,128]{2,1,0:T(8,128)S(1)} %collective-permute-done.7.refs_2_), channel_id=1, source_target_pairs={{0,1},{1,0},{2,3},{3,2},{4,5},{5,4},{6,7},{7,6},{8,9},{9,8},{10,11... | collective-permute-start | bytes 491528 | tf_op jit(solution)/shard_map/ppermute | solution.py:267
  129.6 0.5 shard_map.33
  130.1 0.4 collective-permute-done.8.refs_3_
  130.4 2.5 %shard_map.34 = (f32[2,128,128]{2,1,0:T(8,128)S(1)}, f32[2,128,128]{2,1,0:T(8,128)S(1)}) custom-call(s32[1]{0:T(128)} %bitcast.refs_0_, f32[5,128,128]{2,1,0:T(8,128)S(1)} %get-tuple-element.30.refs_1_, f32[5,64,128]{2,1,0:T(8,128)S(1)} %collective-permute-done.7.refs_2_, f32[5,64,128]{2,1,0:T(8,128)S(1)} %collective-permute-done.8.refs_3_, ...), custom_call_target="tpu_custom_call" | custom-call | tf_op jit(solution)/shard_map/pallas_call | solution.py:64
  132.9 9.5 %collective-permute-start.9 = (f32[2,128,128]{2,1,0:T(8,128)S(1)}, f32[2,128,128]{2,1,0:T(8,128)S(1)}, u32[]{:S(2)}, u32[]{:S(2)}) collective-permute-start(f32[2,128,128]{2,1,0:T(8,128)S(1)} %get-tuple-element.35.refs_1_), channel_id=1, source_target_pairs={{0,384},{64,448},{128,256},{192,320},{256,128},{320,192},{384,0},{... | collective-permute-start | bytes 393224 | tf_op jit(solution)/shard_map/ppermute | solution.py:267
  142.4 0.0 copy-done.1
  142.4 0.0 copy-done.3
  142.4 1.5 %shard_map.35 = (f32[1024,128]{1,0:T(8,128)S(1)}, f32[1024,128]{1,0:T(8,128)S(1)}) custom-call(s32[1]{0:T(128)} %bitcast.refs_0_, f32[2,128,128]{2,1,0:T(8,128)S(1)} %get-tuple-element.36.refs_1_, f32[5,1024,128]{2,1,0:T(8,128)S(1)} %copy-done.1, f32[1024,128]{1,0:T(8,128)S(1)} %copy-done.3, f32[3,128,128]{2,1,0:T(8,128)S(1)} %get-tuple-element.33.refs_4_, ...), custom_call_target="tpu_custom_call" | custom-call | tf_op jit(solution)/shard_map/pallas_call | solution.py:64
  144.0 5.2 %collective-permute-done.9.refs_2_ = f32[2,128,128]{2,1,0:T(8,128)S(1)} collective-permute-done((f32[2,128,128]{2,1,0:T(8,128)S(1)}, f32[2,128,128]{2,1,0:T(8,128)S(1)}, u32[]{:S(2)}, u32[]{:S(2)}) %collective-permute-start.9) | collective-permute-done | bytes 131104 | tf_op jit(solution)/shard_map/ppermute | solution.py:267
  149.2 2.7 %shard_map.36 = f32[1024,128]{1,0:T(8,128)} custom-call(s32[1]{0:T(128)} %bitcast.refs_0_, f32[2,128,128]{2,1,0:T(8,128)S(1)} %get-tuple-element.35.refs_1_, f32[2,128,128]{2,1,0:T(8,128)S(1)} %collective-permute-done.9.refs_2_, f32[1024,128]{1,0:T(8,128)S(1)} %get-tuple-element.37.refs_3_, f32[1024,128]{1,0:T(8,128)S(1)} %get-tuple-element.38.refs_4_), custom_call_target="tpu_custom_call" | custom-call | tf_op jit(solution)/shard_map/pallas_call | solution.py:64
  (5 shorter events, 0.1 us)
Async XLA Ops:
  0.0 1.7 %copy-start = (f32[5,1024,128]{2,1,0:T(8,128)S(1)}, f32[5,1024,128]{2,1,0:T(8,128)}, u32[]{:S(2)}) copy-start(f32[5,1024,128]{2,1,0:T(8,128)} %refs_2_.3) | copy-start | bytes 7864324
  1.7 1.0 copy-start.2
  5.3 4.3 %collective-permute-start = (f32[8,20,8,128]{3,2,1,0:T(8,128)S(1)}, f32[8,20,8,128]{3,2,1,0:T(8,128)S(1)}, u32[]{:S(2)}, u32[]{:S(2)}) collective-permute-start(f32[8,20,8,128]{3,2,1,0:T(8,128)S(1)} %get-tuple-element.23), channel_id=1, source_target_pairs={{0,1},{1,0},{2,3},{3,2},{4,5},{5,4},{6,7},{7,6},{8,9},{9,8},{10,11... | collective-permute-start | bytes 1966088 | tf_op jit(solution)/shard_map/ppermute | solution.py:267
  35.9 5.2 %collective-permute-start.1 = (f32[20,8,128]{2,1,0:T(8,128)S(1)}, f32[20,8,128]{2,1,0:T(8,128)S(1)}, u32[]{:S(2)}, u32[]{:S(2)}) collective-permute-start(f32[20,8,128]{2,1,0:T(8,128)S(1)} %reduce_sum.9), channel_id=1, source_target_pairs={{0,16},{16,0},{32,48},{48,32},{1,17},{17,1},{33,49},{49,33},{2,18}... | collective-permute-start | bytes 245768 | tf_op jit(solution)/shard_map/ppermute | solution.py:267
  62.4 11.5 %collective-permute-start.2 = (f32[8,26,8,128]{3,2,1,0:T(8,128)S(1)}, f32[8,26,8,128]{3,2,1,0:T(8,128)S(1)}, u32[]{:S(2)}, u32[]{:S(2)}) collective-permute-start(f32[8,26,8,128]{3,2,1,0:T(8,128)S(1)} %bitcast.2), channel_id=1, source_target_pairs={{0,1},{1,0},{2,3},{3,2},{4,5},{5,4},{6,7},{7,6},{8,9},{9,8},{10,11... | collective-permute-start | bytes 2555912 | tf_op jit(solution)/shard_map/ppermute | solution.py:267
  77.4 14.8 %collective-permute-start.3 = (f32[14,64,128]{2,1,0:T(8,128)S(1)}, f32[14,64,128]{2,1,0:T(8,128)S(1)}, u32[]{:S(2)}, u32[]{:S(2)}) collective-permute-start(f32[14,64,128]{2,1,0:T(8,128)S(1)} %get-tuple-element.25), channel_id=1, source_target_pairs={{0,48},{16,32},{32,16},{48,0},{1,49},{17,33},{33,17},{49,1},{2,50}... | collective-permute-start | bytes 1376264 | tf_op jit(solution)/shard_map/ppermute | solution.py:267
  92.2 4.6 %collective-permute-start.4 = (f32[14,64,128]{2,1,0:T(8,128)S(1)}, f32[14,64,128]{2,1,0:T(8,128)S(1)}, u32[]{:S(2)}, u32[]{:S(2)}) collective-permute-start(f32[14,64,128]{2,1,0:T(8,128)S(1)} %collective-permute-done.3.refs_2_), channel_id=1, source_target_pairs={{0,1},{1,0},{2,3},{3,2},{4,5},{5,4},{6,7},{7,6},{8,9},{9,8},{10,11... | collective-permute-start | bytes 1376264 | tf_op jit(solution)/shard_map/ppermute | solution.py:267
  96.7 45.7 %copy-start.1 = (f32[5,1024,128]{2,1,0:T(8,128)S(1)}, f32[5,1024,128]{2,1,0:T(8,128)}, u32[]{:S(2)}) copy-start(f32[5,1024,128]{2,1,0:T(8,128)} %refs_2_.3) | copy-start | bytes 7864324
  96.7 45.7 %copy-start.3 = (f32[1024,128]{1,0:T(8,128)S(1)}, f32[1024,128]{1,0:T(8,128)}, u32[]{:S(2)}) copy-start(f32[1024,128]{1,0:T(8,128)} %refs_3_.1) | copy-start | bytes 1572868
  99.9 11.0 %collective-permute-start.5 = (f32[9,64,128]{2,1,0:T(8,128)S(1)}, f32[9,64,128]{2,1,0:T(8,128)S(1)}, u32[]{:S(2)}, u32[]{:S(2)}) collective-permute-start(f32[9,64,128]{2,1,0:T(8,128)S(1)} %get-tuple-element.27), channel_id=1, source_target_pairs={{0,64},{64,0},{128,192},{192,128},{256,320},{320,256},{384,448},{4... | collective-permute-start | bytes 884744 | tf_op jit(solution)/shard_map/ppermute | solution.py:267
  110.9 4.1 %collective-permute-start.6 = (f32[9,64,128]{2,1,0:T(8,128)S(1)}, f32[9,64,128]{2,1,0:T(8,128)S(1)}, u32[]{:S(2)}, u32[]{:S(2)}) collective-permute-start(f32[9,64,128]{2,1,0:T(8,128)S(1)} %collective-permute-done.5.refs_2_), channel_id=1, source_target_pairs={{0,1},{1,0},{2,3},{3,2},{4,5},{5,4},{6,7},{7,6},{8,9},{9,8},{10,11... | collective-permute-start | bytes 884744 | tf_op jit(solution)/shard_map/ppermute | solution.py:267
  117.7 8.9 %collective-permute-start.7 = (f32[5,64,128]{2,1,0:T(8,128)S(1)}, f32[5,64,128]{2,1,0:T(8,128)S(1)}, u32[]{:S(2)}, u32[]{:S(2)}) collective-permute-start(f32[5,64,128]{2,1,0:T(8,128)S(1)} %get-tuple-element.31), channel_id=1, source_target_pairs={{0,128},{64,192},{128,0},{192,64},{256,384},{320,448},{384,256},{4... | collective-permute-start | bytes 491528 | tf_op jit(solution)/shard_map/ppermute | solution.py:267
  126.5 3.9 %collective-permute-start.8 = (f32[5,64,128]{2,1,0:T(8,128)S(1)}, f32[5,64,128]{2,1,0:T(8,128)S(1)}, u32[]{:S(2)}, u32[]{:S(2)}) collective-permute-start(f32[5,64,128]{2,1,0:T(8,128)S(1)} %collective-permute-done.7.refs_2_), channel_id=1, source_target_pairs={{0,1},{1,0},{2,3},{3,2},{4,5},{5,4},{6,7},{7,6},{8,9},{9,8},{10,11... | collective-permute-start | bytes 491528 | tf_op jit(solution)/shard_map/ppermute | solution.py:267
  132.9 16.3 %collective-permute-start.9 = (f32[2,128,128]{2,1,0:T(8,128)S(1)}, f32[2,128,128]{2,1,0:T(8,128)S(1)}, u32[]{:S(2)}, u32[]{:S(2)}) collective-permute-start(f32[2,128,128]{2,1,0:T(8,128)S(1)} %get-tuple-element.35.refs_1_), channel_id=1, source_target_pairs={{0,384},{64,448},{128,256},{192,320},{256,128},{320,192},{384,0},{... | collective-permute-start | bytes 393224 | tf_op jit(solution)/shard_map/ppermute | solution.py:267

commit v3 on v2

--- a/solution.py
+++ b/solution.py
@@ -13,7 +13,6 @@
 HALF = K // 2
 AXES = ("z", "x", "y", "c")
 SIZES = (8, 4, 8, 2)
-HIGHEST = lax.Precision.HIGHEST
 VMEM_SPEC = pl.BlockSpec(memory_space=pltpu.VMEM)
 SMEM_SPEC = pl.BlockSpec(memory_space=pltpu.SMEM)
 
@@ -26,20 +25,6 @@
     return sum(below + 2 for below in range(level_no + 1))
 
 
-def mm(left, right):
-    return jnp.dot(left, right, preferred_element_type=jnp.float32, precision=HIGHEST)
-
-
-def mtm(left, right):
-    return lax.dot_general(
-        left,
-        right,
-        (((0,), (0,)), ((), ())),
-        preferred_element_type=jnp.float32,
-        precision=HIGHEST,
-    )
-
-
 def two_parts(value):
     high = value.astype(jnp.bfloat16)
     return high, (value - high.astype(jnp.float32)).astype(jnp.bfloat16)
@@ -50,6 +35,14 @@
         lax.dot_general, dimension_numbers=(dims, ((), ())), preferred_element_type=jnp.float32
     )
     return dot(left[0], right[0]) + (dot(left[0], right[1]) + dot(left[1], right[0]))
+
+
+def mm(left, right):
+    return dot_parts(two_parts(left), two_parts(right), ((1,), (0,)))
+
+
+def mtm(left, right):
+    return dot_parts(two_parts(left), two_parts(right), ((0,), (0,)))
 
 
 GRANT = pltpu.CompilerParams(vmem_limit_bytes=16 * 2**20)

time: 152 us -> 149 us (0.980)
  Pallas kernels: 19.4 us -> 15.5 us
    pallas_call x9, Pallas kernels: 19.4 us -> 15.5 us  [call(): pl.pallas_call(whole_body, out_shape=[jax.ShapeDtypeStruct(shape, jnp.flo...]
  transfers between devices with their start and end apart: 10 -> 10, of which waited for: 10 -> 10; matrix products, arithmetic and copies ran while one was open for 0% -> 0% of each run, Pallas kernels for 2% -> 1%
where the time goes in v3:
time: 149 us
  blocking collectives  47.5 us (32%)
  waiting for transfers between devices  41.5 us (28%)
  starting transfers between devices  40.9 us (27%)
  Pallas kernels  15.5 us (10%)
  local copies, waits for them, and re-layouts  2.8 us (2%)
    ppermute x10, waiting for transfers between devices, swap(): return lax.ppermute(value, axis, pairs)  41.5 us
    ppermute x10, starting transfers between devices, swap(): return lax.ppermute(value, axis, pairs)  40.9 us
    all_to_all x1, blocking collectives, per_device(): part = lax.all_to_all(part, 'y', 0, 0).sum(0)  26.2 us
    all_gather x1, blocking collectives, gather_chips(): return lax.all_gather(piece, 'y')  21.3 us
    pallas_call x9, Pallas kernels, call(): pl.pallas_call(whole_body, out_shape=[jax.ShapeDtypeStruct(shape, jnp.flo...  15.5 us
  transfers between devices with their start and end apart: 10, of which 10 were waited for; matrix products, arithmetic and copies ran while one was open for 0% of the time, Pallas kernels for 1%

profile of v3, /device:TPU:135, one launch (start us, length us, event | category | flops | bytes accessed | tf_op | source)
XLA Modules:
  0.0 148.5 jit_solution(10734147181262810098)
XLA Ops:
  0.0 0.0 copy-start
  0.0 1.7 %copy-done = f32[5,1024,128]{2,1,0:T(8,128)S(1)} copy-done((f32[5,1024,128]{2,1,0:T(8,128)S(1)}, f32[5,1024,128]{2,1,0:T(8,128)}, u32[]{:S(2)}) %copy-start) | copy-done | bytes 2621464
  1.7 0.0 copy-start.2
  1.7 1.0 copy-done.2
  2.8 2.5 %shard_map.28 = (f32[8,20,8,128]{3,2,1,0:T(8,128)S(1)}, f32[8,20,8,128]{3,2,1,0:T(8,128)S(1)}) custom-call(s32[1]{0:T(128)} %bitcast.refs_0_, f32[5,1024,128]{2,1,0:T(8,128)S(1)} %copy-done, f32[1024,128]{1,0:T(8,128)S(1)} %copy-done.2), custom_call_target="tpu_custom_call" | custom-call | tf_op jit(solution)/shard_map/pallas_call | solution.py:57
  5.3 2.6 %collective-permute-start = (f32[8,20,8,128]{3,2,1,0:T(8,128)S(1)}, f32[8,20,8,128]{3,2,1,0:T(8,128)S(1)}, u32[]{:S(2)}, u32[]{:S(2)}) collective-permute-start(f32[8,20,8,128]{3,2,1,0:T(8,128)S(1)} %get-tuple-element.23), channel_id=1, source_target_pairs={{0,1},{1,0},{2,3},{3,2},{4,5},{5,4},{6,7},{7,6},{8,9},{9,8},{10,11... | collective-permute-start | bytes 1966088 | tf_op jit(solution)/shard_map/ppermute | solution.py:260
  7.9 1.7 %collective-permute-done = f32[8,20,8,128]{3,2,1,0:T(8,128)S(1)} collective-permute-done((f32[8,20,8,128]{3,2,1,0:T(8,128)S(1)}, f32[8,20,8,128]{3,2,1,0:T(8,128)S(1)}, u32[]{:S(2)}, u32[]{:S(2)}) %collective-permute-start) | collective-permute-done | bytes 655392 | tf_op jit(solution)/shard_map/ppermute | solution.py:260
  9.6 0.1 add.6
  9.7 26.2 %all_to_all.5 = f32[8,20,8,128]{3,2,1,0:T(8,128)S(1)} all-to-all(f32[8,20,8,128]{3,2,1,0:T(8,128)S(1)} %add.6), channel_id=1, replica_groups=mesh['z'=8,'x'=4,'y'=8,'c'=2] {'y'}, dimensions={0} | all-to-all | bytes 1310720 | tf_op jit(solution)/shard_map/all_to_all | solution.py:283
  35.9 2.5 %collective-permute-start.1 = (f32[20,8,128]{2,1,0:T(8,128)S(1)}, f32[20,8,128]{2,1,0:T(8,128)S(1)}, u32[]{:S(2)}, u32[]{:S(2)}) collective-permute-start(f32[20,8,128]{2,1,0:T(8,128)S(1)} %reduce_sum.9), channel_id=1, source_target_pairs={{0,16},{16,0},{32,48},{48,32},{1,17},{17,1},{33,49},{49,33},{2,18}... | collective-permute-start | bytes 245768 | tf_op jit(solution)/shard_map/ppermute | solution.py:260
  38.4 2.7 %collective-permute-done.1 = f32[20,8,128]{2,1,0:T(8,128)S(1)} collective-permute-done((f32[20,8,128]{2,1,0:T(8,128)S(1)}, f32[20,8,128]{2,1,0:T(8,128)S(1)}, u32[]{:S(2)}, u32[]{:S(2)}) %collective-permute-start.1) | collective-permute-done | bytes 81952 | tf_op jit(solution)/shard_map/ppermute | solution.py:260
  41.1 21.3 %all-gather = f32[208,8,128]{2,1,0:T(8,128)S(1)} all-gather(f32[26,8,128]{2,1,0:T(8,128)S(1)} %pad_maximum_fusion), channel_id=2, replica_groups=mesh['z'=8,'x'=4,'y'=8,'c'=2] {'y'}, dimensions={0}, use_global_device_ids=true | all-gather | bytes 958464 | tf_op jit(solution)/shard_map/all_gather | solution.py:337
  62.4 9.5 %collective-permute-start.2 = (f32[8,26,8,128]{3,2,1,0:T(8,128)S(1)}, f32[8,26,8,128]{3,2,1,0:T(8,128)S(1)}, u32[]{:S(2)}, u32[]{:S(2)}) collective-permute-start(f32[8,26,8,128]{3,2,1,0:T(8,128)S(1)} %bitcast.2), channel_id=1, source_target_pairs={{0,1},{1,0},{2,3},{3,2},{4,5},{5,4},{6,7},{7,6},{8,9},{9,8},{10,11... | collective-permute-start | bytes 2555912 | tf_op jit(solution)/shard_map/ppermute | solution.py:260
  72.0 2.0 %collective-permute-done.2.refs_2_ = f32[8,26,8,128]{3,2,1,0:T(8,128)S(1)} collective-permute-done((f32[8,26,8,128]{3,2,1,0:T(8,128)S(1)}, f32[8,26,8,128]{3,2,1,0:T(8,128)S(1)}, u32[]{:S(2)}, u32[]{:S(2)}) %collective-permute-start.2) | collective-permute-done | bytes 852000 | tf_op jit(solution)/shard_map/ppermute | solution.py:260
  74.0 2.6 %shard_map.29 = (f32[14,128,128]{2,1,0:T(8,128)S(1)}, f32[14,64,128]{2,1,0:T(8,128)S(1)}, f32[5,128,128]{2,1,0:T(8,128)S(1)}) custom-call(s32[1]{0:T(128)} %bitcast.refs_0_, f32[8,26,8,128]{3,2,1,0:T(8,128)S(1)} %bitcast.3, f32[8,26,8,128]{3,2,1,0:T(8,128)S(1)} %collective-permute-done.2.refs_2_), custom_call_target="tpu_custom_call" | custom-call | tf_op jit(solution)/shard_map/pallas_call | solution.py:57
  76.6 2.1 %collective-permute-start.3 = (f32[14,64,128]{2,1,0:T(8,128)S(1)}, f32[14,64,128]{2,1,0:T(8,128)S(1)}, u32[]{:S(2)}, u32[]{:S(2)}) collective-permute-start(f32[14,64,128]{2,1,0:T(8,128)S(1)} %get-tuple-element.25), channel_id=1, source_target_pairs={{0,48},{16,32},{32,16},{48,0},{1,49},{17,33},{33,17},{49,1},{2,50}... | collective-permute-start | bytes 1376264 | tf_op jit(solution)/shard_map/ppermute | solution.py:260
  78.7 12.7 %collective-permute-done.3.refs_2_ = f32[14,64,128]{2,1,0:T(8,128)S(1)} collective-permute-done((f32[14,64,128]{2,1,0:T(8,128)S(1)}, f32[14,64,128]{2,1,0:T(8,128)S(1)}, u32[]{:S(2)}, u32[]{:S(2)}) %collective-permute-start.3) | collective-permute-done | bytes 458784 | tf_op jit(solution)/shard_map/ppermute | solution.py:260
  91.4 3.1 %collective-permute-start.4 = (f32[14,64,128]{2,1,0:T(8,128)S(1)}, f32[14,64,128]{2,1,0:T(8,128)S(1)}, u32[]{:S(2)}, u32[]{:S(2)}) collective-permute-start(f32[14,64,128]{2,1,0:T(8,128)S(1)} %collective-permute-done.3.refs_2_), channel_id=1, source_target_pairs={{0,1},{1,0},{2,3},{3,2},{4,5},{5,4},{6,7},{7,6},{8,9},{9,8},{10,11... | collective-permute-start | bytes 1376264 | tf_op jit(solution)/shard_map/ppermute | solution.py:260
  94.5 1.4 collective-permute-done.4.refs_3_
  95.9 0.0 copy-start.1
  95.9 0.0 copy-start.3
  95.9 2.2 %shard_map.30 = (f32[9,128,128]{2,1,0:T(8,128)S(1)}, f32[9,64,128]{2,1,0:T(8,128)S(1)}, f32[4,128,128]{2,1,0:T(8,128)S(1)}) custom-call(s32[1]{0:T(128)} %bitcast.refs_0_, f32[14,128,128]{2,1,0:T(8,128)S(1)} %get-tuple-element.24.refs_1_, f32[14,64,128]{2,1,0:T(8,128)S(1)} %collective-permute-done.3.refs_2_, f32[14,64,128]{2,1,0:T(8,128)S(1)} %collective-permute-done.4.refs_3_), custom_call_target="tpu_custom_call" | custom-call | tf_op jit(solution)/shard_map/pallas_call | solution.py:57
  98.2 4.0 %collective-permute-start.5 = (f32[9,64,128]{2,1,0:T(8,128)S(1)}, f32[9,64,128]{2,1,0:T(8,128)S(1)}, u32[]{:S(2)}, u32[]{:S(2)}) collective-permute-start(f32[9,64,128]{2,1,0:T(8,128)S(1)} %get-tuple-element.27), channel_id=1, source_target_pairs={{0,64},{64,0},{128,192},{192,128},{256,320},{320,256},{384,448},{4... | collective-permute-start | bytes 884744 | tf_op jit(solution)/shard_map/ppermute | solution.py:260
  102.2 7.0 %collective-permute-done.5.refs_2_ = f32[9,64,128]{2,1,0:T(8,128)S(1)} collective-permute-done((f32[9,64,128]{2,1,0:T(8,128)S(1)}, f32[9,64,128]{2,1,0:T(8,128)S(1)}, u32[]{:S(2)}, u32[]{:S(2)}) %collective-permute-start.5) | collective-permute-done | bytes 294944 | tf_op jit(solution)/shard_map/ppermute | solution.py:260
  109.2 2.9 %collective-permute-start.6 = (f32[9,64,128]{2,1,0:T(8,128)S(1)}, f32[9,64,128]{2,1,0:T(8,128)S(1)}, u32[]{:S(2)}, u32[]{:S(2)}) collective-permute-start(f32[9,64,128]{2,1,0:T(8,128)S(1)} %collective-permute-done.5.refs_2_), channel_id=1, source_target_pairs={{0,1},{1,0},{2,3},{3,2},{4,5},{5,4},{6,7},{7,6},{8,9},{9,8},{10,11... | collective-permute-start | bytes 884744 | tf_op jit(solution)/shard_map/ppermute | solution.py:260
  112.0 0.3 shard_map.31.refs_4_.refs_2_
  112.3 0.9 collective-permute-done.6.refs_3_
  113.2 2.1 %shard_map.32 = (f32[5,128,128]{2,1,0:T(8,128)S(1)}, f32[5,64,128]{2,1,0:T(8,128)S(1)}, f32[3,128,128]{2,1,0:T(8,128)S(1)}) custom-call(s32[1]{0:T(128)} %bitcast.refs_0_, f32[9,128,128]{2,1,0:T(8,128)S(1)} %get-tuple-element.26.refs_1_, f32[9,64,128]{2,1,0:T(8,128)S(1)} %collective-permute-done.5.refs_2_, f32[9,64,128]{2,1,0:T(8,128)S(1)} %collective-permute-done.6.refs_3_, ...), custom_call_target="tpu_custom_call" | custom-call | tf_op jit(solution)/shard_map/pallas_call | solution.py:57
  115.3 1.9 %collective-permute-start.7 = (f32[5,64,128]{2,1,0:T(8,128)S(1)}, f32[5,64,128]{2,1,0:T(8,128)S(1)}, u32[]{:S(2)}, u32[]{:S(2)}) collective-permute-start(f32[5,64,128]{2,1,0:T(8,128)S(1)} %get-tuple-element.31), channel_id=1, source_target_pairs={{0,128},{64,192},{128,0},{192,64},{256,384},{320,448},{384,256},{4... | collective-permute-start | bytes 491528 | tf_op jit(solution)/shard_map/ppermute | solution.py:260
  117.2 7.0 %collective-permute-done.7.refs_2_ = f32[5,64,128]{2,1,0:T(8,128)S(1)} collective-permute-done((f32[5,64,128]{2,1,0:T(8,128)S(1)}, f32[5,64,128]{2,1,0:T(8,128)S(1)}, u32[]{:S(2)}, u32[]{:S(2)}) %collective-permute-start.7) | collective-permute-done | bytes 163872 | tf_op jit(solution)/shard_map/ppermute | solution.py:260
  124.2 2.8 %collective-permute-start.8 = (f32[5,64,128]{2,1,0:T(8,128)S(1)}, f32[5,64,128]{2,1,0:T(8,128)S(1)}, u32[]{:S(2)}, u32[]{:S(2)}) collective-permute-start(f32[5,64,128]{2,1,0:T(8,128)S(1)} %collective-permute-done.7.refs_2_), channel_id=1, source_target_pairs={{0,1},{1,0},{2,3},{3,2},{4,5},{5,4},{6,7},{7,6},{8,9},{9,8},{10,11... | collective-permute-start | bytes 491528 | tf_op jit(solution)/shard_map/ppermute | solution.py:260
  127.0 0.3 shard_map.33
  127.3 0.7 collective-permute-done.8.refs_3_
  128.0 1.8 %shard_map.34 = (f32[2,128,128]{2,1,0:T(8,128)S(1)}, f32[2,128,128]{2,1,0:T(8,128)S(1)}) custom-call(s32[1]{0:T(128)} %bitcast.refs_0_, f32[5,128,128]{2,1,0:T(8,128)S(1)} %get-tuple-element.30.refs_1_, f32[5,64,128]{2,1,0:T(8,128)S(1)} %collective-permute-done.7.refs_2_, f32[5,64,128]{2,1,0:T(8,128)S(1)} %collective-permute-done.8.refs_3_, ...), custom_call_target="tpu_custom_call" | custom-call | tf_op jit(solution)/shard_map/pallas_call | solution.py:57
  129.9 9.5 %collective-permute-start.9 = (f32[2,128,128]{2,1,0:T(8,128)S(1)}, f32[2,128,128]{2,1,0:T(8,128)S(1)}, u32[]{:S(2)}, u32[]{:S(2)}) collective-permute-start(f32[2,128,128]{2,1,0:T(8,128)S(1)} %get-tuple-element.35.refs_1_), channel_id=1, source_target_pairs={{0,384},{64,448},{128,256},{192,320},{256,128},{320,192},{384,0},{... | collective-permute-start | bytes 393224 | tf_op jit(solution)/shard_map/ppermute | solution.py:260
  139.3 0.0 copy-done.1
  139.3 0.0 copy-done.3
  139.4 1.3 shard_map.35
  140.7 5.4 %collective-permute-done.9.refs_2_ = f32[2,128,128]{2,1,0:T(8,128)S(1)} collective-permute-done((f32[2,128,128]{2,1,0:T(8,128)S(1)}, f32[2,128,128]{2,1,0:T(8,128)S(1)}, u32[]{:S(2)}, u32[]{:S(2)}) %collective-permute-start.9) | collective-permute-done | bytes 131104 | tf_op jit(solution)/shard_map/ppermute | solution.py:260
  146.1 2.4 %shard_map.36 = f32[1024,128]{1,0:T(8,128)} custom-call(s32[1]{0:T(128)} %bitcast.refs_0_, f32[2,128,128]{2,1,0:T(8,128)S(1)} %get-tuple-element.35.refs_1_, f32[2,128,128]{2,1,0:T(8,128)S(1)} %collective-permute-done.9.refs_2_, f32[1024,128]{1,0:T(8,128)S(1)} %get-tuple-element.37.refs_3_, f32[1024,128]{1,0:T(8,128)S(1)} %get-tuple-element.38.refs_4_), custom_call_target="tpu_custom_call" | custom-call | tf_op jit(solution)/shard_map/pallas_call | solution.py:57
  (5 shorter events, 0.1 us)
Async XLA Ops:
  0.0 1.7 %copy-start = (f32[5,1024,128]{2,1,0:T(8,128)S(1)}, f32[5,1024,128]{2,1,0:T(8,128)}, u32[]{:S(2)}) copy-start(f32[5,1024,128]{2,1,0:T(8,128)} %refs_2_.3) | copy-start | bytes 7864324
  1.7 1.0 copy-start.2
  5.3 4.3 %collective-permute-start = (f32[8,20,8,128]{3,2,1,0:T(8,128)S(1)}, f32[8,20,8,128]{3,2,1,0:T(8,128)S(1)}, u32[]{:S(2)}, u32[]{:S(2)}) collective-permute-start(f32[8,20,8,128]{3,2,1,0:T(8,128)S(1)} %get-tuple-element.23), channel_id=1, source_target_pairs={{0,1},{1,0},{2,3},{3,2},{4,5},{5,4},{6,7},{7,6},{8,9},{9,8},{10,11... | collective-permute-start | bytes 1966088 | tf_op jit(solution)/shard_map/ppermute | solution.py:260
  35.9 5.2 %collective-permute-start.1 = (f32[20,8,128]{2,1,0:T(8,128)S(1)}, f32[20,8,128]{2,1,0:T(8,128)S(1)}, u32[]{:S(2)}, u32[]{:S(2)}) collective-permute-start(f32[20,8,128]{2,1,0:T(8,128)S(1)} %reduce_sum.9), channel_id=1, source_target_pairs={{0,16},{16,0},{32,48},{48,32},{1,17},{17,1},{33,49},{49,33},{2,18}... | collective-permute-start | bytes 245768 | tf_op jit(solution)/shard_map/ppermute | solution.py:260
  62.4 11.5 %collective-permute-start.2 = (f32[8,26,8,128]{3,2,1,0:T(8,128)S(1)}, f32[8,26,8,128]{3,2,1,0:T(8,128)S(1)}, u32[]{:S(2)}, u32[]{:S(2)}) collective-permute-start(f32[8,26,8,128]{3,2,1,0:T(8,128)S(1)} %bitcast.2), channel_id=1, source_target_pairs={{0,1},{1,0},{2,3},{3,2},{4,5},{5,4},{6,7},{7,6},{8,9},{9,8},{10,11... | collective-permute-start | bytes 2555912 | tf_op jit(solution)/shard_map/ppermute | solution.py:260
  76.6 14.8 %collective-permute-start.3 = (f32[14,64,128]{2,1,0:T(8,128)S(1)}, f32[14,64,128]{2,1,0:T(8,128)S(1)}, u32[]{:S(2)}, u32[]{:S(2)}) collective-permute-start(f32[14,64,128]{2,1,0:T(8,128)S(1)} %get-tuple-element.25), channel_id=1, source_target_pairs={{0,48},{16,32},{32,16},{48,0},{1,49},{17,33},{33,17},{49,1},{2,50}... | collective-permute-start | bytes 1376264 | tf_op jit(solution)/shard_map/ppermute | solution.py:260
  91.4 4.6 %collective-permute-start.4 = (f32[14,64,128]{2,1,0:T(8,128)S(1)}, f32[14,64,128]{2,1,0:T(8,128)S(1)}, u32[]{:S(2)}, u32[]{:S(2)}) collective-permute-start(f32[14,64,128]{2,1,0:T(8,128)S(1)} %collective-permute-done.3.refs_2_), channel_id=1, source_target_pairs={{0,1},{1,0},{2,3},{3,2},{4,5},{5,4},{6,7},{7,6},{8,9},{9,8},{10,11... | collective-permute-start | bytes 1376264 | tf_op jit(solution)/shard_map/ppermute | solution.py:260
  95.9 43.4 %copy-start.1 = (f32[5,1024,128]{2,1,0:T(8,128)S(1)}, f32[5,1024,128]{2,1,0:T(8,128)}, u32[]{:S(2)}) copy-start(f32[5,1024,128]{2,1,0:T(8,128)} %refs_2_.3) | copy-start | bytes 7864324
  95.9 43.4 %copy-start.3 = (f32[1024,128]{1,0:T(8,128)S(1)}, f32[1024,128]{1,0:T(8,128)}, u32[]{:S(2)}) copy-start(f32[1024,128]{1,0:T(8,128)} %refs_3_.1) | copy-start | bytes 1572868
  98.2 11.0 %collective-permute-start.5 = (f32[9,64,128]{2,1,0:T(8,128)S(1)}, f32[9,64,128]{2,1,0:T(8,128)S(1)}, u32[]{:S(2)}, u32[]{:S(2)}) collective-permute-start(f32[9,64,128]{2,1,0:T(8,128)S(1)} %get-tuple-element.27), channel_id=1, source_target_pairs={{0,64},{64,0},{128,192},{192,128},{256,320},{320,256},{384,448},{4... | collective-permute-start | bytes 884744 | tf_op jit(solution)/shard_map/ppermute | solution.py:260
  109.2 4.0 %collective-permute-start.6 = (f32[9,64,128]{2,1,0:T(8,128)S(1)}, f32[9,64,128]{2,1,0:T(8,128)S(1)}, u32[]{:S(2)}, u32[]{:S(2)}) collective-permute-start(f32[9,64,128]{2,1,0:T(8,128)S(1)} %collective-permute-done.5.refs_2_), channel_id=1, source_target_pairs={{0,1},{1,0},{2,3},{3,2},{4,5},{5,4},{6,7},{7,6},{8,9},{9,8},{10,11... | collective-permute-start | bytes 884744 | tf_op jit(solution)/shard_map/ppermute | solution.py:260
  115.3 8.9 %collective-permute-start.7 = (f32[5,64,128]{2,1,0:T(8,128)S(1)}, f32[5,64,128]{2,1,0:T(8,128)S(1)}, u32[]{:S(2)}, u32[]{:S(2)}) collective-permute-start(f32[5,64,128]{2,1,0:T(8,128)S(1)} %get-tuple-element.31), channel_id=1, source_target_pairs={{0,128},{64,192},{128,0},{192,64},{256,384},{320,448},{384,256},{4... | collective-permute-start | bytes 491528 | tf_op jit(solution)/shard_map/ppermute | solution.py:260
  124.2 3.9 %collective-permute-start.8 = (f32[5,64,128]{2,1,0:T(8,128)S(1)}, f32[5,64,128]{2,1,0:T(8,128)S(1)}, u32[]{:S(2)}, u32[]{:S(2)}) collective-permute-start(f32[5,64,128]{2,1,0:T(8,128)S(1)} %collective-permute-done.7.refs_2_), channel_id=1, source_target_pairs={{0,1},{1,0},{2,3},{3,2},{4,5},{5,4},{6,7},{7,6},{8,9},{9,8},{10,11... | collective-permute-start | bytes 491528 | tf_op jit(solution)/shard_map/ppermute | solution.py:260
  129.9 16.3 %collective-permute-start.9 = (f32[2,128,128]{2,1,0:T(8,128)S(1)}, f32[2,128,128]{2,1,0:T(8,128)S(1)}, u32[]{:S(2)}, u32[]{:S(2)}) collective-permute-start(f32[2,128,128]{2,1,0:T(8,128)S(1)} %get-tuple-element.35.refs_1_), channel_id=1, source_target_pairs={{0,384},{64,448},{128,256},{192,320},{256,128},{320,192},{384,0},{... | collective-permute-start | bytes 393224 | tf_op jit(solution)/shard_map/ppermute | solution.py:260

commit v4 on v3

--- a/solution.py
+++ b/solution.py
@@ -16,13 +16,55 @@
 VMEM_SPEC = pl.BlockSpec(memory_space=pltpu.VMEM)
 SMEM_SPEC = pl.BlockSpec(memory_space=pltpu.SMEM)
 
-TOTAL = sum(level_no + 2 for level_no in range(LEVELS))
 CHIPS = 8
 TILE = HALF // CHIPS
+TOTAL = 18
 
 
 def rows_up_to(level_no):
     return sum(below + 2 for below in range(level_no + 1))
+
+
+def row_order(level_no):
+    return [level_no] + list(range(level_no)) + [LEVELS]
+
+
+def packed_order(level_no):
+    tops = [level_no] if level_no % 2 else [level_no - 1]
+    pairs = [("pair", top, top - 1) for top in range(tops[0], 0, -2)]
+    diagonals = pairs if level_no % 2 else [("one", level_no)] + pairs
+    others = [
+        [(row_no, m_no) for m_no in row_order(row_no)[1:]]
+        for row_no in reversed(range(level_no + 1))
+    ]
+    return diagonals[:1] + others[0] + diagonals[1:] + sum(others[1:], [])
+
+
+def full_index(level_no, row_no, m_no):
+    above = sum(row + 2 for row in range(row_no + 1, level_no + 1))
+    return above + row_order(row_no).index(m_no)
+
+
+def grid_of(rows, first=0):
+    row_no = lax.broadcasted_iota(jnp.int32, (rows, K), 0) + first
+    return row_no, lax.broadcasted_iota(jnp.int32, (rows, K), 1)
+
+
+def diagonal_of(matrix):
+    row_no, column_no = grid_of(K)
+    return jnp.sum(jnp.where(row_no == column_no, matrix, 0.0), 0, keepdims=True)
+
+
+def from_lower(packed):
+    row_no, column_no = grid_of(K)
+    strict = jnp.where(column_no < row_no, packed, 0.0)
+    return jnp.where(column_no <= row_no, packed, 0.0) + strict.T
+
+
+def from_upper(packed, diagonal):
+    row_no, column_no = grid_of(K)
+    strict = jnp.where(column_no > row_no, packed, 0.0)
+    return strict + strict.T + jnp.where(column_no == row_no, diagonal, 0.0)
 
 
 def two_parts(value):
@@ -67,11 +109,29 @@
     return list(outs)
 
 
-def row_order(level_no):
-    return [level_no] + list(range(level_no)) + [LEVELS]
-
-
 GROUPS = (((4, 3), (4, 3, 2, 1, 0, 5)), ((2, 1), (2, 1, 0, 5)), ((0,), (0, 5)))
+
+
+def hidden_diagonals(made):
+    row_no, column_no = grid_of(K)
+    out = jnp.zeros((K, K), jnp.float32)
+    for pair_no, level_no in enumerate((2, 0)):
+        diagonal = jnp.broadcast_to(diagonal_of(made[level_no, level_no]), (K, K))
+        left = pltpu.roll(diagonal, HALF, 1)
+        out = jnp.where(row_no == 2 * pair_no, left, out)
+        out = jnp.where(row_no == 2 * pair_no + 1, diagonal, out)
+    return jnp.where(column_no >= HALF, out, 0.0)
+
+
+def found_diagonals(packed):
+    _, column_no = grid_of(8)
+    found = []
+    for pair_no in range(2):
+        left = jnp.broadcast_to(packed[2 * pair_no : 2 * pair_no + 1], (8, K))
+        right = jnp.broadcast_to(packed[2 * pair_no + 1 : 2 * pair_no + 2], (8, K))
+        both = jnp.where(column_no < HALF, pltpu.roll(left, HALF, 1), right)
+        found.append(both[:1])
+    return found
 
 
 def gram_body(core_ref, bases_ref, targets_ref, keep_ref, send_ref):
@@ -82,22 +142,26 @@
     def wide(fields):
         return [jnp.concatenate([parts[m_no][i] for m_no in fields], 1) for i in range(2)]
 
-    starts = {}
-    at = 0
-    for level_no in reversed(range(LEVELS)):
-        starts[level_no] = at
-        at += level_no + 2
+    made = {}
     for lefts, rights in GROUPS:
         block = dot_parts(wide(lefts), wide(rights), ((0,), (0,)))
         for top, level_no in enumerate(lefts):
-            for m_no, field in enumerate(row_order(level_no)):
+            for field in row_order(level_no):
                 to = rights.index(field)
-                value = block[top * K : (top + 1) * K, to * K : (to + 1) * K]
-                low = value[:HALF].reshape(CHIPS, TILE, K)
-                high = value[HALF:].reshape(CHIPS, TILE, K)
-                at = starts[level_no] + m_no
-                keep_ref[:, at] = jnp.where(first, low, high)
-                send_ref[:, at] = jnp.where(first, high, low)
+                made[level_no, field] = block[top * K : (top + 1) * K, to * K : (to + 1) * K]
+    row_no, column_no = grid_of(K)
+    lower = column_no <= row_no
+    for at, entry in enumerate(packed_order(LEVELS - 1)):
+        if entry[0] == "one":
+            value = jnp.where(lower, made[entry[1], entry[1]], hidden_diagonals(made))
+        elif entry[0] == "pair":
+            value = jnp.where(lower, made[entry[1], entry[1]], made[entry[2], entry[2]])
+        else:
+            value = made[entry]
+        low = value[:HALF].reshape(CHIPS, TILE, K)
+        high = value[HALF:].reshape(CHIPS, TILE, K)
+        keep_ref[:, at] = jnp.where(first, low, high)
+        send_ref[:, at] = jnp.where(first, high, low)
 
 
 def local_grams(core, bases, targets):
@@ -166,32 +230,86 @@
         order = [row_no] + list(range(row_no)) + [level_no]
         picked = [right[:, m_no * K : (m_no + 1) * K] for m_no in order]
         row = mtm(left[:, row_no * K : (row_no + 1) * K], jnp.concatenate(picked, 1))
-        for m_no in range(row_no + 2):
-            next_ref[at] = both(at) - row[:, m_no * K : (m_no + 1) * K]
+        for m_no, field in enumerate(row_order(row_no)):
+            next_ref[at] = both(row_no, field) - row[:, m_no * K : (m_no + 1) * K]
             at += 1
     if send_ref is not None:
+        below = level_no - 1
         first = pl.multiple_of(core_no * HALF, HALF)
-        for at in range(rows_up_to(level_no - 1)):
-            send_ref[at] = next_ref[at, pl.ds(first, HALF)]
-
-
-def finest_body(core_ref, half_ref, far_ref, next_ref, send_ref, coef_ref, work_ref, all_ref):
+        row_no, column_no = grid_of(HALF, first)
+        extra = jnp.zeros((8, K), jnp.float32)
+        extra_row, _ = grid_of(8)
+        extras = 0
+
+        def some(row, m_no):
+            return next_ref[full_index(below, row, m_no), pl.ds(first, HALF)]
+
+        entries = packed_order(below)
+        for at, entry in enumerate(entries):
+            if entry[0] == "one":
+                value = some(entry[1], entry[1])
+            elif entry[0] == "pair":
+                value = jnp.where(
+                    column_no <= row_no,
+                    some(entry[1], entry[1]),
+                    some(entry[2], entry[2]),
+                )
+                lost = next_ref[full_index(below, entry[2], entry[2])]
+                extra = jnp.where(extra_row == extras, diagonal_of(lost), extra)
+                extras += 1
+            else:
+                value = some(*entry)
+            send_ref[at * HALF : (at + 1) * HALF] = value
+        send_ref[len(entries) * HALF :] = extra
+
+
+def unpack(level_no, order, packed_ref, base, diagonals):
+    found = {}
+    pairs = 0
+    for at, entry in enumerate(order):
+        value = packed_ref[base + at]
+        if entry[0] == "one":
+            found[entry[1], entry[1]] = value
+        elif entry[0] == "pair":
+            found[entry[1], entry[1]] = from_lower(value)
+            found[entry[2], entry[2]] = from_upper(value, diagonals[pairs])
+            pairs += 1
+        else:
+            found[entry] = value
+    return found
+
+
+def join_halves(core_no, count, half_ref, far_ref, packed_ref, half_of):
+    own = pl.ds(pl.multiple_of(core_no * HALF, HALF), HALF)
+    far = pl.ds(pl.multiple_of((1 - core_no) * HALF, HALF), HALF)
+    for at in range(count):
+        packed_ref[at, own] = half_of(half_ref, at)
+        packed_ref[at, far] = half_of(far_ref, at)
+
+
+def finest_body(
+    core_ref, half_ref, far_ref, next_ref, send_ref, coef_ref, work_ref, packed_ref
+):
     level_no = LEVELS - 1
     core_no = core_ref[0]
     count = level_no + 2
-    for at in range(half_ref.shape[1]):
-        all_ref[at, pl.ds(pl.multiple_of(core_no * HALF, HALF), HALF)] = half_ref[
-            :, at
-        ].reshape(HALF, K)
-        all_ref[at, pl.ds(pl.multiple_of((1 - core_no) * HALF, HALF), HALF)] = far_ref[
-            :, at
-        ].reshape(HALF, K)
+    join_halves(
+        core_no,
+        half_ref.shape[1],
+        half_ref,
+        far_ref,
+        packed_ref,
+        lambda ref, at: ref[:, at].reshape(HALF, K),
+    )
+    diagonals = found_diagonals(packed_ref[0] + packed_ref[count])
+    order = packed_order(level_no)
+    both = unpack(level_no, order[count:], packed_ref, 2 * count, diagonals)
     eliminate(
         level_no,
         core_no,
-        lambda at: all_ref[at],
-        lambda at: all_ref[count + at],
-        lambda at: all_ref[2 * count + at],
+        lambda m_no: packed_ref[m_no] if m_no else from_lower(packed_ref[0]),
+        lambda m_no: packed_ref[count + m_no] if m_no else from_lower(packed_ref[count]),
+        lambda row_no, field: both[row_no, field],
         next_ref,
         send_ref,
         coef_ref,
@@ -200,18 +318,27 @@
 
 
 def middle_body(level_no, core_ref, own_ref, half_ref, far_ref, next_ref, *refs):
-    send_ref, coef_ref, work_ref, sib_ref = refs if len(refs) == 4 else (None,) + refs
+    send_ref, coef_ref, work_ref, packed_ref = refs if len(refs) == 4 else (None,) + refs
     core_no = core_ref[0]
-    for at in range(half_ref.shape[0]):
-        sib_ref[at, pl.ds(pl.multiple_of(core_no * HALF, HALF), HALF)] = half_ref[at]
-        sib_ref[at, pl.ds(pl.multiple_of((1 - core_no) * HALF, HALF), HALF)] = far_ref[at]
-    below = level_no + 2
+    order = packed_order(level_no)
+    join_halves(
+        core_no,
+        len(order),
+        half_ref,
+        far_ref,
+        packed_ref,
+        lambda ref, at: ref[at * HALF : (at + 1) * HALF],
+    )
+    tail = half_ref[len(order) * HALF :]
+    found = unpack(level_no, order, packed_ref, 0, (tail[0:1], tail[1:2]))
+    fields = row_order(level_no)
     eliminate(
         level_no,
         core_no,
-        lambda at: own_ref[at],
-        lambda at: sib_ref[at],
-        lambda at: own_ref[below + at] + sib_ref[below + at],
+        lambda m_no: own_ref[m_no],
+        lambda m_no: found[level_no, fields[m_no]],
+        lambda row_no, field: own_ref[full_index(level_no, row_no, field)]
+        + found[row_no, field],
         next_ref,
         send_ref,
         coef_ref,
@@ -274,6 +401,10 @@
 WORK = (2, K, K)
 
 
+def sent_shape(level_no):
+    return (len(packed_order(level_no)) * HALF + 8, K)
+
+
 def per_device(bases, targets):
     top = LEVELS - 1
     head = top + 2
@@ -288,7 +419,7 @@
     below = rows_up_to(top - 1)
     own, send, coef = call(
         finest_body,
-        [(below, K, K), (below, HALF, K), (top + 1, K, K)],
+        [(below, K, K), sent_shape(top - 1), (top + 1, K, K)],
         core,
         half,
         far,
@@ -300,7 +431,7 @@
         half = swap(send, *PARTNERS[level_no])
         far = swap_cores(half)
         below = rows_up_to(level_no - 1)
-        shapes = [(below, K, K), (below, HALF, K), (level_no + 1, K, K)]
+        shapes = [(below, K, K), sent_shape(level_no - 1), (level_no + 1, K, K)]
         if level_no == 1:
             del shapes[1]
         outs = call(
@@ -310,7 +441,7 @@
             own,
             half,
             far,
-            scratch=[WORK, own.shape],
+            scratch=[WORK, (len(packed_order(level_no)), K, K)],
             after=folded,
         )
         own, send, coef = outs[0], outs[-2], outs[-1]

time: 149 us -> 144 us (0.966)
  waiting for transfers between devices: 41.5 us -> 37.9 us
    ppermute x10, waiting for transfers between devices: 41.5 us -> 37.9 us  [swap(): return lax.ppermute(value, axis, pairs)]
where the time goes in v4:
time: 144 us
  blocking collectives  46.3 us (32%)
  starting transfers between devices  40.6 us (28%)
  waiting for transfers between devices  37.9 us (26%)
  Pallas kernels  15.8 us (11%)
  local copies, waits for them, and re-layouts  2.79 us (2%)
    ppermute x10, starting transfers between devices, swap(): return lax.ppermute(value, axis, pairs)  40.6 us
    ppermute x10, waiting for transfers between devices, swap(): return lax.ppermute(value, axis, pairs)  37.9 us
    all_to_all x1, blocking collectives, per_device(): part = lax.all_to_all(part, 'y', 0, 0).sum(0)  25 us
    all_gather x1, blocking collectives, gather_chips(): return lax.all_gather(piece, 'y')  21.3 us
    pallas_call x9, Pallas kernels, call(): pl.pallas_call(whole_body, out_shape=[jax.ShapeDtypeStruct(shape, jnp.flo...  15.8 us
  transfers between devices with their start and end apart: 10, of which 10 were waited for; matrix products, arithmetic and copies ran while one was open for 0% of the time, Pallas kernels for 1%

profile of v4, /device:TPU:135, one launch (start us, length us, event | category | flops | bytes accessed | tf_op | source)
XLA Modules:
  0.0 143.6 jit_solution(9232509835871031528)
XLA Ops:
  0.0 0.0 copy-start
  0.0 1.7 %copy-done = f32[5,1024,128]{2,1,0:T(8,128)S(1)} copy-done((f32[5,1024,128]{2,1,0:T(8,128)S(1)}, f32[5,1024,128]{2,1,0:T(8,128)}, u32[]{:S(2)}) %copy-start) | copy-done | bytes 2621464
  1.7 0.0 copy-start.2
  1.7 1.0 copy-done.2
  2.8 2.6 %shard_map.28 = (f32[8,18,8,128]{3,2,1,0:T(8,128)S(1)}, f32[8,18,8,128]{3,2,1,0:T(8,128)S(1)}) custom-call(s32[1]{0:T(128)} %bitcast.refs_0_, f32[5,1024,128]{2,1,0:T(8,128)S(1)} %copy-done, f32[1024,128]{1,0:T(8,128)S(1)} %copy-done.2), custom_call_target="tpu_custom_call" | custom-call | tf_op jit(solution)/shard_map/pallas_call | solution.py:99
  5.3 2.6 %collective-permute-start = (f32[8,18,8,128]{3,2,1,0:T(8,128)S(1)}, f32[8,18,8,128]{3,2,1,0:T(8,128)S(1)}, u32[]{:S(2)}, u32[]{:S(2)}) collective-permute-start(f32[8,18,8,128]{3,2,1,0:T(8,128)S(1)} %get-tuple-element.23), channel_id=1, source_target_pairs={{0,1},{1,0},{2,3},{3,2},{4,5},{5,4},{6,7},{7,6},{8,9},{9,8},{10,11... | collective-permute-start | bytes 1769480 | tf_op jit(solution)/shard_map/ppermute | solution.py:387
  7.9 1.6 %collective-permute-done = f32[8,18,8,128]{3,2,1,0:T(8,128)S(1)} collective-permute-done((f32[8,18,8,128]{3,2,1,0:T(8,128)S(1)}, f32[8,18,8,128]{3,2,1,0:T(8,128)S(1)}, u32[]{:S(2)}, u32[]{:S(2)}) %collective-permute-start) | collective-permute-done | bytes 589856 | tf_op jit(solution)/shard_map/ppermute | solution.py:387
  9.5 0.1 add.6
  9.6 25.0 %all_to_all.5 = f32[8,18,8,128]{3,2,1,0:T(8,128)S(1)} all-to-all(f32[8,18,8,128]{3,2,1,0:T(8,128)S(1)} %add.6), channel_id=1, replica_groups=mesh['z'=8,'x'=4,'y'=8,'c'=2] {'y'}, dimensions={0} | all-to-all | bytes 1179648 | tf_op jit(solution)/shard_map/all_to_all | solution.py:414
  34.7 2.5 %collective-permute-start.1 = (f32[18,8,128]{2,1,0:T(8,128)S(1)}, f32[18,8,128]{2,1,0:T(8,128)S(1)}, u32[]{:S(2)}, u32[]{:S(2)}) collective-permute-start(f32[18,8,128]{2,1,0:T(8,128)S(1)} %reduce_sum.9), channel_id=1, source_target_pairs={{0,16},{16,0},{32,48},{48,32},{1,17},{17,1},{33,49},{49,33},{2,18}... | collective-permute-start | bytes 221192 | tf_op jit(solution)/shard_map/ppermute | solution.py:387
  37.2 2.6 %collective-permute-done.1 = f32[18,8,128]{2,1,0:T(8,128)S(1)} collective-permute-done((f32[18,8,128]{2,1,0:T(8,128)S(1)}, f32[18,8,128]{2,1,0:T(8,128)S(1)}, u32[]{:S(2)}, u32[]{:S(2)}) %collective-permute-start.1) | collective-permute-done | bytes 73760 | tf_op jit(solution)/shard_map/ppermute | solution.py:387
  39.8 21.3 %all-gather = f32[192,8,128]{2,1,0:T(8,128)S(1)} all-gather(f32[24,8,128]{2,1,0:T(8,128)S(1)} %pad_maximum_fusion), channel_id=2, replica_groups=mesh['z'=8,'x'=4,'y'=8,'c'=2] {'y'}, dimensions={0}, use_global_device_ids=true | all-gather | bytes 884736 | tf_op jit(solution)/shard_map/all_gather | solution.py:468
  61.1 9.2 %collective-permute-start.2 = (f32[8,24,8,128]{3,2,1,0:T(8,128)S(1)}, f32[8,24,8,128]{3,2,1,0:T(8,128)S(1)}, u32[]{:S(2)}, u32[]{:S(2)}) collective-permute-start(f32[8,24,8,128]{3,2,1,0:T(8,128)S(1)} %bitcast.2), channel_id=1, source_target_pairs={{0,1},{1,0},{2,3},{3,2},{4,5},{5,4},{6,7},{7,6},{8,9},{9,8},{10,11... | collective-permute-start | bytes 2359304 | tf_op jit(solution)/shard_map/ppermute | solution.py:387
  70.3 1.9 %collective-permute-done.2.refs_2_ = f32[8,24,8,128]{3,2,1,0:T(8,128)S(1)} collective-permute-done((f32[8,24,8,128]{3,2,1,0:T(8,128)S(1)}, f32[8,24,8,128]{3,2,1,0:T(8,128)S(1)}, u32[]{:S(2)}, u32[]{:S(2)}) %collective-permute-start.2) | collective-permute-done | bytes 786464 | tf_op jit(solution)/shard_map/ppermute | solution.py:387
  72.2 2.7 %shard_map.29 = (f32[14,128,128]{2,1,0:T(8,128)S(1)}, f32[776,128]{1,0:T(8,128)S(1)}, f32[5,128,128]{2,1,0:T(8,128)S(1)}) custom-call(s32[1]{0:T(128)} %bitcast.refs_0_, f32[8,24,8,128]{3,2,1,0:T(8,128)S(1)} %bitcast.3, f32[8,24,8,128]{3,2,1,0:T(8,128)S(1)} %collective-permute-done.2.refs_2_), custom_call_target="tpu_custom_call" | custom-call | tf_op jit(solution)/shard_map/pallas_call | solution.py:99
  74.9 2.1 %collective-permute-start.3 = (f32[776,128]{1,0:T(8,128)S(1)}, f32[776,128]{1,0:T(8,128)S(1)}, u32[]{:S(2)}, u32[]{:S(2)}) collective-permute-start(f32[776,128]{1,0:T(8,128)S(1)} %get-tuple-element.25), channel_id=1, source_target_pairs={{0,48},{16,32},{32,16},{48,0},{1,49},{17,33},{33,17},{49,1},{2,50}... | collective-permute-start | bytes 1191944 | tf_op jit(solution)/shard_map/ppermute | solution.py:387
  77.0 11.4 %collective-permute-done.3.refs_2_ = f32[776,128]{1,0:T(8,128)S(1)} collective-permute-done((f32[776,128]{1,0:T(8,128)S(1)}, f32[776,128]{1,0:T(8,128)S(1)}, u32[]{:S(2)}, u32[]{:S(2)}) %collective-permute-start.3) | collective-permute-done | bytes 397344 | tf_op jit(solution)/shard_map/ppermute | solution.py:387
  88.4 3.1 %collective-permute-start.4 = (f32[776,128]{1,0:T(8,128)S(1)}, f32[776,128]{1,0:T(8,128)S(1)}, u32[]{:S(2)}, u32[]{:S(2)}) collective-permute-start(f32[776,128]{1,0:T(8,128)S(1)} %collective-permute-done.3.refs_2_), channel_id=1, source_target_pairs={{0,1},{1,0},{2,3},{3,2},{4,5},{5,4},{6,7},{7,6},{8,9},{9,8},{10,11... | collective-permute-start | bytes 1191944 | tf_op jit(solution)/shard_map/ppermute | solution.py:387
  91.5 1.3 collective-permute-done.4.refs_3_
  92.8 0.0 copy-start.1
  92.9 0.0 copy-start.3
  92.9 2.3 %shard_map.30 = (f32[9,128,128]{2,1,0:T(8,128)S(1)}, f32[520,128]{1,0:T(8,128)S(1)}, f32[4,128,128]{2,1,0:T(8,128)S(1)}) custom-call(s32[1]{0:T(128)} %bitcast.refs_0_, f32[14,128,128]{2,1,0:T(8,128)S(1)} %get-tuple-element.24.refs_1_, f32[776,128]{1,0:T(8,128)S(1)} %collective-permute-done.3.refs_2_, f32[776,128]{1,0:T(8,128)S(1)} %collective-permute-done.4.refs_3_), custom_call_target="tpu_custom_call" | custom-call | tf_op jit(solution)/shard_map/pallas_call | solution.py:99
  95.1 4.0 %collective-permute-start.5 = (f32[520,128]{1,0:T(8,128)S(1)}, f32[520,128]{1,0:T(8,128)S(1)}, u32[]{:S(2)}, u32[]{:S(2)}) collective-permute-start(f32[520,128]{1,0:T(8,128)S(1)} %get-tuple-element.27), channel_id=1, source_target_pairs={{0,64},{64,0},{128,192},{192,128},{256,320},{320,256},{384,448},{4... | collective-permute-start | bytes 798728 | tf_op jit(solution)/shard_map/ppermute | solution.py:387
  99.2 6.4 %collective-permute-done.5.refs_2_ = f32[520,128]{1,0:T(8,128)S(1)} collective-permute-done((f32[520,128]{1,0:T(8,128)S(1)}, f32[520,128]{1,0:T(8,128)S(1)}, u32[]{:S(2)}, u32[]{:S(2)}) %collective-permute-start.5) | collective-permute-done | bytes 266272 | tf_op jit(solution)/shard_map/ppermute | solution.py:387
  105.5 2.8 %collective-permute-start.6 = (f32[520,128]{1,0:T(8,128)S(1)}, f32[520,128]{1,0:T(8,128)S(1)}, u32[]{:S(2)}, u32[]{:S(2)}) collective-permute-start(f32[520,128]{1,0:T(8,128)S(1)} %collective-permute-done.5.refs_2_), channel_id=1, source_target_pairs={{0,1},{1,0},{2,3},{3,2},{4,5},{5,4},{6,7},{7,6},{8,9},{9,8},{10,11... | collective-permute-start | bytes 798728 | tf_op jit(solution)/shard_map/ppermute | solution.py:387
  108.4 0.3 shard_map.31.refs_4_.refs_2_
  108.7 0.9 collective-permute-done.6.refs_3_
  109.5 2.1 %shard_map.32 = (f32[5,128,128]{2,1,0:T(8,128)S(1)}, f32[264,128]{1,0:T(8,128)S(1)}, f32[3,128,128]{2,1,0:T(8,128)S(1)}) custom-call(s32[1]{0:T(128)} %bitcast.refs_0_, f32[9,128,128]{2,1,0:T(8,128)S(1)} %get-tuple-element.26.refs_1_, f32[520,128]{1,0:T(8,128)S(1)} %collective-permute-done.5.refs_2_, f32[520,128]{1,0:T(8,128)S(1)} %collective-permute-done.6.refs_3_, ...), custom_call_target="tpu_custom_call" | custom-call | tf_op jit(solution)/shard_map/pallas_call | solution.py:99
  111.6 1.9 %collective-permute-start.7 = (f32[264,128]{1,0:T(8,128)S(1)}, f32[264,128]{1,0:T(8,128)S(1)}, u32[]{:S(2)}, u32[]{:S(2)}) collective-permute-start(f32[264,128]{1,0:T(8,128)S(1)} %get-tuple-element.31), channel_id=1, source_target_pairs={{0,128},{64,192},{128,0},{192,64},{256,384},{320,448},{384,256},{4... | collective-permute-start | bytes 405512 | tf_op jit(solution)/shard_map/ppermute | solution.py:387
  113.6 5.7 %collective-permute-done.7.refs_2_ = f32[264,128]{1,0:T(8,128)S(1)} collective-permute-done((f32[264,128]{1,0:T(8,128)S(1)}, f32[264,128]{1,0:T(8,128)S(1)}, u32[]{:S(2)}, u32[]{:S(2)}) %collective-permute-start.7) | collective-permute-done | bytes 135200 | tf_op jit(solution)/shard_map/ppermute | solution.py:387
  119.3 3.1 %collective-permute-start.8 = (f32[264,128]{1,0:T(8,128)S(1)}, f32[264,128]{1,0:T(8,128)S(1)}, u32[]{:S(2)}, u32[]{:S(2)}) collective-permute-start(f32[264,128]{1,0:T(8,128)S(1)} %collective-permute-done.7.refs_2_), channel_id=1, source_target_pairs={{0,1},{1,0},{2,3},{3,2},{4,5},{5,4},{6,7},{7,6},{8,9},{9,8},{10,11... | collective-permute-start | bytes 405512 | tf_op jit(solution)/shard_map/ppermute | solution.py:387
  122.4 0.3 shard_map.33
  122.7 0.6 collective-permute-done.8.refs_3_
  123.4 1.9 %shard_map.34 = (f32[2,128,128]{2,1,0:T(8,128)S(1)}, f32[2,128,128]{2,1,0:T(8,128)S(1)}) custom-call(s32[1]{0:T(128)} %bitcast.refs_0_, f32[5,128,128]{2,1,0:T(8,128)S(1)} %get-tuple-element.30.refs_1_, f32[264,128]{1,0:T(8,128)S(1)} %collective-permute-done.7.refs_2_, f32[264,128]{1,0:T(8,128)S(1)} %collective-permute-done.8.refs_3_, ...), custom_call_target="tpu_custom_call" | custom-call | tf_op jit(solution)/shard_map/pallas_call | solution.py:99
  125.3 9.2 %collective-permute-start.9 = (f32[2,128,128]{2,1,0:T(8,128)S(1)}, f32[2,128,128]{2,1,0:T(8,128)S(1)}, u32[]{:S(2)}, u32[]{:S(2)}) collective-permute-start(f32[2,128,128]{2,1,0:T(8,128)S(1)} %get-tuple-element.35.refs_1_), channel_id=1, source_target_pairs={{0,384},{64,448},{128,256},{192,320},{256,128},{320,192},{384,0},{... | collective-permute-start | bytes 393224 | tf_op jit(solution)/shard_map/ppermute | solution.py:387
  134.5 0.0 copy-done.1
  134.5 0.0 copy-done.3
  134.5 1.3 shard_map.35
  135.8 5.4 %collective-permute-done.9.refs_2_ = f32[2,128,128]{2,1,0:T(8,128)S(1)} collective-permute-done((f32[2,128,128]{2,1,0:T(8,128)S(1)}, f32[2,128,128]{2,1,0:T(8,128)S(1)}, u32[]{:S(2)}, u32[]{:S(2)}) %collective-permute-start.9) | collective-permute-done | bytes 131104 | tf_op jit(solution)/shard_map/ppermute | solution.py:387
  141.2 2.4 %shard_map.36 = f32[1024,128]{1,0:T(8,128)} custom-call(s32[1]{0:T(128)} %bitcast.refs_0_, f32[2,128,128]{2,1,0:T(8,128)S(1)} %get-tuple-element.35.refs_1_, f32[2,128,128]{2,1,0:T(8,128)S(1)} %collective-permute-done.9.refs_2_, f32[1024,128]{1,0:T(8,128)S(1)} %get-tuple-element.37.refs_3_, f32[1024,128]{1,0:T(8,128)S(1)} %get-tuple-element.38.refs_4_), custom_call_target="tpu_custom_call" | custom-call | tf_op jit(solution)/shard_map/pallas_call | solution.py:99
  (5 shorter events, 0.1 us)
Async XLA Ops:
  0.0 1.7 %copy-start = (f32[5,1024,128]{2,1,0:T(8,128)S(1)}, f32[5,1024,128]{2,1,0:T(8,128)}, u32[]{:S(2)}) copy-start(f32[5,1024,128]{2,1,0:T(8,128)} %refs_2_.3) | copy-start | bytes 7864324
  1.7 1.0 copy-start.2
  5.3 4.2 %collective-permute-start = (f32[8,18,8,128]{3,2,1,0:T(8,128)S(1)}, f32[8,18,8,128]{3,2,1,0:T(8,128)S(1)}, u32[]{:S(2)}, u32[]{:S(2)}) collective-permute-start(f32[8,18,8,128]{3,2,1,0:T(8,128)S(1)} %get-tuple-element.23), channel_id=1, source_target_pairs={{0,1},{1,0},{2,3},{3,2},{4,5},{5,4},{6,7},{7,6},{8,9},{9,8},{10,11... | collective-permute-start | bytes 1769480 | tf_op jit(solution)/shard_map/ppermute | solution.py:387
  34.7 5.1 %collective-permute-start.1 = (f32[18,8,128]{2,1,0:T(8,128)S(1)}, f32[18,8,128]{2,1,0:T(8,128)S(1)}, u32[]{:S(2)}, u32[]{:S(2)}) collective-permute-start(f32[18,8,128]{2,1,0:T(8,128)S(1)} %reduce_sum.9), channel_id=1, source_target_pairs={{0,16},{16,0},{32,48},{48,32},{1,17},{17,1},{33,49},{49,33},{2,18}... | collective-permute-start | bytes 221192 | tf_op jit(solution)/shard_map/ppermute | solution.py:387
  61.1 11.1 %collective-permute-start.2 = (f32[8,24,8,128]{3,2,1,0:T(8,128)S(1)}, f32[8,24,8,128]{3,2,1,0:T(8,128)S(1)}, u32[]{:S(2)}, u32[]{:S(2)}) collective-permute-start(f32[8,24,8,128]{3,2,1,0:T(8,128)S(1)} %bitcast.2), channel_id=1, source_target_pairs={{0,1},{1,0},{2,3},{3,2},{4,5},{5,4},{6,7},{7,6},{8,9},{9,8},{10,11... | collective-permute-start | bytes 2359304 | tf_op jit(solution)/shard_map/ppermute | solution.py:387
  74.9 13.5 %collective-permute-start.3 = (f32[776,128]{1,0:T(8,128)S(1)}, f32[776,128]{1,0:T(8,128)S(1)}, u32[]{:S(2)}, u32[]{:S(2)}) collective-permute-start(f32[776,128]{1,0:T(8,128)S(1)} %get-tuple-element.25), channel_id=1, source_target_pairs={{0,48},{16,32},{32,16},{48,0},{1,49},{17,33},{33,17},{49,1},{2,50}... | collective-permute-start | bytes 1191944 | tf_op jit(solution)/shard_map/ppermute | solution.py:387
  88.4 4.5 %collective-permute-start.4 = (f32[776,128]{1,0:T(8,128)S(1)}, f32[776,128]{1,0:T(8,128)S(1)}, u32[]{:S(2)}, u32[]{:S(2)}) collective-permute-start(f32[776,128]{1,0:T(8,128)S(1)} %collective-permute-done.3.refs_2_), channel_id=1, source_target_pairs={{0,1},{1,0},{2,3},{3,2},{4,5},{5,4},{6,7},{7,6},{8,9},{9,8},{10,11... | collective-permute-start | bytes 1191944 | tf_op jit(solution)/shard_map/ppermute | solution.py:387
  92.8 41.6 %copy-start.1 = (f32[5,1024,128]{2,1,0:T(8,128)S(1)}, f32[5,1024,128]{2,1,0:T(8,128)}, u32[]{:S(2)}) copy-start(f32[5,1024,128]{2,1,0:T(8,128)} %refs_2_.3) | copy-start | bytes 7864324
  92.9 41.6 %copy-start.3 = (f32[1024,128]{1,0:T(8,128)S(1)}, f32[1024,128]{1,0:T(8,128)}, u32[]{:S(2)}) copy-start(f32[1024,128]{1,0:T(8,128)} %refs_3_.1) | copy-start | bytes 1572868
  95.1 10.4 %collective-permute-start.5 = (f32[520,128]{1,0:T(8,128)S(1)}, f32[520,128]{1,0:T(8,128)S(1)}, u32[]{:S(2)}, u32[]{:S(2)}) collective-permute-start(f32[520,128]{1,0:T(8,128)S(1)} %get-tuple-element.27), channel_id=1, source_target_pairs={{0,64},{64,0},{128,192},{192,128},{256,320},{320,256},{384,448},{4... | collective-permute-start | bytes 798728 | tf_op jit(solution)/shard_map/ppermute | solution.py:387
  105.5 4.0 %collective-permute-start.6 = (f32[520,128]{1,0:T(8,128)S(1)}, f32[520,128]{1,0:T(8,128)S(1)}, u32[]{:S(2)}, u32[]{:S(2)}) collective-permute-start(f32[520,128]{1,0:T(8,128)S(1)} %collective-permute-done.5.refs_2_), channel_id=1, source_target_pairs={{0,1},{1,0},{2,3},{3,2},{4,5},{5,4},{6,7},{7,6},{8,9},{9,8},{10,11... | collective-permute-start | bytes 798728 | tf_op jit(solution)/shard_map/ppermute | solution.py:387
  111.6 7.7 %collective-permute-start.7 = (f32[264,128]{1,0:T(8,128)S(1)}, f32[264,128]{1,0:T(8,128)S(1)}, u32[]{:S(2)}, u32[]{:S(2)}) collective-permute-start(f32[264,128]{1,0:T(8,128)S(1)} %get-tuple-element.31), channel_id=1, source_target_pairs={{0,128},{64,192},{128,0},{192,64},{256,384},{320,448},{384,256},{4... | collective-permute-start | bytes 405512 | tf_op jit(solution)/shard_map/ppermute | solution.py:387
  119.3 4.1 %collective-permute-start.8 = (f32[264,128]{1,0:T(8,128)S(1)}, f32[264,128]{1,0:T(8,128)S(1)}, u32[]{:S(2)}, u32[]{:S(2)}) collective-permute-start(f32[264,128]{1,0:T(8,128)S(1)} %collective-permute-done.7.refs_2_), channel_id=1, source_target_pairs={{0,1},{1,0},{2,3},{3,2},{4,5},{5,4},{6,7},{7,6},{8,9},{9,8},{10,11... | collective-permute-start | bytes 405512 | tf_op jit(solution)/shard_map/ppermute | solution.py:387
  125.3 15.9 %collective-permute-start.9 = (f32[2,128,128]{2,1,0:T(8,128)S(1)}, f32[2,128,128]{2,1,0:T(8,128)S(1)}, u32[]{:S(2)}, u32[]{:S(2)}) collective-permute-start(f32[2,128,128]{2,1,0:T(8,128)S(1)} %get-tuple-element.35.refs_1_), channel_id=1, source_target_pairs={{0,384},{64,448},{128,256},{192,320},{256,128},{320,192},{384,0},{... | collective-permute-start | bytes 393224 | tf_op jit(solution)/shard_map/ppermute | solution.py:387

commit v5 on v4

--- a/solution.py
+++ b/solution.py
@@ -465,7 +465,8 @@
 
 
 def gather_chips(piece):
-    return lax.all_gather(piece, "y")
+    copies = jnp.broadcast_to(piece.reshape(1, -1, K), (CHIPS, piece.size // K, K))
+    return lax.all_to_all(copies, "y", 0, 0).reshape((CHIPS,) + piece.shape)
 
 
 def solution(mesh):

time: 144 us -> 142 us (0.986)
  starting transfers between devices: 40.6 us -> 37.2 us
    all_to_all x0 -> x1, blocking collectives: none -> 22.6 us  [gather_chips(): return lax.all_to_all(copies, 'y', 0, 0).reshape((CHIPS,) + piece.shape)]
    all_gather x1 -> x0, blocking collectives: 21.3 us -> none  [gather_chips(): return lax.all_gather(piece, 'y')]
    ppermute x10, starting transfers between devices: 40.6 us -> 37.2 us  [swap(): return lax.ppermute(value, axis, pairs)]
where the time goes in v5:
time: 142 us
  blocking collectives  47.6 us (34%)
  waiting for transfers between devices  37.9 us (27%)
  starting transfers between devices  37.2 us (26%)
  Pallas kernels  15.8 us (11%)
  local copies, waits for them, and re-layouts  2.85 us (2%)
    ppermute x10, waiting for transfers between devices, swap(): return lax.ppermute(value, axis, pairs)  37.9 us
    ppermute x10, starting transfers between devices, swap(): return lax.ppermute(value, axis, pairs)  37.2 us
    all_to_all x1, blocking collectives, per_device(): part = lax.all_to_all(part, 'y', 0, 0).sum(0)  25 us
    all_to_all x1, blocking collectives, gather_chips(): return lax.all_to_all(copies, 'y', 0, 0).reshape((CHIPS,) + piece.shape)  22.6 us
    pallas_call x9, Pallas kernels, call(): pl.pallas_call(whole_body, out_shape=[jax.ShapeDtypeStruct(shape, jnp.flo...  15.8 us
  transfers between devices with their start and end apart: 10, of which 10 were waited for; matrix products, arithmetic and copies ran while one was open for 0% of the time, Pallas kernels for 1%

profile of v5, /device:TPU:135, one launch (start us, length us, event | category | flops | bytes accessed | tf_op | source)
XLA Modules:
  0.0 141.6 jit_solution(1637219539906560483)
XLA Ops:
  0.0 0.0 copy-start
  0.0 1.7 %copy-done = f32[5,1024,128]{2,1,0:T(8,128)S(1)} copy-done((f32[5,1024,128]{2,1,0:T(8,128)S(1)}, f32[5,1024,128]{2,1,0:T(8,128)}, u32[]{:S(2)}) %copy-start) | copy-done | bytes 2621464
  1.7 0.0 copy-start.2
  1.7 1.0 copy-done.2
  2.8 2.6 %shard_map.28 = (f32[8,18,8,128]{3,2,1,0:T(8,128)S(1)}, f32[8,18,8,128]{3,2,1,0:T(8,128)S(1)}) custom-call(s32[1]{0:T(128)} %bitcast.refs_0_, f32[5,1024,128]{2,1,0:T(8,128)S(1)} %copy-done, f32[1024,128]{1,0:T(8,128)S(1)} %copy-done.2), custom_call_target="tpu_custom_call" | custom-call | tf_op jit(solution)/shard_map/pallas_call | solution.py:99
  5.3 2.6 %collective-permute-start = (f32[8,18,8,128]{3,2,1,0:T(8,128)S(1)}, f32[8,18,8,128]{3,2,1,0:T(8,128)S(1)}, u32[]{:S(2)}, u32[]{:S(2)}) collective-permute-start(f32[8,18,8,128]{3,2,1,0:T(8,128)S(1)} %get-tuple-element.23), channel_id=1, source_target_pairs={{0,1},{1,0},{2,3},{3,2},{4,5},{5,4},{6,7},{7,6},{8,9},{9,8},{10,11... | collective-permute-start | bytes 1769480 | tf_op jit(solution)/shard_map/ppermute | solution.py:387
  7.9 1.6 %collective-permute-done = f32[8,18,8,128]{3,2,1,0:T(8,128)S(1)} collective-permute-done((f32[8,18,8,128]{3,2,1,0:T(8,128)S(1)}, f32[8,18,8,128]{3,2,1,0:T(8,128)S(1)}, u32[]{:S(2)}, u32[]{:S(2)}) %collective-permute-start) | collective-permute-done | bytes 589856 | tf_op jit(solution)/shard_map/ppermute | solution.py:387
  9.5 0.1 add.6
  9.6 25.0 %all_to_all.10 = f32[8,18,8,128]{3,2,1,0:T(8,128)S(1)} all-to-all(f32[8,18,8,128]{3,2,1,0:T(8,128)S(1)} %add.6), channel_id=1, replica_groups=mesh['z'=8,'x'=4,'y'=8,'c'=2] {'y'}, dimensions={0} | all-to-all | bytes 1179648 | tf_op jit(solution)/shard_map/all_to_all | solution.py:414
  34.7 2.5 %collective-permute-start.1 = (f32[18,8,128]{2,1,0:T(8,128)S(1)}, f32[18,8,128]{2,1,0:T(8,128)S(1)}, u32[]{:S(2)}, u32[]{:S(2)}) collective-permute-start(f32[18,8,128]{2,1,0:T(8,128)S(1)} %reduce_sum.9), channel_id=1, source_target_pairs={{0,16},{16,0},{32,48},{48,32},{1,17},{17,1},{33,49},{49,33},{2,18}... | collective-permute-start | bytes 221192 | tf_op jit(solution)/shard_map/ppermute | solution.py:387
  37.2 2.6 %collective-permute-done.1 = f32[18,8,128]{2,1,0:T(8,128)S(1)} collective-permute-done((f32[18,8,128]{2,1,0:T(8,128)S(1)}, f32[18,8,128]{2,1,0:T(8,128)S(1)}, u32[]{:S(2)}, u32[]{:S(2)}) %collective-permute-start.1) | collective-permute-done | bytes 73760 | tf_op jit(solution)/shard_map/ppermute | solution.py:387
  39.8 0.1 broadcast_in_dim.8
  39.9 22.6 %all_to_all.11 = f32[8,192,128]{2,1,0:T(8,128)S(1)} all-to-all(f32[8,192,128]{2,1,0:T(8,128)S(1)} %broadcast_in_dim.8), channel_id=1, replica_groups=mesh['z'=8,'x'=4,'y'=8,'c'=2] {'y'}, dimensions={0} | all-to-all | bytes 1572864 | tf_op jit(solution)/shard_map/all_to_all | solution.py:469
  62.4 5.8 %collective-permute-start.2 = (f32[8,24,8,128]{3,2,1,0:T(8,128)S(1)}, f32[8,24,8,128]{3,2,1,0:T(8,128)S(1)}, u32[]{:S(2)}, u32[]{:S(2)}) collective-permute-start(f32[8,24,8,128]{3,2,1,0:T(8,128)S(1)} %bitcast.4), channel_id=1, source_target_pairs={{0,1},{1,0},{2,3},{3,2},{4,5},{5,4},{6,7},{7,6},{8,9},{9,8},{10,11... | collective-permute-start | bytes 2359304 | tf_op jit(solution)/shard_map/ppermute | solution.py:387
  68.3 1.9 %collective-permute-done.2.refs_2_ = f32[8,24,8,128]{3,2,1,0:T(8,128)S(1)} collective-permute-done((f32[8,24,8,128]{3,2,1,0:T(8,128)S(1)}, f32[8,24,8,128]{3,2,1,0:T(8,128)S(1)}, u32[]{:S(2)}, u32[]{:S(2)}) %collective-permute-start.2) | collective-permute-done | bytes 786464 | tf_op jit(solution)/shard_map/ppermute | solution.py:387
  70.1 2.7 %shard_map.29 = (f32[14,128,128]{2,1,0:T(8,128)S(1)}, f32[776,128]{1,0:T(8,128)S(1)}, f32[5,128,128]{2,1,0:T(8,128)S(1)}) custom-call(s32[1]{0:T(128)} %bitcast.refs_0_, f32[8,24,8,128]{3,2,1,0:T(8,128)S(1)} %bitcast.5, f32[8,24,8,128]{3,2,1,0:T(8,128)S(1)} %collective-permute-done.2.refs_2_), custom_call_target="tpu_custom_call" | custom-call | tf_op jit(solution)/shard_map/pallas_call | solution.py:99
  72.8 2.1 %collective-permute-start.3 = (f32[776,128]{1,0:T(8,128)S(1)}, f32[776,128]{1,0:T(8,128)S(1)}, u32[]{:S(2)}, u32[]{:S(2)}) collective-permute-start(f32[776,128]{1,0:T(8,128)S(1)} %get-tuple-element.25), channel_id=1, source_target_pairs={{0,48},{16,32},{32,16},{48,0},{1,49},{17,33},{33,17},{49,1},{2,50}... | collective-permute-start | bytes 1191944 | tf_op jit(solution)/shard_map/ppermute | solution.py:387
  74.9 11.4 %collective-permute-done.3.refs_2_ = f32[776,128]{1,0:T(8,128)S(1)} collective-permute-done((f32[776,128]{1,0:T(8,128)S(1)}, f32[776,128]{1,0:T(8,128)S(1)}, u32[]{:S(2)}, u32[]{:S(2)}) %collective-permute-start.3) | collective-permute-done | bytes 397344 | tf_op jit(solution)/shard_map/ppermute | solution.py:387
  86.3 3.1 %collective-permute-start.4 = (f32[776,128]{1,0:T(8,128)S(1)}, f32[776,128]{1,0:T(8,128)S(1)}, u32[]{:S(2)}, u32[]{:S(2)}) collective-permute-start(f32[776,128]{1,0:T(8,128)S(1)} %collective-permute-done.3.refs_2_), channel_id=1, source_target_pairs={{0,1},{1,0},{2,3},{3,2},{4,5},{5,4},{6,7},{7,6},{8,9},{9,8},{10,11... | collective-permute-start | bytes 1191944 | tf_op jit(solution)/shard_map/ppermute | solution.py:387
  89.5 1.3 collective-permute-done.4.refs_3_
  90.8 0.0 copy-start.1
  90.8 0.0 copy-start.3
  90.8 2.3 %shard_map.30 = (f32[9,128,128]{2,1,0:T(8,128)S(1)}, f32[520,128]{1,0:T(8,128)S(1)}, f32[4,128,128]{2,1,0:T(8,128)S(1)}) custom-call(s32[1]{0:T(128)} %bitcast.refs_0_, f32[14,128,128]{2,1,0:T(8,128)S(1)} %get-tuple-element.24.refs_1_, f32[776,128]{1,0:T(8,128)S(1)} %collective-permute-done.3.refs_2_, f32[776,128]{1,0:T(8,128)S(1)} %collective-permute-done.4.refs_3_), custom_call_target="tpu_custom_call" | custom-call | tf_op jit(solution)/shard_map/pallas_call | solution.py:99
  93.1 4.0 %collective-permute-start.5 = (f32[520,128]{1,0:T(8,128)S(1)}, f32[520,128]{1,0:T(8,128)S(1)}, u32[]{:S(2)}, u32[]{:S(2)}) collective-permute-start(f32[520,128]{1,0:T(8,128)S(1)} %get-tuple-element.27), channel_id=1, source_target_pairs={{0,64},{64,0},{128,192},{192,128},{256,320},{320,256},{384,448},{4... | collective-permute-start | bytes 798728 | tf_op jit(solution)/shard_map/ppermute | solution.py:387
  97.1 6.4 %collective-permute-done.5.refs_2_ = f32[520,128]{1,0:T(8,128)S(1)} collective-permute-done((f32[520,128]{1,0:T(8,128)S(1)}, f32[520,128]{1,0:T(8,128)S(1)}, u32[]{:S(2)}, u32[]{:S(2)}) %collective-permute-start.5) | collective-permute-done | bytes 266272 | tf_op jit(solution)/shard_map/ppermute | solution.py:387
  103.5 2.8 %collective-permute-start.6 = (f32[520,128]{1,0:T(8,128)S(1)}, f32[520,128]{1,0:T(8,128)S(1)}, u32[]{:S(2)}, u32[]{:S(2)}) collective-permute-start(f32[520,128]{1,0:T(8,128)S(1)} %collective-permute-done.5.refs_2_), channel_id=1, source_target_pairs={{0,1},{1,0},{2,3},{3,2},{4,5},{5,4},{6,7},{7,6},{8,9},{9,8},{10,11... | collective-permute-start | bytes 798728 | tf_op jit(solution)/shard_map/ppermute | solution.py:387
  106.3 0.3 shard_map.31.refs_4_.refs_2_
  106.6 0.9 collective-permute-done.6.refs_3_
  107.5 2.1 %shard_map.32 = (f32[5,128,128]{2,1,0:T(8,128)S(1)}, f32[264,128]{1,0:T(8,128)S(1)}, f32[3,128,128]{2,1,0:T(8,128)S(1)}) custom-call(s32[1]{0:T(128)} %bitcast.refs_0_, f32[9,128,128]{2,1,0:T(8,128)S(1)} %get-tuple-element.26.refs_1_, f32[520,128]{1,0:T(8,128)S(1)} %collective-permute-done.5.refs_2_, f32[520,128]{1,0:T(8,128)S(1)} %collective-permute-done.6.refs_3_, ...), custom_call_target="tpu_custom_call" | custom-call | tf_op jit(solution)/shard_map/pallas_call | solution.py:99
  109.6 1.9 %collective-permute-start.7 = (f32[264,128]{1,0:T(8,128)S(1)}, f32[264,128]{1,0:T(8,128)S(1)}, u32[]{:S(2)}, u32[]{:S(2)}) collective-permute-start(f32[264,128]{1,0:T(8,128)S(1)} %get-tuple-element.31), channel_id=1, source_target_pairs={{0,128},{64,192},{128,0},{192,64},{256,384},{320,448},{384,256},{4... | collective-permute-start | bytes 405512 | tf_op jit(solution)/shard_map/ppermute | solution.py:387
  111.5 5.7 %collective-permute-done.7.refs_2_ = f32[264,128]{1,0:T(8,128)S(1)} collective-permute-done((f32[264,128]{1,0:T(8,128)S(1)}, f32[264,128]{1,0:T(8,128)S(1)}, u32[]{:S(2)}, u32[]{:S(2)}) %collective-permute-start.7) | collective-permute-done | bytes 135200 | tf_op jit(solution)/shard_map/ppermute | solution.py:387
  117.2 3.1 %collective-permute-start.8 = (f32[264,128]{1,0:T(8,128)S(1)}, f32[264,128]{1,0:T(8,128)S(1)}, u32[]{:S(2)}, u32[]{:S(2)}) collective-permute-start(f32[264,128]{1,0:T(8,128)S(1)} %collective-permute-done.7.refs_2_), channel_id=1, source_target_pairs={{0,1},{1,0},{2,3},{3,2},{4,5},{5,4},{6,7},{7,6},{8,9},{9,8},{10,11... | collective-permute-start | bytes 405512 | tf_op jit(solution)/shard_map/ppermute | solution.py:387
  120.4 0.3 shard_map.33
  120.7 0.6 collective-permute-done.8.refs_3_
  121.3 1.9 %shard_map.34 = (f32[2,128,128]{2,1,0:T(8,128)S(1)}, f32[2,128,128]{2,1,0:T(8,128)S(1)}) custom-call(s32[1]{0:T(128)} %bitcast.refs_0_, f32[5,128,128]{2,1,0:T(8,128)S(1)} %get-tuple-element.30.refs_1_, f32[264,128]{1,0:T(8,128)S(1)} %collective-permute-done.7.refs_2_, f32[264,128]{1,0:T(8,128)S(1)} %collective-permute-done.8.refs_3_, ...), custom_call_target="tpu_custom_call" | custom-call | tf_op jit(solution)/shard_map/pallas_call | solution.py:99
  123.2 9.2 %collective-permute-start.9 = (f32[2,128,128]{2,1,0:T(8,128)S(1)}, f32[2,128,128]{2,1,0:T(8,128)S(1)}, u32[]{:S(2)}, u32[]{:S(2)}) collective-permute-start(f32[2,128,128]{2,1,0:T(8,128)S(1)} %get-tuple-element.35.refs_1_), channel_id=1, source_target_pairs={{0,384},{64,448},{128,256},{192,320},{256,128},{320,192},{384,0},{... | collective-permute-start | bytes 393224 | tf_op jit(solution)/shard_map/ppermute | solution.py:387
  132.4 0.0 copy-done.1
  132.4 0.0 copy-done.3
  132.4 1.3 shard_map.35
  133.8 5.4 %collective-permute-done.9.refs_2_ = f32[2,128,128]{2,1,0:T(8,128)S(1)} collective-permute-done((f32[2,128,128]{2,1,0:T(8,128)S(1)}, f32[2,128,128]{2,1,0:T(8,128)S(1)}, u32[]{:S(2)}, u32[]{:S(2)}) %collective-permute-start.9) | collective-permute-done | bytes 131104 | tf_op jit(solution)/shard_map/ppermute | solution.py:387
  139.2 2.4 %shard_map.36 = f32[1024,128]{1,0:T(8,128)} custom-call(s32[1]{0:T(128)} %bitcast.refs_0_, f32[2,128,128]{2,1,0:T(8,128)S(1)} %get-tuple-element.35.refs_1_, f32[2,128,128]{2,1,0:T(8,128)S(1)} %collective-permute-done.9.refs_2_, f32[1024,128]{1,0:T(8,128)S(1)} %get-tuple-element.37.refs_3_, f32[1024,128]{1,0:T(8,128)S(1)} %get-tuple-element.38.refs_4_), custom_call_target="tpu_custom_call" | custom-call | tf_op jit(solution)/shard_map/pallas_call | solution.py:99
  (5 shorter events, 0.1 us)
Async XLA Ops:
  0.0 1.7 %copy-start = (f32[5,1024,128]{2,1,0:T(8,128)S(1)}, f32[5,1024,128]{2,1,0:T(8,128)}, u32[]{:S(2)}) copy-start(f32[5,1024,128]{2,1,0:T(8,128)} %refs_2_.3) | copy-start | bytes 7864324
  1.7 1.0 copy-start.2
  5.3 4.2 %collective-permute-start = (f32[8,18,8,128]{3,2,1,0:T(8,128)S(1)}, f32[8,18,8,128]{3,2,1,0:T(8,128)S(1)}, u32[]{:S(2)}, u32[]{:S(2)}) collective-permute-start(f32[8,18,8,128]{3,2,1,0:T(8,128)S(1)} %get-tuple-element.23), channel_id=1, source_target_pairs={{0,1},{1,0},{2,3},{3,2},{4,5},{5,4},{6,7},{7,6},{8,9},{9,8},{10,11... | collective-permute-start | bytes 1769480 | tf_op jit(solution)/shard_map/ppermute | solution.py:387
  34.7 5.1 %collective-permute-start.1 = (f32[18,8,128]{2,1,0:T(8,128)S(1)}, f32[18,8,128]{2,1,0:T(8,128)S(1)}, u32[]{:S(2)}, u32[]{:S(2)}) collective-permute-start(f32[18,8,128]{2,1,0:T(8,128)S(1)} %reduce_sum.9), channel_id=1, source_target_pairs={{0,16},{16,0},{32,48},{48,32},{1,17},{17,1},{33,49},{49,33},{2,18}... | collective-permute-start | bytes 221192 | tf_op jit(solution)/shard_map/ppermute | solution.py:387
  62.4 7.7 %collective-permute-start.2 = (f32[8,24,8,128]{3,2,1,0:T(8,128)S(1)}, f32[8,24,8,128]{3,2,1,0:T(8,128)S(1)}, u32[]{:S(2)}, u32[]{:S(2)}) collective-permute-start(f32[8,24,8,128]{3,2,1,0:T(8,128)S(1)} %bitcast.4), channel_id=1, source_target_pairs={{0,1},{1,0},{2,3},{3,2},{4,5},{5,4},{6,7},{7,6},{8,9},{9,8},{10,11... | collective-permute-start | bytes 2359304 | tf_op jit(solution)/shard_map/ppermute | solution.py:387
  72.8 13.5 %collective-permute-start.3 = (f32[776,128]{1,0:T(8,128)S(1)}, f32[776,128]{1,0:T(8,128)S(1)}, u32[]{:S(2)}, u32[]{:S(2)}) collective-permute-start(f32[776,128]{1,0:T(8,128)S(1)} %get-tuple-element.25), channel_id=1, source_target_pairs={{0,48},{16,32},{32,16},{48,0},{1,49},{17,33},{33,17},{49,1},{2,50}... | collective-permute-start | bytes 1191944 | tf_op jit(solution)/shard_map/ppermute | solution.py:387
  86.3 4.5 %collective-permute-start.4 = (f32[776,128]{1,0:T(8,128)S(1)}, f32[776,128]{1,0:T(8,128)S(1)}, u32[]{:S(2)}, u32[]{:S(2)}) collective-permute-start(f32[776,128]{1,0:T(8,128)S(1)} %collective-permute-done.3.refs_2_), channel_id=1, source_target_pairs={{0,1},{1,0},{2,3},{3,2},{4,5},{5,4},{6,7},{7,6},{8,9},{9,8},{10,11... | collective-permute-start | bytes 1191944 | tf_op jit(solution)/shard_map/ppermute | solution.py:387
  90.8 41.6 %copy-start.1 = (f32[5,1024,128]{2,1,0:T(8,128)S(1)}, f32[5,1024,128]{2,1,0:T(8,128)}, u32[]{:S(2)}) copy-start(f32[5,1024,128]{2,1,0:T(8,128)} %refs_2_.3) | copy-start | bytes 7864324
  90.8 41.6 %copy-start.3 = (f32[1024,128]{1,0:T(8,128)S(1)}, f32[1024,128]{1,0:T(8,128)}, u32[]{:S(2)}) copy-start(f32[1024,128]{1,0:T(8,128)} %refs_3_.1) | copy-start | bytes 1572868
  93.1 10.4 %collective-permute-start.5 = (f32[520,128]{1,0:T(8,128)S(1)}, f32[520,128]{1,0:T(8,128)S(1)}, u32[]{:S(2)}, u32[]{:S(2)}) collective-permute-start(f32[520,128]{1,0:T(8,128)S(1)} %get-tuple-element.27), channel_id=1, source_target_pairs={{0,64},{64,0},{128,192},{192,128},{256,320},{320,256},{384,448},{4... | collective-permute-start | bytes 798728 | tf_op jit(solution)/shard_map/ppermute | solution.py:387
  103.5 4.0 %collective-permute-start.6 = (f32[520,128]{1,0:T(8,128)S(1)}, f32[520,128]{1,0:T(8,128)S(1)}, u32[]{:S(2)}, u32[]{:S(2)}) collective-permute-start(f32[520,128]{1,0:T(8,128)S(1)} %collective-permute-done.5.refs_2_), channel_id=1, source_target_pairs={{0,1},{1,0},{2,3},{3,2},{4,5},{5,4},{6,7},{7,6},{8,9},{9,8},{10,11... | collective-permute-start | bytes 798728 | tf_op jit(solution)/shard_map/ppermute | solution.py:387
  109.6 7.7 %collective-permute-start.7 = (f32[264,128]{1,0:T(8,128)S(1)}, f32[264,128]{1,0:T(8,128)S(1)}, u32[]{:S(2)}, u32[]{:S(2)}) collective-permute-start(f32[264,128]{1,0:T(8,128)S(1)} %get-tuple-element.31), channel_id=1, source_target_pairs={{0,128},{64,192},{128,0},{192,64},{256,384},{320,448},{384,256},{4... | collective-permute-start | bytes 405512 | tf_op jit(solution)/shard_map/ppermute | solution.py:387
  117.2 4.1 %collective-permute-start.8 = (f32[264,128]{1,0:T(8,128)S(1)}, f32[264,128]{1,0:T(8,128)S(1)}, u32[]{:S(2)}, u32[]{:S(2)}) collective-permute-start(f32[264,128]{1,0:T(8,128)S(1)} %collective-permute-done.7.refs_2_), channel_id=1, source_target_pairs={{0,1},{1,0},{2,3},{3,2},{4,5},{5,4},{6,7},{7,6},{8,9},{9,8},{10,11... | collective-permute-start | bytes 405512 | tf_op jit(solution)/shard_map/ppermute | solution.py:387
  123.2 16.0 %collective-permute-start.9 = (f32[2,128,128]{2,1,0:T(8,128)S(1)}, f32[2,128,128]{2,1,0:T(8,128)S(1)}, u32[]{:S(2)}, u32[]{:S(2)}) collective-permute-start(f32[2,128,128]{2,1,0:T(8,128)S(1)} %get-tuple-element.35.refs_1_), channel_id=1, source_target_pairs={{0,384},{64,448},{128,256},{192,320},{256,128},{320,192},{384,0},{... | collective-permute-start | bytes 393224 | tf_op jit(solution)/shard_map/ppermute | solution.py:387

commit v6 on v4

--- a/solution.py
+++ b/solution.py
@@ -11,8 +11,10 @@
 LEVELS = 5
 K = 128
 HALF = K // 2
-AXES = ("z", "x", "y", "c")
-SIZES = (8, 4, 8, 2)
+AXES = ("z", "x1", "x0", "y", "c")
+SIZES = (8, 2, 2, 8, 2)
+X_AXES = ("x1", "x0")
+PAIR_AXES = ("x0", "y")
 VMEM_SPEC = pl.BlockSpec(memory_space=pltpu.VMEM)
 SMEM_SPEC = pl.BlockSpec(memory_space=pltpu.SMEM)
 
@@ -110,6 +112,15 @@
 
 
 GROUPS = (((4, 3), (4, 3, 2, 1, 0, 5)), ((2, 1), (2, 1, 0, 5)), ((0,), (0, 5)))
+
+
+HEAD = LEVELS + 1
+
+
+def owner_of(at):
+    if at < HEAD:
+        return at % 2, at // 2
+    return (at - HEAD) % 2, HEAD // 2 + (at - HEAD) // 2
 
 
 def hidden_diagonals(made):
@@ -160,12 +171,13 @@
             value = made[entry]
         low = value[:HALF].reshape(CHIPS, TILE, K)
         high = value[HALF:].reshape(CHIPS, TILE, K)
-        keep_ref[:, at] = jnp.where(first, low, high)
-        send_ref[:, at] = jnp.where(first, high, low)
+        side, to = owner_of(at)
+        keep_ref[side, :, to] = jnp.where(first, low, high)
+        send_ref[side, :, to] = jnp.where(first, high, low)
 
 
 def local_grams(core, bases, targets):
-    shape = (CHIPS, TOTAL, TILE, K)
+    shape = (2, CHIPS, TOTAL // 2, TILE, K)
     return call(gram_body, [shape, shape], core, bases, targets)
 
 
@@ -288,19 +300,23 @@
 
 
 def finest_body(
-    core_ref, half_ref, far_ref, next_ref, send_ref, coef_ref, work_ref, packed_ref
+    place_ref, half_ref, far_ref, next_ref, send_ref, coef_ref, work_ref, packed_ref
 ):
     level_no = LEVELS - 1
-    core_no = core_ref[0]
+    core_no = place_ref[0]
     count = level_no + 2
-    join_halves(
-        core_no,
-        half_ref.shape[1],
-        half_ref,
-        far_ref,
-        packed_ref,
-        lambda ref, at: ref[:, at].reshape(HALF, K),
-    )
+    own = pl.ds(pl.multiple_of(core_no * HALF, HALF), HALF)
+    far = pl.ds(pl.multiple_of((1 - core_no) * HALF, HALF), HALF)
+    for at in range(TOTAL):
+        side, source = owner_of(at)
+        if at < HEAD:
+            mine = place_ref[1] * HEAD + at
+            moves = ((source, mine), (HEAD // 2 + source, HEAD + 2 * at - mine))
+        else:
+            moves = ((HEAD // 2 + source, HEAD + at),)
+        for source, to in moves:
+            packed_ref[to, own] = half_ref[side, :, source].reshape(HALF, K)
+            packed_ref[to, far] = far_ref[side, :, source].reshape(HALF, K)
     diagonals = found_diagonals(packed_ref[0] + packed_ref[count])
     order = packed_order(level_no)
     both = unpack(level_no, order[count:], packed_ref, 2 * count, diagonals)
@@ -392,8 +408,7 @@
 
 
 PARTNERS = {
-    4: ("x", lambda at: at ^ 1),
-    3: ("x", lambda at: 3 - at),
+    3: (X_AXES, lambda at: 3 - at),
     2: ("z", lambda at: at ^ 1),
     1: ("z", lambda at: at ^ 2),
     0: ("z", lambda at: (6, 7, 4, 5, 2, 3, 0, 1)[at]),
@@ -408,12 +423,15 @@
 def per_device(bases, targets):
     top = LEVELS - 1
     head = top + 2
-    core = lax.axis_index("c").astype(jnp.int32).reshape(1)
+    place = [lax.axis_index(axis).astype(jnp.int32) for axis in ("c", "x0")]
+    core = jnp.stack(place)
     keep, send = local_grams(core, bases, targets)
     part = keep + swap_cores(send)
-    part = lax.all_to_all(part, "y", 0, 0).sum(0)
-    other = swap(part, *PARTNERS[top])
-    piece = jnp.concatenate([part[:head], other[:head], part[head:] + other[head:]], 0)
+    part = part.reshape(2 * CHIPS, TOTAL // 2 * TILE, K)
+    part = lax.all_to_all(part, PAIR_AXES, 0, 0)
+    sums = part.reshape(2, CHIPS, TOTAL // 2, TILE, K).sum(1)
+    mine = head // 2
+    piece = jnp.concatenate([sums[0, :mine], sums[1, :mine], sums[0, mine:] + sums[1, mine:]], 0)
     half = gather_chips(piece)
     far = swap_cores(half)
     below = rows_up_to(top - 1)
@@ -423,7 +441,7 @@
         core,
         half,
         far,
-        scratch=[WORK, (piece.shape[0], K, K)],
+        scratch=[WORK, (2 * piece.shape[0], K, K)],
     )
     mults = [coef]
     folded = []
@@ -465,7 +483,9 @@
 
 
 def gather_chips(piece):
-    return lax.all_gather(piece, "y")
+    copies = jnp.broadcast_to(piece.reshape(1, -1, K), (2 * CHIPS, piece.size // K, K))
+    gathered = lax.all_to_all(copies, PAIR_AXES, 0, 0)
+    return gathered.reshape((2, CHIPS) + piece.shape)
 
 
 def solution(mesh):

time: 144 us -> 141 us (0.979)
  the two profiles are of different devices: /device:TPU:135 before, /device:TPU:137 now
where the time goes in v6:
time: 141 us; the launch traced here: 140 us
  blocking collectives  50 us (35%)
  starting transfers between devices  34.7 us (25%)
  waiting for transfers between devices  31.7 us (22%)
  Pallas kernels  20.7 us (15%)
  local copies, waits for them, and re-layouts  2.86 us (2%)
    ppermute x9, starting transfers between devices, swap(): return lax.ppermute(value, axis, pairs)  34.7 us
    ppermute x9, waiting for transfers between devices, swap(): return lax.ppermute(value, axis, pairs)  31.7 us
    all_to_all x1, blocking collectives, gather_chips(): gathered = lax.all_to_all(copies, PAIR_AXES, 0, 0)  25 us
    all_to_all x1, blocking collectives, per_device(): part = lax.all_to_all(part, PAIR_AXES, 0, 0)  24.9 us
    pallas_call x9, Pallas kernels, call(): pl.pallas_call(whole_body, out_shape=[jax.ShapeDtypeStruct(shape, jnp.flo...  20.7 us
  transfers between devices with their start and end apart: 9, of which 9 were waited for; matrix products, arithmetic and copies ran while one was open for 0% of the time, Pallas kernels for 3%

profile of v6, /device:TPU:137, one launch (start us, length us, event | category | flops | bytes accessed | tf_op | source)
XLA Modules:
  0.0 140.3 jit_solution(12760737991332759811)
XLA Ops:
  0.0 0.1 pad_add_fusion.refs_0_
  0.1 0.0 copy-start
  0.1 1.7 %copy-done = f32[5,1024,128]{2,1,0:T(8,128)S(1)} copy-done((f32[5,1024,128]{2,1,0:T(8,128)S(1)}, f32[5,1024,128]{2,1,0:T(8,128)}, u32[]{:S(2)}) %copy-start) | copy-done | bytes 2621464
  1.8 0.0 copy-start.2
  1.8 1.0 copy-done.2
  2.9 3.1 %shard_map.28 = (f32[2,8,9,8,128]{4,3,2,1,0:T(8,128)S(1)}, f32[2,8,9,8,128]{4,3,2,1,0:T(8,128)S(1)}) custom-call(s32[2]{0:T(128)S(1)} %pad_add_fusion.refs_0_, f32[5,1024,128]{2,1,0:T(8,128)S(1)} %copy-done, f32[1024,128]{1,0:T(8,128)S(1)} %copy-done.2), custom_call_target="tpu_custom_call" | custom-call | tf_op jit(solution)/shard_map/pallas_call | solution.py:101
  6.0 2.6 %collective-permute-start = (f32[2,8,9,8,128]{4,3,2,1,0:T(8,128)S(1)}, f32[2,8,9,8,128]{4,3,2,1,0:T(8,128)S(1)}, u32[]{:S(2)}, u32[]{:S(2)}) collective-permute-start(f32[2,8,9,8,128]{4,3,2,1,0:T(8,128)S(1)} %get-tuple-element.23), channel_id=1, source_target_pairs={{0,1},{1,0},{2,3},{3,2},{4,5},{5,4},{6,7},{7,6},{8,9},{9,8},{10,11... | collective-permute-start | bytes 1769480 | tf_op jit(solution)/shard_map/ppermute | solution.py:403
  8.5 1.6 %collective-permute-done = f32[2,8,9,8,128]{4,3,2,1,0:T(8,128)S(1)} collective-permute-done((f32[2,8,9,8,128]{4,3,2,1,0:T(8,128)S(1)}, f32[2,8,9,8,128]{4,3,2,1,0:T(8,128)S(1)}, u32[]{:S(2)}, u32[]{:S(2)}) %collective-permute-start) | collective-permute-done | bytes 589856 | tf_op jit(solution)/shard_map/ppermute | solution.py:403
  10.2 0.1 add.9
  10.2 24.9 %all_to_all.10 = f32[16,72,128]{2,1,0:T(8,128)S(1)} all-to-all(f32[16,72,128]{2,1,0:T(8,128)S(1)} %bitcast.15), channel_id=1, replica_groups=mesh['z'=8,'x1'=2,'x0'=2,'y'=8,'c'=2] {'x0','y'}, dimensions={0} | all-to-all | bytes 1179648 | tf_op jit(solution)/shard_map/all_to_all | solution.py:431
  35.2 0.1 broadcast_in_dim.8
  35.3 25.0 %all_to_all.11 = f32[16,96,128]{2,1,0:T(8,128)S(1)} all-to-all(f32[16,96,128]{2,1,0:T(8,128)S(1)} %broadcast_in_dim.8), channel_id=1, replica_groups=mesh['z'=8,'x1'=2,'x0'=2,'y'=8,'c'=2] {'x0','y'}, dimensions={0} | all-to-all | bytes 1572864 | tf_op jit(solution)/shard_map/all_to_all | solution.py:487
  60.3 3.9 %collective-permute-start.1 = (f32[2,8,12,8,128]{4,3,2,1,0:T(8,128)S(1)}, f32[2,8,12,8,128]{4,3,2,1,0:T(8,128)S(1)}, u32[]{:S(2)}, u32[]{:S(2)}) collective-permute-start(f32[2,8,12,8,128]{4,3,2,1,0:T(8,128)S(1)} %bitcast.13), channel_id=1, source_target_pairs={{0,1},{1,0},{2,3},{3,2},{4,5},{5,4},{6,7},{7,6},{8,9},{9,8},{10,11... | collective-permute-start | bytes 2359304 | tf_op jit(solution)/shard_map/ppermute | solution.py:403
  64.2 1.9 %collective-permute-done.1.refs_2_ = f32[2,8,12,8,128]{4,3,2,1,0:T(8,128)S(1)} collective-permute-done((f32[2,8,12,8,128]{4,3,2,1,0:T(8,128)S(1)}, f32[2,8,12,8,128]{4,3,2,1,0:T(8,128)S(1)}, u32[]{:S(2)}, u32[]{:S(2)}) %collective-permute-start.1) | collective-permute-done | bytes 786464 | tf_op jit(solution)/shard_map/ppermute | solution.py:403
  66.1 3.2 %shard_map.29 = (f32[14,128,128]{2,1,0:T(8,128)S(1)}, f32[776,128]{1,0:T(8,128)S(1)}, f32[5,128,128]{2,1,0:T(8,128)S(1)}) custom-call(s32[2]{0:T(128)S(1)} %pad_add_fusion.refs_0_, f32[2,8,12,8,128]{4,3,2,1,0:T(8,128)S(1)} %bitcast.14, f32[2,8,12,8,128]{4,3,2,1,0:T(8,128)S(1)} %collective-permute-done.1.refs_2_), custom_call_target="tpu_custom_call" | custom-call | tf_op jit(solution)/shard_map/pallas_call | solution.py:101
  69.4 4.0 %collective-permute-start.2 = (f32[776,128]{1,0:T(8,128)S(1)}, f32[776,128]{1,0:T(8,128)S(1)}, u32[]{:S(2)}, u32[]{:S(2)}) collective-permute-start(f32[776,128]{1,0:T(8,128)S(1)} %get-tuple-element.25), channel_id=1, source_target_pairs={{0,48},{16,32},{32,16},{48,0},{1,49},{17,33},{33,17},{49,1},{2,50}... | collective-permute-start | bytes 1191944 | tf_op jit(solution)/shard_map/ppermute | solution.py:403
  73.4 9.5 %collective-permute-done.2.refs_2_ = f32[776,128]{1,0:T(8,128)S(1)} collective-permute-done((f32[776,128]{1,0:T(8,128)S(1)}, f32[776,128]{1,0:T(8,128)S(1)}, u32[]{:S(2)}, u32[]{:S(2)}) %collective-permute-start.2) | collective-permute-done | bytes 397344 | tf_op jit(solution)/shard_map/ppermute | solution.py:403
  82.9 3.1 %collective-permute-start.3 = (f32[776,128]{1,0:T(8,128)S(1)}, f32[776,128]{1,0:T(8,128)S(1)}, u32[]{:S(2)}, u32[]{:S(2)}) collective-permute-start(f32[776,128]{1,0:T(8,128)S(1)} %collective-permute-done.2.refs_2_), channel_id=1, source_target_pairs={{0,1},{1,0},{2,3},{3,2},{4,5},{5,4},{6,7},{7,6},{8,9},{9,8},{10,11... | collective-permute-start | bytes 1191944 | tf_op jit(solution)/shard_map/ppermute | solution.py:403
  86.0 1.3 collective-permute-done.3.refs_3_
  87.3 0.0 copy-start.1
  87.3 0.0 copy-start.3
  87.3 2.8 %shard_map.30 = (f32[9,128,128]{2,1,0:T(8,128)S(1)}, f32[520,128]{1,0:T(8,128)S(1)}, f32[4,128,128]{2,1,0:T(8,128)S(1)}) custom-call(s32[2]{0:T(128)S(1)} %pad_add_fusion.refs_0_, f32[14,128,128]{2,1,0:T(8,128)S(1)} %get-tuple-element.24.refs_1_, f32[776,128]{1,0:T(8,128)S(1)} %collective-permute-done.2.refs_2_, f32[776,128]{1,0:T(8,128)S(1)} %collective-permute-done.3.refs_3_), custom_call_target="tpu_custom_call" | custom-call | tf_op jit(solution)/shard_map/pallas_call | solution.py:101
  90.2 4.0 %collective-permute-start.4 = (f32[520,128]{1,0:T(8,128)S(1)}, f32[520,128]{1,0:T(8,128)S(1)}, u32[]{:S(2)}, u32[]{:S(2)}) collective-permute-start(f32[520,128]{1,0:T(8,128)S(1)} %get-tuple-element.27), channel_id=1, source_target_pairs={{0,64},{64,0},{128,192},{192,128},{256,320},{320,256},{384,448},{4... | collective-permute-start | bytes 798728 | tf_op jit(solution)/shard_map/ppermute | solution.py:403
  94.2 6.4 %collective-permute-done.4.refs_2_ = f32[520,128]{1,0:T(8,128)S(1)} collective-permute-done((f32[520,128]{1,0:T(8,128)S(1)}, f32[520,128]{1,0:T(8,128)S(1)}, u32[]{:S(2)}, u32[]{:S(2)}) %collective-permute-start.4) | collective-permute-done | bytes 266272 | tf_op jit(solution)/shard_map/ppermute | solution.py:403
  100.6 2.8 %collective-permute-start.5 = (f32[520,128]{1,0:T(8,128)S(1)}, f32[520,128]{1,0:T(8,128)S(1)}, u32[]{:S(2)}, u32[]{:S(2)}) collective-permute-start(f32[520,128]{1,0:T(8,128)S(1)} %collective-permute-done.4.refs_2_), channel_id=1, source_target_pairs={{0,1},{1,0},{2,3},{3,2},{4,5},{5,4},{6,7},{7,6},{8,9},{9,8},{10,11... | collective-permute-start | bytes 798728 | tf_op jit(solution)/shard_map/ppermute | solution.py:403
  103.4 0.8 shard_map.31.refs_4_.refs_2_
  104.2 0.3 collective-permute-done.5.refs_3_
  104.6 2.6 %shard_map.32 = (f32[5,128,128]{2,1,0:T(8,128)S(1)}, f32[264,128]{1,0:T(8,128)S(1)}, f32[3,128,128]{2,1,0:T(8,128)S(1)}) custom-call(s32[2]{0:T(128)S(1)} %pad_add_fusion.refs_0_, f32[9,128,128]{2,1,0:T(8,128)S(1)} %get-tuple-element.26.refs_1_, f32[520,128]{1,0:T(8,128)S(1)} %collective-permute-done.4.refs_2_, ...), custom_call_target="tpu_custom_call" | custom-call | tf_op jit(solution)/shard_map/pallas_call | solution.py:101
  107.2 1.9 %collective-permute-start.6 = (f32[264,128]{1,0:T(8,128)S(1)}, f32[264,128]{1,0:T(8,128)S(1)}, u32[]{:S(2)}, u32[]{:S(2)}) collective-permute-start(f32[264,128]{1,0:T(8,128)S(1)} %get-tuple-element.31), channel_id=1, source_target_pairs={{0,128},{64,192},{128,0},{192,64},{256,384},{320,448},{384,256},{4... | collective-permute-start | bytes 405512 | tf_op jit(solution)/shard_map/ppermute | solution.py:403
  109.1 5.7 %collective-permute-done.6.refs_2_ = f32[264,128]{1,0:T(8,128)S(1)} collective-permute-done((f32[264,128]{1,0:T(8,128)S(1)}, f32[264,128]{1,0:T(8,128)S(1)}, u32[]{:S(2)}, u32[]{:S(2)}) %collective-permute-start.6) | collective-permute-done | bytes 135200 | tf_op jit(solution)/shard_map/ppermute | solution.py:403
  114.8 3.1 %collective-permute-start.7 = (f32[264,128]{1,0:T(8,128)S(1)}, f32[264,128]{1,0:T(8,128)S(1)}, u32[]{:S(2)}, u32[]{:S(2)}) collective-permute-start(f32[264,128]{1,0:T(8,128)S(1)} %collective-permute-done.6.refs_2_), channel_id=1, source_target_pairs={{0,1},{1,0},{2,3},{3,2},{4,5},{5,4},{6,7},{7,6},{8,9},{9,8},{10,11... | collective-permute-start | bytes 405512 | tf_op jit(solution)/shard_map/ppermute | solution.py:403
  118.0 0.9 shard_map.33
  118.8 0.1 collective-permute-done.7.refs_3_
  118.9 2.4 %shard_map.34 = (f32[2,128,128]{2,1,0:T(8,128)S(1)}, f32[2,128,128]{2,1,0:T(8,128)S(1)}) custom-call(s32[2]{0:T(128)S(1)} %pad_add_fusion.refs_0_, f32[5,128,128]{2,1,0:T(8,128)S(1)} %get-tuple-element.30.refs_1_, f32[264,128]{1,0:T(8,128)S(1)} %collective-permute-done.6.refs_2_, f32[264,128]{1,0:T(8,128)S(1)} %collective-permute-done.7.refs_3_, ...), custom_call_target="tpu_custom_call" | custom-call | tf_op jit(solution)/shard_map/pallas_call | solution.py:101
  121.4 9.2 %collective-permute-start.8 = (f32[2,128,128]{2,1,0:T(8,128)S(1)}, f32[2,128,128]{2,1,0:T(8,128)S(1)}, u32[]{:S(2)}, u32[]{:S(2)}) collective-permute-start(f32[2,128,128]{2,1,0:T(8,128)S(1)} %get-tuple-element.35.refs_1_), channel_id=1, source_target_pairs={{0,384},{64,448},{128,256},{192,320},{256,128},{320,192},{384,0},{... | collective-permute-start | bytes 393224 | tf_op jit(solution)/shard_map/ppermute | solution.py:403
  130.6 0.0 copy-done.1
  130.6 0.0 copy-done.3
  130.6 1.9 %shard_map.35 = (f32[1024,128]{1,0:T(8,128)S(1)}, f32[1024,128]{1,0:T(8,128)S(1)}) custom-call(s32[2]{0:T(128)S(1)} %pad_add_fusion.refs_0_, f32[2,128,128]{2,1,0:T(8,128)S(1)} %get-tuple-element.36.refs_1_, f32[5,1024,128]{2,1,0:T(8,128)S(1)} %copy-done.1, f32[1024,128]{1,0:T(8,128)S(1)} %copy-done.3, f32[3,128,128]{2,1,0:T(8,128)S(1)} %get-tuple-element.33.refs_4_, ...), custom_call_target="tpu_custom_call" | custom-call | tf_op jit(solution)/shard_map/pallas_call | solution.py:101
  132.5 4.9 %collective-permute-done.8.refs_2_ = f32[2,128,128]{2,1,0:T(8,128)S(1)} collective-permute-done((f32[2,128,128]{2,1,0:T(8,128)S(1)}, f32[2,128,128]{2,1,0:T(8,128)S(1)}, u32[]{:S(2)}, u32[]{:S(2)}) %collective-permute-start.8) | collective-permute-done | bytes 131104 | tf_op jit(solution)/shard_map/ppermute | solution.py:403
  137.4 2.9 %shard_map.36 = f32[1024,128]{1,0:T(8,128)} custom-call(s32[2]{0:T(128)S(1)} %pad_add_fusion.refs_0_, f32[2,128,128]{2,1,0:T(8,128)S(1)} %get-tuple-element.35.refs_1_, f32[2,128,128]{2,1,0:T(8,128)S(1)} %collective-permute-done.8.refs_2_, f32[1024,128]{1,0:T(8,128)S(1)} %get-tuple-element.37.refs_3_, f32[1024,128]{1,0:T(8,128)S(1)} %get-tuple-element.38.refs_4_), custom_call_target="tpu_custom_call" | custom-call | tf_op jit(solution)/shard_map/pallas_call | solution.py:101
  (4 shorter events, 0.0 us)
Async XLA Ops:
  0.1 1.7 %copy-start = (f32[5,1024,128]{2,1,0:T(8,128)S(1)}, f32[5,1024,128]{2,1,0:T(8,128)}, u32[]{:S(2)}) copy-start(f32[5,1024,128]{2,1,0:T(8,128)} %refs_2_.3) | copy-start | bytes 7864324
  1.8 1.0 copy-start.2
  6.0 4.2 %collective-permute-start = (f32[2,8,9,8,128]{4,3,2,1,0:T(8,128)S(1)}, f32[2,8,9,8,128]{4,3,2,1,0:T(8,128)S(1)}, u32[]{:S(2)}, u32[]{:S(2)}) collective-permute-start(f32[2,8,9,8,128]{4,3,2,1,0:T(8,128)S(1)} %get-tuple-element.23), channel_id=1, source_target_pairs={{0,1},{1,0},{2,3},{3,2},{4,5},{5,4},{6,7},{7,6},{8,9},{9,8},{10,11... | collective-permute-start | bytes 1769480 | tf_op jit(solution)/shard_map/ppermute | solution.py:403
  60.3 5.8 %collective-permute-start.1 = (f32[2,8,12,8,128]{4,3,2,1,0:T(8,128)S(1)}, f32[2,8,12,8,128]{4,3,2,1,0:T(8,128)S(1)}, u32[]{:S(2)}, u32[]{:S(2)}) collective-permute-start(f32[2,8,12,8,128]{4,3,2,1,0:T(8,128)S(1)} %bitcast.13), channel_id=1, source_target_pairs={{0,1},{1,0},{2,3},{3,2},{4,5},{5,4},{6,7},{7,6},{8,9},{9,8},{10,11... | collective-permute-start | bytes 2359304 | tf_op jit(solution)/shard_map/ppermute | solution.py:403
  69.4 13.5 %collective-permute-start.2 = (f32[776,128]{1,0:T(8,128)S(1)}, f32[776,128]{1,0:T(8,128)S(1)}, u32[]{:S(2)}, u32[]{:S(2)}) collective-permute-start(f32[776,128]{1,0:T(8,128)S(1)} %get-tuple-element.25), channel_id=1, source_target_pairs={{0,48},{16,32},{32,16},{48,0},{1,49},{17,33},{33,17},{49,1},{2,50}... | collective-permute-start | bytes 1191944 | tf_op jit(solution)/shard_map/ppermute | solution.py:403
  82.9 4.5 %collective-permute-start.3 = (f32[776,128]{1,0:T(8,128)S(1)}, f32[776,128]{1,0:T(8,128)S(1)}, u32[]{:S(2)}, u32[]{:S(2)}) collective-permute-start(f32[776,128]{1,0:T(8,128)S(1)} %collective-permute-done.2.refs_2_), channel_id=1, source_target_pairs={{0,1},{1,0},{2,3},{3,2},{4,5},{5,4},{6,7},{7,6},{8,9},{9,8},{10,11... | collective-permute-start | bytes 1191944 | tf_op jit(solution)/shard_map/ppermute | solution.py:403
  87.3 43.2 %copy-start.1 = (f32[5,1024,128]{2,1,0:T(8,128)S(1)}, f32[5,1024,128]{2,1,0:T(8,128)}, u32[]{:S(2)}) copy-start(f32[5,1024,128]{2,1,0:T(8,128)} %refs_2_.3) | copy-start | bytes 7864324
  87.3 43.3 %copy-start.3 = (f32[1024,128]{1,0:T(8,128)S(1)}, f32[1024,128]{1,0:T(8,128)}, u32[]{:S(2)}) copy-start(f32[1024,128]{1,0:T(8,128)} %refs_3_.1) | copy-start | bytes 1572868
  90.2 10.4 %collective-permute-start.4 = (f32[520,128]{1,0:T(8,128)S(1)}, f32[520,128]{1,0:T(8,128)S(1)}, u32[]{:S(2)}, u32[]{:S(2)}) collective-permute-start(f32[520,128]{1,0:T(8,128)S(1)} %get-tuple-element.27), channel_id=1, source_target_pairs={{0,64},{64,0},{128,192},{192,128},{256,320},{320,256},{384,448},{4... | collective-permute-start | bytes 798728 | tf_op jit(solution)/shard_map/ppermute | solution.py:403
  100.6 4.0 %collective-permute-start.5 = (f32[520,128]{1,0:T(8,128)S(1)}, f32[520,128]{1,0:T(8,128)S(1)}, u32[]{:S(2)}, u32[]{:S(2)}) collective-permute-start(f32[520,128]{1,0:T(8,128)S(1)} %collective-permute-done.4.refs_2_), channel_id=1, source_target_pairs={{0,1},{1,0},{2,3},{3,2},{4,5},{5,4},{6,7},{7,6},{8,9},{9,8},{10,11... | collective-permute-start | bytes 798728 | tf_op jit(solution)/shard_map/ppermute | solution.py:403
  107.2 7.7 %collective-permute-start.6 = (f32[264,128]{1,0:T(8,128)S(1)}, f32[264,128]{1,0:T(8,128)S(1)}, u32[]{:S(2)}, u32[]{:S(2)}) collective-permute-start(f32[264,128]{1,0:T(8,128)S(1)} %get-tuple-element.31), channel_id=1, source_target_pairs={{0,128},{64,192},{128,0},{192,64},{256,384},{320,448},{384,256},{4... | collective-permute-start | bytes 405512 | tf_op jit(solution)/shard_map/ppermute | solution.py:403
  114.8 4.1 %collective-permute-start.7 = (f32[264,128]{1,0:T(8,128)S(1)}, f32[264,128]{1,0:T(8,128)S(1)}, u32[]{:S(2)}, u32[]{:S(2)}) collective-permute-start(f32[264,128]{1,0:T(8,128)S(1)} %collective-permute-done.6.refs_2_), channel_id=1, source_target_pairs={{0,1},{1,0},{2,3},{3,2},{4,5},{5,4},{6,7},{7,6},{8,9},{9,8},{10,11... | collective-permute-start | bytes 405512 | tf_op jit(solution)/shard_map/ppermute | solution.py:403
  121.4 16.0 %collective-permute-start.8 = (f32[2,128,128]{2,1,0:T(8,128)S(1)}, f32[2,128,128]{2,1,0:T(8,128)S(1)}, u32[]{:S(2)}, u32[]{:S(2)}) collective-permute-start(f32[2,128,128]{2,1,0:T(8,128)S(1)} %get-tuple-element.35.refs_1_), channel_id=1, source_target_pairs={{0,384},{64,448},{128,256},{192,320},{256,128},{320,192},{384,0},{... | collective-permute-start | bytes 393224 | tf_op jit(solution)/shard_map/ppermute | solution.py:403
